TPU v7x, 32 devices: a whole 2x2x4 slice. The times are simulated.
32 devices in a mesh: dp: 8 (over y, x, core), tensor: 4 (over z).
Axes of the slice: x: 2, y: 2, z: 4, core: 2. Of those that a mesh axis runs over, the one named last changes fastest.
Arguments:
- layer_input: bfloat16 [13312, 1536], P(('dp', 'tensor')), may hold values from -6 to 6
- piece_starts: int32 [8, 2], P('dp'), may hold values from 0 to 1408, as said below
- query_weight: bfloat16 [1536, 1536], P('dp', 'tensor'), may hold values from -0.15625 to 0.15625
- key_weight: bfloat16 [1536, 1536], P('dp', 'tensor'), may hold values from -0.15625 to 0.15625
- value_weight: bfloat16 [1536, 1536], P('dp', 'tensor'), may hold values from -0.15625 to 0.15625
- out_weight: bfloat16 [1536, 1536], P('tensor', 'dp'), may hold values from -0.15625 to 0.15625
- gate_weight: bfloat16 [1536, 4096], P('dp', 'tensor'), may hold values from -0.15625 to 0.15625
- up_weight: bfloat16 [1536, 4096], P('dp', 'tensor'), may hold values from -0.15625 to 0.15625
- down_weight: bfloat16 [4096, 1536], P('tensor', 'dp'), may hold values from -0.09375 to 0.09375
- attention_gain: float32 [1536], replicated, may hold values from 0.5 to 1.5
- feedforward_gain: float32 [1536], replicated, may hold values from 0.5 to 1.5
- head_gain: float32 [1536], replicated, may hold values from 0.5 to 1.5
- score_kernel: float32 [16, 6, 11], replicated, may hold values from -1 to 1
- head_mix: float32 [8, 2, 2], replicated, may hold values from 0.3 to 1
- output_grad: bfloat16 [13312, 1536], P(('dp', 'tensor')), may hold values from -6 to 6
Outputs:
- layer_output: bfloat16 [13312, 1536], P(('dp', 'tensor'))
- input_grad: bfloat16 [13312, 1536], P(('dp', 'tensor'))
- query_grad: float32 [1536, 1536], P('dp', 'tensor')
- key_grad: float32 [1536, 1536], P('dp', 'tensor')
- value_grad: float32 [1536, 1536], P('dp', 'tensor')
- out_weight_grad: float32 [1536, 1536], P('tensor', 'dp')
- gate_grad: float32 [1536, 4096], P('dp', 'tensor')
- up_grad: float32 [1536, 4096], P('dp', 'tensor')
- down_grad: float32 [4096, 1536], P('tensor', 'dp')
- attention_gain_grad: float32 [1536], replicated
- feedforward_gain_grad: float32 [1536], replicated
- head_gain_grad: float32 [1536], replicated
- score_kernel_grad: float32 [16, 6, 11], replicated
- head_mix_grad: float32 [8, 2, 2], replicated
Inputs may be any that keep to these rules, and one draw needn't show every extreme that they name: `piece_starts`: each sequence's 2 pieces of 256 tokens lie inside it, start in rising order and don't intersect.
All inputs are finite; a program needn't handle non-finite values.
Results may differ from a plain program's by a relative error of at most 0.02.
Values may be sent and summed in bfloat16 or wider, within the bound.
No kernel may reach another device: no remote copies, remote signals or barrier semaphores. Data moves between devices by JAX's collectives and lax.ppermute only.
A program may use at most 704 MiB of HBM per device.

v0:
```python
import math

import jax
import jax.numpy as jnp
from jax import lax
from jax.sharding import PartitionSpec as P

HD = 96
LEN = 1664
PIC = 256


epsilon = 1e-05


def rms_norm(values, gain):
    return values * lax.rsqrt(jnp.mean(values * values, axis=-1, keepdims=True) + epsilon) * gain


def group_norm(values, gain):
    centred = values - jnp.mean(values, axis=-1, keepdims=True)
    return centred * lax.rsqrt(jnp.mean(centred * centred, axis=-1, keepdims=True) + epsilon) * gain


def swiglu(gate, upper):
    return jax.nn.silu(gate) * upper


def piece_index(positions, starts):
    inside = (positions[:, None] >= starts[None, :]) & (positions[:, None] < starts[None, :] + PIC)
    labels = jnp.arange(1, starts.shape[0] + 1, dtype=jnp.int32)
    return jnp.max(jnp.where(inside, labels[None, :], 0), axis=1) - 1


def allowed_mask(positions, columns, starts):
    row_piece = piece_index(positions, starts)
    col_piece = piece_index(columns, starts)
    causal = columns[None, :] <= positions[:, None]
    shared = (row_piece[:, None] == col_piece[None, :]) & (row_piece[:, None] >= 0)
    return (causal | shared) & (positions[:, None] >= 0)


def mix_heads(probs, mixing):
    grouped = probs.reshape((mixing.shape[0], 1, 2) + probs.shape[1:])
    return jnp.sum(mixing[:, :, :, None, None] * grouped, axis=2).reshape(probs.shape)


def conv_probs(raw_scores, kernel, mixing, halo_mask, block_mask, score_scale):
    lags = kernel.shape[1]
    taps = kernel.shape[2]
    middle = taps // 2
    block_rows = block_mask.shape[0]
    length = block_mask.shape[1]
    masked = jnp.where(halo_mask[None], raw_scores * score_scale, 0.0)
    padded = jnp.pad(masked, ((0, 0), (0, 0), (middle, taps - 1 - middle)))

    def lag_step(convolved, lag_item):
        row_lag, lag_kernel = lag_item
        rows = lax.dynamic_slice_in_dim(padded, lags - 1 - row_lag, block_rows, 1)
        for key_tap in range(taps):
            window = rows[:, :, 2 * middle - key_tap : 2 * middle - key_tap + length]
            convolved = convolved + lag_kernel[:, key_tap][:, None, None] * window
        return (convolved, None)

    start = jnp.zeros((raw_scores.shape[0], block_rows, length), jnp.float32)
    lag_kernels = jnp.transpose(kernel, (1, 0, 2))
    convolved, _ = lax.scan(
        jax.checkpoint(lag_step), start, (jnp.arange(lags, dtype=jnp.int32), lag_kernels)
    )
    logits = jnp.where(block_mask[None], convolved, -1e30)
    largest = jnp.max(logits, axis=-1, keepdims=True)
    exponent = jnp.exp(logits - largest)
    probs = exponent / jnp.sum(exponent, axis=-1, keepdims=True)
    return mix_heads(probs, mixing)


def project(left, right):
    return jnp.dot(left, right, preferred_element_type=jnp.float32)


def contract_rows(left, right):
    return lax.dot_general(
        left, right, (((0,), (0,)), ((), ())), preferred_element_type=jnp.float32
    )


def contract_cols(left, right):
    return lax.dot_general(
        left, right, (((1,), (1,)), ((), ())), preferred_element_type=jnp.float32
    )


def block_inputs(padded, key_rows, starts, lags, first_row, block_rows):
    extended = padded[first_row : first_row + block_rows + lags - 1]
    raw_scores = jnp.einsum("qhd,khd->hqk", extended, key_rows, preferred_element_type=jnp.float32)
    positions = first_row - (lags - 1) + jnp.arange(block_rows + lags - 1, dtype=jnp.int32)
    columns = jnp.arange(key_rows.shape[0], dtype=jnp.int32)
    return (extended, raw_scores, allowed_mask(positions, columns, starts))


def sequence_forward(seq_item, kernel, mixing, score_scale):
    queries, key_rows, values, starts = seq_item
    lags = kernel.shape[1]
    block_rows = LEN // 2
    padded = jnp.pad(queries, ((lags - 1, 0), (0, 0), (0, 0)))
    outputs = []
    for block_index in range(2):
        first_row = block_index * block_rows
        extended, raw_scores, halo_mask = block_inputs(
            padded, key_rows, starts, lags, first_row, block_rows
        )
        mixed = conv_probs(
            raw_scores, kernel, mixing, halo_mask, halo_mask[lags - 1 :], score_scale
        )
        outputs.append(
            jnp.einsum(
                "hqk,khd->qhd",
                mixed.astype(jnp.bfloat16),
                values,
                preferred_element_type=jnp.float32,
            )
        )
    return jnp.concatenate(outputs, axis=0)


def sequence_backward(seq_item, kernel, mixing, score_scale):
    queries, key_rows, values, starts, out_grads = seq_item
    lags = kernel.shape[1]
    block_rows = LEN // 2
    padded = jnp.pad(queries, ((lags - 1, 0), (0, 0), (0, 0)))
    query_acc = jnp.zeros(padded.shape, jnp.float32)
    key_acc = jnp.zeros(key_rows.shape, jnp.float32)
    value_acc = jnp.zeros(values.shape, jnp.float32)
    kernel_acc = jnp.zeros(kernel.shape, jnp.float32)
    mixing_acc = jnp.zeros(mixing.shape, jnp.float32)
    for block_index in range(2):
        first_row = block_index * block_rows
        extended, raw_scores, halo_mask = block_inputs(
            padded, key_rows, starts, lags, first_row, block_rows
        )

        def probs_of(scores_in, kernel_in, mixing_in):
            return conv_probs(
                scores_in, kernel_in, mixing_in, halo_mask, halo_mask[lags - 1 :], score_scale
            )

        mixed, pullback = jax.vjp(probs_of, raw_scores, kernel, mixing)
        mixed_low = mixed.astype(jnp.bfloat16)
        block_grads = out_grads[first_row : first_row + block_rows]
        value_acc = value_acc + jnp.einsum(
            "hqk,qhd->khd", mixed_low, block_grads, preferred_element_type=jnp.float32
        )
        mixed_grads = jnp.einsum(
            "qhd,khd->hqk", block_grads, values, preferred_element_type=jnp.float32
        )
        score_grads, kernel_grads, mixing_grads = pullback(mixed_grads)
        score_low = score_grads.astype(jnp.bfloat16)
        query_part = jnp.einsum(
            "hqk,khd->qhd", score_low, key_rows, preferred_element_type=jnp.float32
        )
        query_acc = query_acc.at[first_row : first_row + block_rows + lags - 1].add(query_part)
        key_acc = key_acc + jnp.einsum(
            "hqk,qhd->khd", score_low, extended, preferred_element_type=jnp.float32
        )
        kernel_acc = kernel_acc + kernel_grads
        mixing_acc = mixing_acc + mixing_grads
    return (
        query_acc[lags - 1 :].astype(jnp.bfloat16),
        key_acc.astype(jnp.bfloat16),
        value_acc.astype(jnp.bfloat16),
        kernel_acc,
        mixing_acc,
    )


def shards(
    layer_input,
    piece_starts,
    query_weight,
    key_weight,
    value_weight,
    out_weight,
    gate_weight,
    up_weight,
    down_weight,
    attention_gain,
    feedforward_gain,
    head_gain,
    score_kernel,
    head_mix,
    output_grad,
):
    width_local = query_weight.shape[1]
    heads_local = width_local // HD
    tensor_index = lax.axis_index("tensor")
    kernel_local = lax.dynamic_slice_in_dim(
        score_kernel, tensor_index * heads_local, heads_local, 0
    )
    mixing_local = lax.dynamic_slice_in_dim(
        head_mix, tensor_index * (heads_local // 2), heads_local // 2, 0
    )
    gain_local = lax.dynamic_slice_in_dim(head_gain, tensor_index * width_local, width_local, 0)
    score_scale = 1.0 / math.sqrt(HD)
    local_rows = layer_input.shape[0]
    inputs = layer_input.astype(jnp.float32)
    normed, first_pull = jax.vjp(rms_norm, inputs, attention_gain)
    rows_all = lax.all_gather(normed.astype(jnp.bfloat16), "tensor", axis=0, tiled=True)
    query_full, key_full, value_full, out_full = (
        lax.all_gather(query_weight, "dp", axis=0, tiled=True),
        lax.all_gather(key_weight, "dp", axis=0, tiled=True),
        lax.all_gather(value_weight, "dp", axis=0, tiled=True),
        lax.all_gather(out_weight, "dp", axis=1, tiled=True),
    )
    seq_count = rows_all.shape[0] // LEN
    head_shape = (seq_count, LEN, heads_local, HD)
    queries = project(rows_all, query_full).astype(jnp.bfloat16).reshape(head_shape)
    key_rows = project(rows_all, key_full).astype(jnp.bfloat16).reshape(head_shape)
    values = project(rows_all, value_full).astype(jnp.bfloat16).reshape(head_shape)
    heads_out = lax.map(
        lambda seq_item: sequence_forward(seq_item, kernel_local, mixing_local, score_scale),
        (queries, key_rows, values, piece_starts),
    )
    normed_heads, group_pull = jax.vjp(group_norm, heads_out, gain_local.reshape(heads_local, HD))
    mixed_rows = normed_heads.astype(jnp.bfloat16).reshape(seq_count * LEN, width_local)
    attended = lax.psum_scatter(
        project(
            lax.slice_in_dim(mixed_rows, 0, local_rows * lax.axis_size("tensor"), axis=0), out_full
        ).astype(jnp.bfloat16),
        "tensor",
        scatter_dimension=0,
        tiled=True,
    ).astype(jnp.float32)
    hidden = inputs + attended
    ffn_in, second_pull = jax.vjp(rms_norm, hidden, feedforward_gain)
    ffn_all = lax.all_gather(ffn_in.astype(jnp.bfloat16), "tensor", axis=0, tiled=True)
    gate_full, up_full, down_full = (
        lax.all_gather(gate_weight, "dp", axis=0, tiled=True),
        lax.all_gather(up_weight, "dp", axis=0, tiled=True),
        lax.all_gather(down_weight, "dp", axis=1, tiled=True),
    )
    gate = project(ffn_all, gate_full)
    upper = project(ffn_all, up_full)
    activated, act_pull = jax.vjp(swiglu, gate, upper)
    act_low = activated.astype(jnp.bfloat16)
    ffn_term = lax.psum_scatter(
        project(
            lax.slice_in_dim(act_low, 0, local_rows * lax.axis_size("tensor"), axis=0), down_full
        ).astype(jnp.bfloat16),
        "tensor",
        scatter_dimension=0,
        tiled=True,
    ).astype(jnp.float32)
    layer_output = (hidden + ffn_term).astype(jnp.bfloat16)
    query_back, key_back, value_back, out_back, gate_back, up_back, down_back = (
        lax.all_gather(query_weight, "dp", axis=0, tiled=True),
        lax.all_gather(key_weight, "dp", axis=0, tiled=True),
        lax.all_gather(value_weight, "dp", axis=0, tiled=True),
        lax.all_gather(out_weight, "dp", axis=1, tiled=True),
        lax.all_gather(gate_weight, "dp", axis=0, tiled=True),
        lax.all_gather(up_weight, "dp", axis=0, tiled=True),
        lax.all_gather(down_weight, "dp", axis=1, tiled=True),
    )
    grads_all = lax.all_gather(output_grad, "tensor", axis=0, tiled=True)
    act_grads = contract_cols(grads_all, down_back)
    down_part = contract_rows(act_low, grads_all)
    gate_grads, up_grads = act_pull(act_grads)
    gate_low = gate_grads.astype(jnp.bfloat16)
    up_low = up_grads.astype(jnp.bfloat16)
    gate_part = contract_rows(ffn_all, gate_low)
    up_part = contract_rows(ffn_all, up_low)
    gate_grad, up_grad, down_grad = (
        lax.psum_scatter(
            gate_part.astype(jnp.bfloat16), "dp", scatter_dimension=0, tiled=True
        ).astype(jnp.float32),
        lax.psum_scatter(
            up_part.astype(jnp.bfloat16), "dp", scatter_dimension=0, tiled=True
        ).astype(jnp.float32),
        lax.psum_scatter(
            down_part.astype(jnp.bfloat16), "dp", scatter_dimension=1, tiled=True
        ).astype(jnp.float32),
    )
    gate_rows = lax.slice_in_dim(gate_low, 0, local_rows * lax.axis_size("tensor"), axis=0)
    up_rows = lax.slice_in_dim(up_low, 0, local_rows * lax.axis_size("tensor"), axis=0)
    ffn_in_grad = lax.psum_scatter(
        (contract_cols(gate_rows, gate_back) + contract_cols(up_rows, up_back)).astype(
            jnp.bfloat16
        ),
        "tensor",
        scatter_dimension=0,
        tiled=True,
    ).astype(jnp.float32)
    hidden_part, feedforward_gain_part = second_pull(ffn_in_grad)
    hidden_grad = output_grad.astype(jnp.float32) + hidden_part
    attn_grads = lax.all_gather(hidden_grad.astype(jnp.bfloat16), "tensor", axis=0, tiled=True)
    mixed_grads = contract_cols(attn_grads, out_back)
    out_part = contract_rows(mixed_rows, attn_grads)
    head_grads, head_gain_part = group_pull(mixed_grads.reshape(head_shape))
    head_low = head_grads.astype(jnp.bfloat16)
    query_low, key_low, value_low, kernel_parts, mixing_parts = lax.map(
        lambda seq_item: sequence_backward(seq_item, kernel_local, mixing_local, score_scale),
        (queries, key_rows, values, piece_starts, head_low),
    )
    query_low = query_low.reshape(seq_count * LEN, width_local)
    key_low = key_low.reshape(seq_count * LEN, width_local)
    value_low = value_low.reshape(seq_count * LEN, width_local)
    query_part = contract_rows(rows_all, query_low)
    key_part = contract_rows(rows_all, key_low)
    value_part = contract_rows(rows_all, value_low)
    query_grad, key_grad, value_grad, out_weight_grad = (
        lax.psum_scatter(
            query_part.astype(jnp.bfloat16), "dp", scatter_dimension=0, tiled=True
        ).astype(jnp.float32),
        lax.psum_scatter(
            key_part.astype(jnp.bfloat16), "dp", scatter_dimension=0, tiled=True
        ).astype(jnp.float32),
        lax.psum_scatter(
            value_part.astype(jnp.bfloat16), "dp", scatter_dimension=0, tiled=True
        ).astype(jnp.float32),
        lax.psum_scatter(
            out_part.astype(jnp.bfloat16), "dp", scatter_dimension=1, tiled=True
        ).astype(jnp.float32),
    )
    total = contract_cols(query_low, query_back)
    total = total + contract_cols(key_low, key_back)
    normed_grad = lax.psum_scatter(
        (
            total
            + contract_cols(
                lax.slice_in_dim(value_low, 0, local_rows * lax.axis_size("tensor"), axis=0),
                value_back,
            )
        ).astype(jnp.bfloat16),
        "tensor",
        scatter_dimension=0,
        tiled=True,
    ).astype(jnp.float32)
    input_part, attention_gain_part = first_pull(normed_grad)
    input_grad = (hidden_grad + input_part).astype(jnp.bfloat16)
    head_gain_full = lax.dynamic_update_slice_in_dim(
        jnp.zeros(head_gain.shape, jnp.float32),
        head_gain_part.reshape(-1),
        tensor_index * width_local,
        0,
    )
    kernel_full = lax.dynamic_update_slice_in_dim(
        jnp.zeros(score_kernel.shape, jnp.float32),
        jnp.sum(kernel_parts, axis=0),
        tensor_index * heads_local,
        0,
    )
    mixing_full = lax.dynamic_update_slice_in_dim(
        jnp.zeros(head_mix.shape, jnp.float32),
        jnp.sum(mixing_parts, axis=0),
        tensor_index * (heads_local // 2),
        0,
    )
    attention_gain_grad, feedforward_gain_grad, head_gain_grad, score_kernel_grad, head_mix_grad = (
        lax.psum(
            (attention_gain_part, feedforward_gain_part, head_gain_full, kernel_full, mixing_full),
            ("dp", "tensor"),
        )
    )
    return (
        layer_output,
        input_grad,
        query_grad,
        key_grad,
        value_grad,
        out_weight_grad,
        gate_grad,
        up_grad,
        down_grad,
        attention_gain_grad,
        feedforward_gain_grad,
        head_gain_grad,
        score_kernel_grad,
        head_mix_grad,
    )


def solution(mesh):
    placed = (
        P(("dp", "tensor"), None),
        P("dp", None),
        P("dp", "tensor"),
        P("dp", "tensor"),
        P("dp", "tensor"),
        P("tensor", "dp"),
        P("dp", "tensor"),
        P("dp", "tensor"),
        P("tensor", "dp"),
        P(),
        P(),
        P(),
        P(),
        P(),
        P(("dp", "tensor"), None),
    )
    return jax.shard_map(
        shards,
        mesh=mesh,
        in_specs=placed,
        out_specs=(
            P(("dp", "tensor"), None),
            P(("dp", "tensor"), None),
            P("dp", "tensor"),
            P("dp", "tensor"),
            P("dp", "tensor"),
            P("tensor", "dp"),
            P("dp", "tensor"),
            P("dp", "tensor"),
            P("tensor", "dp"),
            P(),
            P(),
            P(),
            P(),
            P(),
        ),
        check_vma=False,
    )
```

profile of v0, /device:TPU:0, one launch (start us, length us, event | category | flops | bytes accessed | tf_op | source)
XLA Modules:
  0.0 7532.1 jit_solution(8802383334359004474)
XLA Ops:
  182.0 793.4 %while.107 = (s32[]{:T(128)}, f32[4,832,1664]{2,1,0:T(8,128)}, f32[6,4,11]{2,1,0:T(4,128)S(1)}, s32[6]{0:T(128)S(1)}, f32[4,837,1674]{2,1,0:T(8,128)}, /*index=5...) while((s32[]{:T(128)}, f32[4,832,1664]{2,1,0:T(8,128)}, ...), condition=%wide.region_10.11_spmd.clone, body=%wide.region_9.10_spmd.clone.sunk | while | flops 127369232 | bytes 287966496 | solution.py:67
  315.8 130.1 %fusion.180 = f32[4,832,1664]{2,1,0:T(8,128)} fusion(f32[4,837,1674]{2,1,0:T(8,128)} %get-tuple-element.1220, s32[]{:T(128)S(6)} %select_n.192, s32[]{:T(128)S(6)} %add.990, s32[]{:T(128)S(6)} %add.991, s32[]{:T(128)S(6)} %add.992, s32[]{:T(128)S(6)} %add.993, s32[]{:T(128)S(6)} %add.994, s32[]{:T(128)S(6)} %add.995, s32[]{:T(128)S(6)} %add.996, ...), kind=kLoop, calls=%fused_computation.134.clone.1 | loop fusion | flops 127369216 | bytes 287965408 | tf_op jit(solution)/shard_map/while/body/eval_jaxpr/while/body/eval_jaxpr/checkpoint/add | solution.py:62
  448.2 130.1 %fusion.180 = f32[4,832,1664]{2,1,0:T(8,128)} fusion(f32[4,837,1674]{2,1,0:T(8,128)} %get-tuple-element.1220, s32[]{:T(128)S(6)} %select_n.192, s32[]{:T(128)S(6)} %add.990, s32[]{:T(128)S(6)} %add.991, s32[]{:T(128)S(6)} %add.992, s32[]{:T(128)S(6)} %add.993, s32[]{:T(128)S(6)} %add.994, s32[]{:T(128)S(6)} %add.995, s32[]{:T(128)S(6)} %add.996, ...), kind=kLoop, calls=%fused_computation.134.clone.1 | loop fusion | flops 127369216 | bytes 287965408 | tf_op jit(solution)/shard_map/while/body/eval_jaxpr/while/body/eval_jaxpr/checkpoint/add | solution.py:62
  580.6 130.1 %fusion.180 = f32[4,832,1664]{2,1,0:T(8,128)} fusion(f32[4,837,1674]{2,1,0:T(8,128)} %get-tuple-element.1220, s32[]{:T(128)S(6)} %select_n.192, s32[]{:T(128)S(6)} %add.990, s32[]{:T(128)S(6)} %add.991, s32[]{:T(128)S(6)} %add.992, s32[]{:T(128)S(6)} %add.993, s32[]{:T(128)S(6)} %add.994, s32[]{:T(128)S(6)} %add.995, s32[]{:T(128)S(6)} %add.996, ...), kind=kLoop, calls=%fused_computation.134.clone.1 | loop fusion | flops 127369216 | bytes 287965408 | tf_op jit(solution)/shard_map/while/body/eval_jaxpr/while/body/eval_jaxpr/checkpoint/add | solution.py:62
  712.9 130.1 %fusion.180 = f32[4,832,1664]{2,1,0:T(8,128)} fusion(f32[4,837,1674]{2,1,0:T(8,128)} %get-tuple-element.1220, s32[]{:T(128)S(6)} %select_n.192, s32[]{:T(128)S(6)} %add.990, s32[]{:T(128)S(6)} %add.991, s32[]{:T(128)S(6)} %add.992, s32[]{:T(128)S(6)} %add.993, s32[]{:T(128)S(6)} %add.994, s32[]{:T(128)S(6)} %add.995, s32[]{:T(128)S(6)} %add.996, ...), kind=kLoop, calls=%fused_computation.134.clone.1 | loop fusion | flops 127369216 | bytes 287965408 | tf_op jit(solution)/shard_map/while/body/eval_jaxpr/while/body/eval_jaxpr/checkpoint/add | solution.py:62
  845.3 130.1 %fusion.180 = f32[4,832,1664]{2,1,0:T(8,128)} fusion(f32[4,837,1674]{2,1,0:T(8,128)} %get-tuple-element.1220, s32[]{:T(128)S(6)} %select_n.192, s32[]{:T(128)S(6)} %add.990, s32[]{:T(128)S(6)} %add.991, s32[]{:T(128)S(6)} %add.992, s32[]{:T(128)S(6)} %add.993, s32[]{:T(128)S(6)} %add.994, s32[]{:T(128)S(6)} %add.995, s32[]{:T(128)S(6)} %add.996, ...), kind=kLoop, calls=%fused_computation.134.clone.1 | loop fusion | flops 127369216 | bytes 287965408 | tf_op jit(solution)/shard_map/while/body/eval_jaxpr/while/body/eval_jaxpr/checkpoint/add | solution.py:62
  1032.5 790.8 %while.106 = (s32[]{:T(128)}, f32[4,832,1664]{2,1,0:T(8,128)}, f32[6,4,11]{2,1,0:T(4,128)S(1)}, s32[6]{0:T(128)S(1)}, f32[4,837,1674]{2,1,0:T(8,128)}, /*index=5...) while((s32[]{:T(128)}, f32[4,832,1664]{2,1,0:T(8,128)}, ...), condition=%wide.region_4.5_spmd.clone, body=%wide.region_3.4_spmd.clone.sunk | while | flops 127369232 | bytes 287966496 | solution.py:67
  1166.4 129.6 %fusion.178 = f32[4,832,1664]{2,1,0:T(8,128)} fusion(f32[4,837,1674]{2,1,0:T(8,128)} %get-tuple-element.1163, s32[]{:T(128)S(6)} %select_n.191, s32[]{:T(128)S(6)} %add.967, s32[]{:T(128)S(6)} %add.968, s32[]{:T(128)S(6)} %add.969, s32[]{:T(128)S(6)} %add.970, s32[]{:T(128)S(6)} %add.971, s32[]{:T(128)S(6)} %add.972, s32[]{:T(128)S(6)} %add.973, ...), kind=kLoop, calls=%fused_computation.99.clone.1 | loop fusion | flops 127369216 | bytes 287965408 | tf_op jit(solution)/shard_map/while/body/eval_jaxpr/while/body/eval_jaxpr/checkpoint/add | solution.py:62
  1298.2 129.6 %fusion.178 = f32[4,832,1664]{2,1,0:T(8,128)} fusion(f32[4,837,1674]{2,1,0:T(8,128)} %get-tuple-element.1163, s32[]{:T(128)S(6)} %select_n.191, s32[]{:T(128)S(6)} %add.967, s32[]{:T(128)S(6)} %add.968, s32[]{:T(128)S(6)} %add.969, s32[]{:T(128)S(6)} %add.970, s32[]{:T(128)S(6)} %add.971, s32[]{:T(128)S(6)} %add.972, s32[]{:T(128)S(6)} %add.973, ...), kind=kLoop, calls=%fused_computation.99.clone.1 | loop fusion | flops 127369216 | bytes 287965408 | tf_op jit(solution)/shard_map/while/body/eval_jaxpr/while/body/eval_jaxpr/checkpoint/add | solution.py:62
  1561.9 129.6 %fusion.178 = f32[4,832,1664]{2,1,0:T(8,128)} fusion(f32[4,837,1674]{2,1,0:T(8,128)} %get-tuple-element.1163, s32[]{:T(128)S(6)} %select_n.191, s32[]{:T(128)S(6)} %add.967, s32[]{:T(128)S(6)} %add.968, s32[]{:T(128)S(6)} %add.969, s32[]{:T(128)S(6)} %add.970, s32[]{:T(128)S(6)} %add.971, s32[]{:T(128)S(6)} %add.972, s32[]{:T(128)S(6)} %add.973, ...), kind=kLoop, calls=%fused_computation.99.clone.1 | loop fusion | flops 127369216 | bytes 287965408 | tf_op jit(solution)/shard_map/while/body/eval_jaxpr/while/body/eval_jaxpr/checkpoint/add | solution.py:62
  2795.6 2166.8 %while.104 = (s32[]{:T(128)}, f32[4,837,1674]{2,1,0:T(8,128)}, f32[4,832,1664]{2,1,0:T(8,128)}, f32[6,4,11]{2,1,0:T(4,128)}, s32[6]{0:T(128)S(1)}, /*index=5*/f3...) while((s32[]{:T(128)}, f32[4,837,1674]{2,1,0:T(8,128)}, ...), condition=%wide.region_39.40_spmd, body=%wide.region_27.39_spmd.sunk | while | flops 244029344 | bytes 864432768 | solution.py:67
  2841.4 166.9 %fusion.174 = (f32[4]{0:T(128)S(1)}, f32[4]{0:T(128)S(1)}, f32[4]{0:T(128)S(1)}, f32[4]{0:T(128)S(1)}, f32[4]{0:T(128)S(1)}, /*index=5*/f32[4]{0:T(128)S(1)}, f3...) fusion(f32[4,832,1664]{2,1,0:T(8,128)} %get-tuple-element.1279,, ...), kind=kLoop, calls=%fused_computation.22.clone.1 | loop fusion | flops 155058144 | bytes 398721344 | tf_op jit(solution)/shard_map/while/body/eval_jaxpr/transpose(jvp())/while/body/eval_jaxpr/checkpoint/reduce_sum | solution.py:62
  3202.0 166.9 %fusion.174 = (f32[4]{0:T(128)S(1)}, f32[4]{0:T(128)S(1)}, f32[4]{0:T(128)S(1)}, f32[4]{0:T(128)S(1)}, f32[4]{0:T(128)S(1)}, /*index=5*/f32[4]{0:T(128)S(1)}, f3...) fusion(f32[4,832,1664]{2,1,0:T(8,128)} %get-tuple-element.1279,, ...), kind=kLoop, calls=%fused_computation.22.clone.1 | loop fusion | flops 155058144 | bytes 398721344 | tf_op jit(solution)/shard_map/while/body/eval_jaxpr/transpose(jvp())/while/body/eval_jaxpr/checkpoint/reduce_sum | solution.py:62
  3563.2 166.9 %fusion.174 = (f32[4]{0:T(128)S(1)}, f32[4]{0:T(128)S(1)}, f32[4]{0:T(128)S(1)}, f32[4]{0:T(128)S(1)}, f32[4]{0:T(128)S(1)}, /*index=5*/f32[4]{0:T(128)S(1)}, f3...) fusion(f32[4,832,1664]{2,1,0:T(8,128)} %get-tuple-element.1279,, ...), kind=kLoop, calls=%fused_computation.22.clone.1 | loop fusion | flops 155058144 | bytes 398721344 | tf_op jit(solution)/shard_map/while/body/eval_jaxpr/transpose(jvp())/while/body/eval_jaxpr/checkpoint/reduce_sum | solution.py:62
  3924.3 166.9 %fusion.174 = (f32[4]{0:T(128)S(1)}, f32[4]{0:T(128)S(1)}, f32[4]{0:T(128)S(1)}, f32[4]{0:T(128)S(1)}, f32[4]{0:T(128)S(1)}, /*index=5*/f32[4]{0:T(128)S(1)}, f3...) fusion(f32[4,832,1664]{2,1,0:T(8,128)} %get-tuple-element.1279,, ...), kind=kLoop, calls=%fused_computation.22.clone.1 | loop fusion | flops 155058144 | bytes 398721344 | tf_op jit(solution)/shard_map/while/body/eval_jaxpr/transpose(jvp())/while/body/eval_jaxpr/checkpoint/reduce_sum | solution.py:62
  4285.5 166.9 %fusion.174 = (f32[4]{0:T(128)S(1)}, f32[4]{0:T(128)S(1)}, f32[4]{0:T(128)S(1)}, f32[4]{0:T(128)S(1)}, f32[4]{0:T(128)S(1)}, /*index=5*/f32[4]{0:T(128)S(1)}, f3...) fusion(f32[4,832,1664]{2,1,0:T(8,128)} %get-tuple-element.1279,, ...), kind=kLoop, calls=%fused_computation.22.clone.1 | loop fusion | flops 155058144 | bytes 398721344 | tf_op jit(solution)/shard_map/while/body/eval_jaxpr/transpose(jvp())/while/body/eval_jaxpr/checkpoint/reduce_sum | solution.py:62
  4646.7 166.9 %fusion.174 = (f32[4]{0:T(128)S(1)}, f32[4]{0:T(128)S(1)}, f32[4]{0:T(128)S(1)}, f32[4]{0:T(128)S(1)}, f32[4]{0:T(128)S(1)}, /*index=5*/f32[4]{0:T(128)S(1)}, f3...) fusion(f32[4,832,1664]{2,1,0:T(8,128)} %get-tuple-element.1279,, ...), kind=kLoop, calls=%fused_computation.22.clone.1 | loop fusion | flops 155058144 | bytes 398721344 | tf_op jit(solution)/shard_map/while/body/eval_jaxpr/transpose(jvp())/while/body/eval_jaxpr/checkpoint/reduce_sum | solution.py:62
  4973.1 2167.0 %while.105 = (s32[]{:T(128)}, f32[4,837,1674]{2,1,0:T(8,128)}, f32[4,832,1664]{2,1,0:T(8,128)}, f32[6,4,11]{2,1,0:T(4,128)}, s32[6]{0:T(128)S(1)}, /*index=5*/f3...) while((s32[]{:T(128)}, f32[4,837,1674]{2,1,0:T(8,128)}, ...), condition=%wide.region_56.57_spmd, body=%wide.region_44.56_spmd.sunk | while | flops 244029344 | bytes 864432768 | solution.py:67
  5018.7 166.6 %fusion.176 = (f32[4]{0:T(128)S(1)}, f32[4]{0:T(128)S(1)}, f32[4]{0:T(128)S(1)}, f32[4]{0:T(128)S(1)}, f32[4]{0:T(128)S(1)}, /*index=5*/f32[4]{0:T(128)S(1)}, f3...) fusion(f32[4,832,1664]{2,1,0:T(8,128)} %get-tuple-element.1342,, ...), kind=kLoop, calls=%fused_computation.71.clone.1 | loop fusion | flops 155058144 | bytes 398721344 | tf_op jit(solution)/shard_map/while/body/eval_jaxpr/transpose(jvp())/while/body/eval_jaxpr/checkpoint/reduce_sum | solution.py:62
  5379.1 166.6 %fusion.176 = (f32[4]{0:T(128)S(1)}, f32[4]{0:T(128)S(1)}, f32[4]{0:T(128)S(1)}, f32[4]{0:T(128)S(1)}, f32[4]{0:T(128)S(1)}, /*index=5*/f32[4]{0:T(128)S(1)}, f3...) fusion(f32[4,832,1664]{2,1,0:T(8,128)} %get-tuple-element.1342,, ...), kind=kLoop, calls=%fused_computation.71.clone.1 | loop fusion | flops 155058144 | bytes 398721344 | tf_op jit(solution)/shard_map/while/body/eval_jaxpr/transpose(jvp())/while/body/eval_jaxpr/checkpoint/reduce_sum | solution.py:62
  5740.4 166.6 %fusion.176 = (f32[4]{0:T(128)S(1)}, f32[4]{0:T(128)S(1)}, f32[4]{0:T(128)S(1)}, f32[4]{0:T(128)S(1)}, f32[4]{0:T(128)S(1)}, /*index=5*/f32[4]{0:T(128)S(1)}, f3...) fusion(f32[4,832,1664]{2,1,0:T(8,128)} %get-tuple-element.1342,, ...), kind=kLoop, calls=%fused_computation.71.clone.1 | loop fusion | flops 155058144 | bytes 398721344 | tf_op jit(solution)/shard_map/while/body/eval_jaxpr/transpose(jvp())/while/body/eval_jaxpr/checkpoint/reduce_sum | solution.py:62
  6101.6 166.6 %fusion.176 = (f32[4]{0:T(128)S(1)}, f32[4]{0:T(128)S(1)}, f32[4]{0:T(128)S(1)}, f32[4]{0:T(128)S(1)}, f32[4]{0:T(128)S(1)}, /*index=5*/f32[4]{0:T(128)S(1)}, f3...) fusion(f32[4,832,1664]{2,1,0:T(8,128)} %get-tuple-element.1342,, ...), kind=kLoop, calls=%fused_computation.71.clone.1 | loop fusion | flops 155058144 | bytes 398721344 | tf_op jit(solution)/shard_map/while/body/eval_jaxpr/transpose(jvp())/while/body/eval_jaxpr/checkpoint/reduce_sum | solution.py:62
  6462.8 166.6 %fusion.176 = (f32[4]{0:T(128)S(1)}, f32[4]{0:T(128)S(1)}, f32[4]{0:T(128)S(1)}, f32[4]{0:T(128)S(1)}, f32[4]{0:T(128)S(1)}, /*index=5*/f32[4]{0:T(128)S(1)}, f3...) fusion(f32[4,832,1664]{2,1,0:T(8,128)} %get-tuple-element.1342,, ...), kind=kLoop, calls=%fused_computation.71.clone.1 | loop fusion | flops 155058144 | bytes 398721344 | tf_op jit(solution)/shard_map/while/body/eval_jaxpr/transpose(jvp())/while/body/eval_jaxpr/checkpoint/reduce_sum | solution.py:62
  6824.1 166.6 %fusion.176 = (f32[4]{0:T(128)S(1)}, f32[4]{0:T(128)S(1)}, f32[4]{0:T(128)S(1)}, f32[4]{0:T(128)S(1)}, f32[4]{0:T(128)S(1)}, /*index=5*/f32[4]{0:T(128)S(1)}, f3...) fusion(f32[4,832,1664]{2,1,0:T(8,128)} %get-tuple-element.1342,, ...), kind=kLoop, calls=%fused_computation.71.clone.1 | loop fusion | flops 155058144 | bytes 398721344 | tf_op jit(solution)/shard_map/while/body/eval_jaxpr/transpose(jvp())/while/body/eval_jaxpr/checkpoint/reduce_sum | solution.py:62
  (546 shorter events, 4443.4 us)
Async XLA Ops:
  7.2 29.5 all-gather.16.cloned.1.call-start
  7.9 126.9 %all-gather.12.cloned.1.call-start = ((), (), s32[]{:S(2)}) async-start(), calls=%async_computation.11 | async-start | bytes 6389760 | tf_op jit(solution)/shard_map/all_gather | solution.py:207
  13.5 145.7 %all-gather.18.cloned.1.call-start = ((), (), s32[]{:S(2)}) async-start(), calls=%async_computation.14 | async-start | bytes 1327104 | tf_op jit(solution)/shard_map/all_gather | solution.py:210
  14.2 1870.4 %all-gather.14.cloned.1.call-start = ((), (), s32[]{:S(2)}) async-start(), calls=%async_computation.12 | async-start | bytes 1327104 | tf_op jit(solution)/shard_map/all_gather | solution.py:211
  14.8 1889.6 %all-gather.20.cloned.1.call-start = ((), (), s32[]{:S(2)}) async-start(), calls=%async_computation.15 | async-start | bytes 1327104 | tf_op jit(solution)/shard_map/all_gather | solution.py:212
  15.4 1987.8 %reduce-scatter.12.cloned.1.call-start = ((), (), s32[]{:S(2)}) async-start(), calls=%async_computation.16 | async-start | bytes 6389760 | tf_op jit(solution)/shard_map/reduce_scatter | solution.py:225
  182.0 793.4 %copy-start.7 = (pred[832,1664]{1,0:T(8,128)(4,1)S(1)}, pred[832,1664]{1,0:T(8,128)(4,1)}, u32[]{:S(2)}) copy-start(pred[832,1664]{1,0:T(8,128)(4,1)} %slice.872) | copy-start | bytes 4153348
  1911.4 126.5 %all-gather.26.cloned.1.call-start = ((), (), s32[]{:S(2)}) async-start(), calls=%async_computation.19 | async-start | bytes 3538944 | tf_op jit(solution)/shard_map/all_gather | solution.py:238
  1912.2 223.3 %all-gather.22.cloned.1.call-start = ((), (), s32[]{:S(2)}) async-start(), calls=%async_computation.17 | async-start | bytes 6389760 | tf_op jit(solution)/shard_map/all_gather | solution.py:235
  2008.7 159.4 %all-gather.24.cloned.1.call-start = ((), (), s32[]{:S(2)}) async-start(), calls=%async_computation.18 | async-start | bytes 3538944 | tf_op jit(solution)/shard_map/all_gather | solution.py:237
  2009.4 192.8 %all-gather.28.cloned.1.call-start = ((), (), s32[]{:S(2)}) async-start(), calls=%async_computation.20 | async-start | bytes 3538944 | tf_op jit(solution)/shard_map/all_gather | solution.py:239
  2010.0 289.7 %all-gather.30.cloned.1.call-start = ((), (), s32[]{:S(2)}) async-start(), calls=%async_computation.22 | async-start | bytes 6389760 | tf_op jit(solution)/shard_map/all_gather | solution.py:263
  2010.7 412.5 %reduce-scatter.16.cloned.1.call-start = ((), (), s32[]{:S(2)}) async-start(), calls=%async_computation.23 | async-start | bytes 6389760 | tf_op jit(solution)/shard_map/reduce_scatter | solution.py:284
  2333.0 195.0 %all-gather.32.cloned.1.call-start = ((), (), s32[]{:S(2)}) async-start(), calls=%async_computation.24 | async-start | bytes 6389760 | tf_op jit(solution)/shard_map/all_gather | solution.py:294
  2431.4 4851.6 %reduce-scatter.32.cloned.1.call-start = ((), (), s32[]{:S(2)}) async-start(), calls=%async_computation.32 | async-start | bytes 3538944 | tf_op jit(solution)/shard_map/reduce_scatter | solution.py:278
  2441.6 4843.6 %reduce-scatter.30.cloned.1.call-start = ((), (), s32[]{:S(2)}) async-start(), calls=%async_computation.31 | async-start | bytes 3538944 | tf_op jit(solution)/shard_map/reduce_scatter | solution.py:275
  2452.1 4835.0 %reduce-scatter.28.cloned.1.call-start = ((), (), s32[]{:S(2)}) async-start(), calls=%async_computation.30 | async-start | bytes 3538944 | tf_op jit(solution)/shard_map/reduce_scatter | solution.py:272
  2462.8 4827.3 %reduce-scatter.26.cloned.1.call-start = ((), (), s32[]{:S(2)}) async-start(), calls=%async_computation.29 | async-start | bytes 1327104 | tf_op jit(solution)/shard_map/reduce_scatter | solution.py:319
  4973.1 2167.0 %copy-start.27 = (bf16[1664,384]{0,1:T(8,128)(2,1)S(1)}, bf16[1664,384]{0,1:T(8,128)(2,1)}, u32[]{:S(2)}) copy-start(bf16[1664,384]{0,1:T(8,128)(2,1)} %multiply_convert_fusion.5) | copy-start | bytes 3833860
  7173.5 118.3 %reduce-scatter.24.cloned.1.call-start = ((), (), s32[]{:S(2)}) async-start(), calls=%async_computation.28 | async-start | bytes 1327104 | tf_op jit(solution)/shard_map/reduce_scatter | solution.py:316
  7196.3 97.1 %reduce-scatter.22.cloned.1.call-start = ((), (), s32[]{:S(2)}) async-start(), calls=%async_computation.27 | async-start | bytes 1327104 | tf_op jit(solution)/shard_map/reduce_scatter | solution.py:313
  7221.8 108.1 %reduce-scatter.20.cloned.1.call-start = ((), (), s32[]{:S(2)}) async-start(), calls=%async_computation.26 | async-start | bytes 1327104 | tf_op jit(solution)/shard_map/reduce_scatter | solution.py:310
  7255.3 168.7 %reduce-scatter.18.cloned.1.call-start = ((), (), s32[]{:S(2)}) async-start(), calls=%async_computation.25 | async-start | bytes 6389760 | tf_op jit(solution)/shard_map/reduce_scatter | solution.py:325
  7273.1 246.6 %reduce-scatter.14.cloned.1.call-start = ((), (), s32[]{:S(2)}) async-start(), calls=%async_computation.21 | async-start | bytes 6389760 | tf_op jit(solution)/shard_map/reduce_scatter | solution.py:245
  (96 other events, 4770.6 us)
Sparse Core Ops, SparseCore 0:
  9.9 26.7 all-gather.15
  38.8 95.8 all-gather.11
  136.7 22.4 all-gather.17
  160.9 24.0 all-gather.13
  186.8 24.0 all-gather.19
  1911.5 91.6 reduce-scatter.11
  2005.1 32.8 all-gather.25
  2039.5 95.8 all-gather.21
  2137.3 30.7 all-gather.23
  2169.8 32.3 all-gather.27
  2203.7 95.8 all-gather.29
  2333.1 90.0 reduce-scatter.15
  2431.6 96.3 all-gather.31
  2531.2 44.6 reduce-scatter.31
  2579.5 46.2 reduce-scatter.29
  2629.0 46.1 reduce-scatter.27
  7173.6 35.4 reduce-scatter.25
  7212.2 36.7 reduce-scatter.23
  7252.6 36.7 reduce-scatter.21
  7293.0 36.7 reduce-scatter.19
  7332.3 91.5 reduce-scatter.17
  7426.3 93.2 reduce-scatter.13
where the time goes:
time: 7560 us; the launch traced here: 7530 us
  other arithmetic  5550 us (73%)
  waiting for transfers between devices  813 us (11%)
  local copies, waits for them, and re-layouts  787 us (10%)
  matrix products  282 us (4%)
    reduce_sum x12, other arithmetic, lag_step(): convolved = convolved + lag_kernel[:, key_tap][:, None, None] * window  2000 us
    add x12, other arithmetic, lag_step(): convolved = convolved + lag_kernel[:, key_tap][:, None, None] * window  1560 us
    dynamic_update_slice x12, other arithmetic, lag_step(): rows = lax.dynamic_slice_in_dim(padded, lags - 1 - row_lag, block_rows, 1)  1110 us
    add_any x12, local copies, waits for them, and re-layouts, conv_probs(): lax.scan(jax.checkpoint(lag_step), start, (jnp.arange(lags, dtype=jnp.int...  668 us
    mul x12, other arithmetic, lag_step(): convolved = convolved + lag_kernel[:, key_tap][:, None, None] * window  510 us
  transfers between devices with their start and end apart: 22, of which 14 were waited for; matrix products, arithmetic and copies ran while one was open for 87% of the time, Pallas kernels for 0%

commit v1 on v0

v1 whole, which is shorter than its diff:
```python
import functools
import math

import jax
import jax.numpy as jnp
from jax import lax
from jax.experimental import pallas as pl
from jax.experimental.pallas import tpu as pltpu
from jax.sharding import PartitionSpec as P

HD = 96
LEN = 1664
PIC = 256
TILE = 128
LANES = 128
FRONT = 64
ROWPAD = 16
VMEM_BYTES = 56 * 1024 * 1024
epsilon = 1e-05


def dot_nn(left, right):
    return jnp.dot(left, right, preferred_element_type=jnp.float32)


def dot_nt(left, right):
    return lax.dot_general(left, right, (((1,), (1,)), ((), ())), preferred_element_type=jnp.float32)


def dot_tn(left, right):
    return lax.dot_general(left, right, (((0,), (0,)), ((), ())), preferred_element_type=jnp.float32)


def row_ends(rows, starts_ref, pics):
    ends = rows
    for piece in range(pics):
        first = starts_ref[piece]
        ends = jnp.where((rows >= first) & (rows < first + PIC), first + PIC - 1, ends)
    return ends


def filter_keys(kt_ref, thi_ref, tlo_ref, kcat_ref, lags):
    for head in range(2):

        def tile_step(tile, carry):
            first = pl.multiple_of(tile * TILE, TILE)
            window = kt_ref[head, :, pl.ds(first, 2 * TILE)]
            filtered = dot_nn(window, thi_ref[head]) + dot_nn(window, tlo_ref[head])
            for lag in range(lags):
                kcat_ref[head, lag * LANES : (lag + 1) * LANES, pl.ds(first, TILE)] = filtered[
                    :, lag * TILE : (lag + 1) * TILE
                ].astype(jnp.bfloat16)
            return carry

        lax.fori_loop(0, LEN // TILE, tile_step, 0)


def lagged(rows, lags):
    return jnp.concatenate(
        [rows[ROWPAD - lag : ROWPAD - lag + TILE] for lag in range(lags)], axis=1
    ).astype(jnp.bfloat16)


def forward_kernel(
    bounds_ref, starts_ref, q_ref, kt_ref, v_ref, thi_ref, tlo_ref,
    e_ref, o_ref, inv_ref,
    kcat_ref, c_ref, qcat_ref, top_ref, sum_ref,
    *, lags, pics,
):
    block = pl.program_id(1)
    blocks = pl.num_programs(1)
    first_row = pl.multiple_of(block * TILE, TILE)

    @pl.when(block == 0)
    def _():
        filter_keys(kt_ref, thi_ref, tlo_ref, kcat_ref, lags)

    full = bounds_ref[block]
    last = bounds_ref[blocks + block]
    for head in range(2):
        rows = q_ref[head, pl.ds(first_row, TILE + ROWPAD), :].astype(jnp.float32)
        qcat_ref[head] = lagged(rows, lags)
        top_ref[head] = jnp.full((TILE, LANES), -1e30, jnp.float32)
        sum_ref[head] = jnp.zeros((TILE, LANES), jnp.float32)
        o_ref[head] = jnp.zeros(o_ref.shape[1:], jnp.float32)

    def full_tiles(first, width):
        for head in range(2):
            logits = dot_nn(qcat_ref[head], kcat_ref[head, :, pl.ds(first, width)])
            c_ref[head, :, pl.ds(first, width)] = logits
            top = top_ref[head]
            for part in range(width // LANES):
                top = jnp.maximum(top, logits[:, part * LANES : (part + 1) * LANES])
            top_ref[head] = top

    def full_step(pair, carry):
        full_tiles(pl.multiple_of(pair * 2 * TILE, 2 * TILE), 2 * TILE)
        return carry

    lax.fori_loop(0, full // 2, full_step, 0)

    @pl.when(full % 2 == 1)
    def _():
        full_tiles(pl.multiple_of((full - 1) * TILE, TILE), TILE)

    source_rows = first_row - ROWPAD + lax.broadcasted_iota(jnp.int32, (TILE + ROWPAD, 1), 0)
    source_ends = row_ends(source_rows, starts_ref, pics)
    target_rows = first_row + lax.broadcasted_iota(jnp.int32, (TILE, 1), 0)
    target_ends = row_ends(target_rows, starts_ref, pics)

    def mixed_step(tile, carry):
        first = pl.multiple_of(tile * TILE, TILE)
        columns = first - FRONT + lax.broadcasted_iota(jnp.int32, (1, 2 * TILE), 1)
        source_allowed = columns <= source_ends
        target_allowed = first + lax.broadcasted_iota(jnp.int32, (1, TILE), 1) <= target_ends
        for head in range(2):
            raw = dot_nn(q_ref[head, pl.ds(first_row, TILE + ROWPAD), :], kt_ref[head, :, pl.ds(first, 2 * TILE)])
            raw = jnp.where(source_allowed, raw, 0.0)
            high = raw.astype(jnp.bfloat16)
            low = (raw - high.astype(jnp.float32)).astype(jnp.bfloat16)
            taps = dot_nn(high, thi_ref[head]) + dot_nn(low, thi_ref[head]) + dot_nn(high, tlo_ref[head])
            logits = taps[ROWPAD:, :TILE]
            for lag in range(1, lags):
                logits = logits + taps[ROWPAD - lag : ROWPAD - lag + TILE, lag * TILE : (lag + 1) * TILE]
            logits = jnp.where(target_allowed, logits, -1e30)
            c_ref[head, :, pl.ds(first, TILE)] = logits
            top_ref[head] = jnp.maximum(top_ref[head], logits)
        return carry

    lax.fori_loop(full, last + 1, mixed_step, 0)

    for head in range(2):
        top_ref[head] = jnp.broadcast_to(
            jnp.max(top_ref[head], axis=1, keepdims=True), (TILE, LANES)
        )

    def soft_tiles(first, width):
        for head in range(2):
            parts = []
            total = sum_ref[head]
            for part in range(width // LANES):
                logits = c_ref[head, :, pl.ds(first + part * LANES, LANES)]
                value = jnp.exp(logits - top_ref[head])
                total = total + value
                parts.append(value.astype(jnp.bfloat16))
            sum_ref[head] = total
            weights = parts[0] if len(parts) == 1 else jnp.concatenate(parts, axis=1)
            e_ref[head, :, pl.ds(first, width)] = weights
            o_ref[head] += dot_nn(weights, v_ref[0, pl.ds(first, width), :])

    def soft_step(pair, carry):
        soft_tiles(pl.multiple_of(pair * 2 * TILE, 2 * TILE), 2 * TILE)
        return carry

    lax.fori_loop(0, (last + 1) // 2, soft_step, 0)

    @pl.when(last % 2 == 0)
    def _():
        soft_tiles(pl.multiple_of(last * TILE, TILE), TILE)

    for head in range(2):
        inverse = 1.0 / jnp.sum(sum_ref[head], axis=1, keepdims=True)
        inv_ref[head] = jnp.broadcast_to(inverse, (TILE, LANES))
        o_ref[head] = o_ref[head] * inverse


def backward_kernel(
    bounds_ref, starts_ref, mix_ref, q_ref, kt_ref, k_ref, vt_ref, thi_ref, tlo_ref, ttr_ref,
    e_ref, o_ref, inv_ref, og_ref,
    dq_ref, dkt_ref, dvt_ref, gram_ref,
    kcat_ref, dkcat_ref, dqcat_ref, qcatt_ref, x_ref, xt_ref, delta_ref,
    *, lags, pics,
):
    group = pl.program_id(0)
    block = pl.program_id(1)
    blocks = pl.num_programs(1)
    first_row = pl.multiple_of(block * TILE, TILE)

    @pl.when(block == 0)
    def _():
        filter_keys(kt_ref, thi_ref, tlo_ref, kcat_ref, lags)
        dkcat_ref[...] = jnp.zeros(dkcat_ref.shape, jnp.float32)
        dq_ref[...] = jnp.zeros(dq_ref.shape, jnp.float32)
        dkt_ref[...] = jnp.zeros(dkt_ref.shape, jnp.float32)
        dvt_ref[...] = jnp.zeros(dvt_ref.shape, jnp.float32)
        gram_ref[...] = jnp.zeros(gram_ref.shape, jnp.float32)

    full = bounds_ref[block]
    last = bounds_ref[blocks + block]
    for head in range(2):
        rows = q_ref[head, pl.ds(first_row, TILE + ROWPAD), :].astype(jnp.float32)
        for lag in range(lags):
            turned = jnp.transpose(rows[ROWPAD - lag : ROWPAD - lag + TILE])
            qcatt_ref[head, lag * HD : (lag + 1) * HD, :] = turned[:HD].astype(jnp.bfloat16)
        dqcat_ref[head] = jnp.zeros(dqcat_ref.shape[1:], jnp.float32)
        inverse = inv_ref[head]
        delta = jnp.zeros((TILE, 1), jnp.float32)
        for out_head in range(2):
            weight = mix_ref[group * 4 + out_head * 2 + head]
            scaled = og_ref[out_head].astype(jnp.float32) * (inverse * weight)
            lanes = slice(out_head * LANES, (out_head + 1) * LANES)
            delta = delta + jnp.sum(scaled * o_ref[head, :, lanes], axis=1, keepdims=True)
            x_ref[head, :, lanes] = scaled.astype(jnp.bfloat16)
            xt_ref[head, lanes, :] = jnp.transpose(scaled).astype(jnp.bfloat16)
        delta_ref[head] = jnp.broadcast_to(delta, (TILE, LANES))

    def score_grads(head, first, width):
        prob_grads = dot_nn(x_ref[head], vt_ref[0, :, pl.ds(first, width)])
        weights = e_ref[head, :, pl.ds(first, width)]
        dvt_ref[0, :, pl.ds(first, width)] += dot_nn(xt_ref[head], weights)
        delta = delta_ref[head]
        parts = [
            weights[:, part * LANES : (part + 1) * LANES].astype(jnp.float32)
            * (prob_grads[:, part * LANES : (part + 1) * LANES] - delta)
            for part in range(width // LANES)
        ]
        return parts[0] if len(parts) == 1 else jnp.concatenate(parts, axis=1)

    def full_tiles(first, width):
        for head in range(2):
            grads = score_grads(head, first, width).astype(jnp.bfloat16)
            dqcat_ref[head] += dot_nt(grads, kcat_ref[head, :, pl.ds(first, width)])
            dkcat_ref[head, :, pl.ds(first, width)] += dot_nn(qcatt_ref[head], grads)

    def full_step(pair, carry):
        full_tiles(pl.multiple_of(pair * 2 * TILE, 2 * TILE), 2 * TILE)
        return carry

    lax.fori_loop(0, full // 2, full_step, 0)

    @pl.when(full % 2 == 1)
    def _():
        full_tiles(pl.multiple_of((full - 1) * TILE, TILE), TILE)

    source_rows = first_row - ROWPAD + lax.broadcasted_iota(jnp.int32, (TILE + ROWPAD, 1), 0)
    source_ends = row_ends(source_rows, starts_ref, pics)
    turned_rows = first_row - ROWPAD + lax.broadcasted_iota(jnp.int32, (1, TILE + ROWPAD), 1)
    turned_ends = row_ends(turned_rows, starts_ref, pics)

    def mixed_step(tile, carry):
        first = pl.multiple_of(tile * TILE, TILE)
        columns = first - FRONT + lax.broadcasted_iota(jnp.int32, (1, 2 * TILE), 1)
        turned_columns = first - FRONT + lax.broadcasted_iota(jnp.int32, (2 * TILE, 1), 0)
        for head in range(2):
            rows_low = q_ref[head, pl.ds(first_row, TILE + ROWPAD), :]
            grads = score_grads(head, first, TILE)
            padded = jnp.concatenate(
                [jnp.zeros((ROWPAD, TILE), jnp.float32), grads, jnp.zeros((8, TILE), jnp.float32)], axis=0
            )
            shifted = jnp.concatenate(
                [padded[lag : lag + TILE + ROWPAD] for lag in range(lags)], axis=1
            ).astype(jnp.bfloat16)
            raw_grads = jnp.where(columns <= source_ends, dot_nn(shifted, ttr_ref[head]), 0.0).astype(jnp.bfloat16)
            dq_ref[head, pl.ds(first_row, TILE + ROWPAD), :] += dot_nt(
                raw_grads, kt_ref[head, :, pl.ds(first, 2 * TILE)]
            )
            dkt_ref[head, :, pl.ds(first, 2 * TILE)] += dot_tn(rows_low, raw_grads)
            turned = dot_nt(k_ref[head, pl.ds(first, 2 * TILE), :], rows_low)
            turned = jnp.where(turned_columns <= turned_ends, turned, 0.0).astype(jnp.bfloat16)
            gram_ref[head] += dot_nn(turned, shifted)
        return carry

    lax.fori_loop(full, last + 1, mixed_step, 0)

    for head in range(2):
        parts = [dqcat_ref[head, :, lag * LANES : (lag + 1) * LANES] for lag in range(lags)]
        total = jnp.zeros((TILE + ROWPAD, LANES), jnp.float32)
        for lag in range(lags):
            pieces = [jnp.zeros((ROWPAD, LANES), jnp.float32), parts[lag], jnp.zeros((8, LANES), jnp.float32)]
            total = total + jnp.concatenate(pieces, axis=0)[lag : lag + TILE + ROWPAD]
        dq_ref[head, pl.ds(first_row, TILE + ROWPAD), :] += total

    @pl.when(block == blocks - 1)
    def _():
        for head in range(2):

            def tile_step(tile, carry):
                first = pl.multiple_of(tile * TILE, TILE)
                filtered = jnp.concatenate(
                    [dkcat_ref[head, lag * HD : (lag + 1) * HD, pl.ds(first, TILE)] for lag in range(lags)], axis=1
                ).astype(jnp.bfloat16)
                dkt_ref[head, :HD, pl.ds(first, 2 * TILE)] += dot_nn(filtered, ttr_ref[head])
                gram_ref[head] += dot_nn(k_ref[head, pl.ds(first, 2 * TILE), :HD], filtered)
                return carry

            lax.fori_loop(0, LEN // TILE, tile_step, 0)


def banded_taps(kernel, scale):
    heads, lags, taps = kernel.shape
    source = lax.broadcasted_iota(jnp.int32, (2 * TILE, TILE), 0)
    target = lax.broadcasted_iota(jnp.int32, (2 * TILE, TILE), 1)
    tap = target + FRONT + taps // 2 - source
    banded = jnp.zeros((heads, 2 * TILE, lags, TILE), jnp.float32)
    for index in range(taps):
        banded = jnp.where(
            (tap == index)[None, :, None, :], (kernel[:, :, index] * scale)[:, None, :, None], banded
        )
    return banded.reshape(heads, 2 * TILE, lags * TILE)


def gather_taps(gram, lags, taps, scale):
    heads = gram.shape[0]
    source = lax.broadcasted_iota(jnp.int32, (2 * TILE, TILE), 0)
    target = lax.broadcasted_iota(jnp.int32, (2 * TILE, TILE), 1)
    tap = target + FRONT + taps // 2 - source
    split = gram.reshape(heads, 2 * TILE, lags, TILE)
    sums = [
        jnp.sum(jnp.where((tap == index)[None, :, None, :], split, 0.0), axis=(1, 3)) for index in range(taps)
    ]
    return jnp.stack(sums, axis=2) * scale


def tile_bounds(starts):
    pics = starts.shape[0]
    blocks = LEN // TILE

    def ends(rows):
        found = rows
        for piece in range(pics):
            found = jnp.where(
                (rows >= starts[piece]) & (rows < starts[piece] + PIC), starts[piece] + PIC - 1, found
            )
        return found

    firsts = jnp.arange(blocks, dtype=jnp.int32) * TILE
    full = jnp.maximum((ends(firsts - 5) - 4) // TILE, 0)
    last = ends(firsts + TILE - 1) // TILE
    return jnp.concatenate([full, last])


def pad_heads(rows, heads, front, back):
    split = rows.reshape(LEN, heads, HD).transpose(1, 0, 2)
    return jnp.pad(split, ((0, 0), (front, back), (0, LANES - HD)))


def attention_inputs(queries, key_rows, values, kernel):
    heads = kernel.shape[0]
    q_pad = pad_heads(queries, heads, ROWPAD, 0)
    k_pad = pad_heads(key_rows, heads, FRONT, FRONT)
    kt_pad = k_pad.transpose(0, 2, 1)
    v_pad = pad_heads(values, heads, 0, 0)
    v_cat = v_pad.reshape(heads // 2, 2, LEN, LANES).transpose(0, 2, 1, 3).reshape(heads // 2, LEN, 2 * LANES)
    banded = banded_taps(kernel, 1.0 / math.sqrt(HD))
    thi = banded.astype(jnp.bfloat16)
    tlo = (banded - thi.astype(jnp.float32)).astype(jnp.bfloat16)
    return q_pad, k_pad, kt_pad, v_cat, thi, tlo


SMEM = pl.BlockSpec(memory_space=pltpu.SMEM)


def pair_spec(*shape):
    return pl.BlockSpec((2,) + shape, lambda group, block: (group,) + (0,) * len(shape))


def one_spec(*shape):
    return pl.BlockSpec((1,) + shape, lambda group, block: (group,) + (0,) * len(shape))


def row_spec(*shape):
    return pl.BlockSpec((2,) + shape, lambda group, block: (group, block) + (0,) * (len(shape) - 1))


def attention_forward(bounds, starts, q_pad, kt_pad, v_cat, thi, tlo, lags):
    heads = q_pad.shape[0]
    cols = LEN + 2 * FRONT
    return pl.pallas_call(
        functools.partial(forward_kernel, lags=lags, pics=starts.shape[0]),
        grid=(heads // 2, LEN // TILE),
        in_specs=[
            SMEM, SMEM,
            pair_spec(LEN + ROWPAD, LANES),
            pair_spec(LANES, cols),
            one_spec(LEN, 2 * LANES),
            pair_spec(2 * TILE, lags * TILE),
            pair_spec(2 * TILE, lags * TILE),
        ],
        out_specs=[row_spec(TILE, LEN), row_spec(TILE, 2 * LANES), row_spec(TILE, LANES)],
        out_shape=[
            jax.ShapeDtypeStruct((heads, LEN, LEN), jnp.bfloat16),
            jax.ShapeDtypeStruct((heads, LEN, 2 * LANES), jnp.float32),
            jax.ShapeDtypeStruct((heads, LEN, LANES), jnp.float32),
        ],
        scratch_shapes=[
            pltpu.VMEM((2, lags * LANES, LEN), jnp.bfloat16),
            pltpu.VMEM((2, TILE, LEN), jnp.float32),
            pltpu.VMEM((2, TILE, lags * LANES), jnp.bfloat16),
            pltpu.VMEM((2, TILE, LANES), jnp.float32),
            pltpu.VMEM((2, TILE, LANES), jnp.float32),
        ],
        compiler_params=pltpu.CompilerParams(vmem_limit_bytes=VMEM_BYTES),
        name="attention_forward",
    )(bounds, starts, q_pad, kt_pad, v_cat, thi, tlo)


def attention_backward(bounds, starts, mixing, q_pad, k_pad, kt_pad, v_cat, thi, tlo, e, o, inv, out_grads, lags):
    heads = q_pad.shape[0]
    cols = LEN + 2 * FRONT
    vt = v_cat.transpose(0, 2, 1)
    ttr = thi.transpose(0, 2, 1)
    return pl.pallas_call(
        functools.partial(backward_kernel, lags=lags, pics=starts.shape[0]),
        grid=(heads // 2, LEN // TILE),
        in_specs=[
            SMEM, SMEM, SMEM,
            pair_spec(LEN + ROWPAD, LANES),
            pair_spec(LANES, cols),
            pair_spec(cols, LANES),
            one_spec(2 * LANES, LEN),
            pair_spec(2 * TILE, lags * TILE),
            pair_spec(2 * TILE, lags * TILE),
            pair_spec(lags * TILE, 2 * TILE),
            row_spec(TILE, LEN), row_spec(TILE, 2 * LANES), row_spec(TILE, LANES),
            row_spec(TILE, LANES),
        ],
        out_specs=[
            pair_spec(LEN + ROWPAD, LANES),
            pair_spec(LANES, cols),
            one_spec(2 * LANES, LEN),
            pair_spec(2 * TILE, lags * TILE),
        ],
        out_shape=[
            jax.ShapeDtypeStruct((heads, LEN + ROWPAD, LANES), jnp.float32),
            jax.ShapeDtypeStruct((heads, LANES, cols), jnp.float32),
            jax.ShapeDtypeStruct((heads // 2, 2 * LANES, LEN), jnp.float32),
            jax.ShapeDtypeStruct((heads, 2 * TILE, lags * TILE), jnp.float32),
        ],
        scratch_shapes=[
            pltpu.VMEM((2, lags * LANES, LEN), jnp.bfloat16),
            pltpu.VMEM((2, lags * HD, LEN), jnp.float32),
            pltpu.VMEM((2, TILE, lags * LANES), jnp.float32),
            pltpu.VMEM((2, lags * HD, TILE), jnp.bfloat16),
            pltpu.VMEM((2, TILE, 2 * LANES), jnp.bfloat16),
            pltpu.VMEM((2, 2 * LANES, TILE), jnp.bfloat16),
            pltpu.VMEM((2, TILE, LANES), jnp.float32),
        ],
        compiler_params=pltpu.CompilerParams(vmem_limit_bytes=VMEM_BYTES),
        name="attention_backward",
    )(bounds, starts, mixing.reshape(-1), q_pad, kt_pad, k_pad, vt, thi, tlo, ttr, e, o, inv, out_grads)


def seq_forward(queries, key_rows, values, starts, kernel, mixing):
    heads, lags, taps = kernel.shape
    bounds = tile_bounds(starts)
    q_pad, k_pad, kt_pad, v_cat, thi, tlo = attention_inputs(queries, key_rows, values, kernel)
    e, o, inv = attention_forward(bounds, starts, q_pad, kt_pad, v_cat, thi, tlo, lags)
    split = o.reshape(heads // 2, 2, LEN, 2, LANES)[..., :HD]
    heads_out = jnp.einsum("gbiaf,gab->igaf", split, mixing, precision=lax.Precision.HIGHEST).reshape(LEN, heads, HD)
    return heads_out, (bounds, q_pad, k_pad, kt_pad, v_cat, thi, tlo, e, o, inv)


def seq_backward(saved, starts, kernel, mixing, out_grads):
    heads, lags, taps = kernel.shape
    bounds, q_pad, k_pad, kt_pad, v_cat, thi, tlo, e, o, inv = saved
    og = pad_heads(out_grads.reshape(LEN, heads * HD), heads, 0, 0)
    dq, dkt, dvt, gram = attention_backward(
        bounds, starts, mixing, q_pad, k_pad, kt_pad, v_cat, thi, tlo, e, o, inv, og, lags
    )
    query_back = dq[:, ROWPAD:, :HD].transpose(1, 0, 2).reshape(LEN, heads * HD).astype(jnp.bfloat16)
    key_back = dkt[:, :HD, FRONT : FRONT + LEN].transpose(2, 0, 1).reshape(LEN, heads * HD).astype(jnp.bfloat16)
    dv = dvt.reshape(heads // 2, 2, LANES, LEN)[:, :, :HD]
    value_back = dv.transpose(3, 0, 1, 2).reshape(LEN, heads * HD).astype(jnp.bfloat16)
    kernel_grad = gather_taps(gram, lags, taps, 1.0 / math.sqrt(HD))
    split = o.reshape(heads // 2, 2, LEN, 2, LANES)
    grads = og.reshape(heads // 2, 2, LEN, LANES).astype(jnp.float32)
    mixing_grad = jnp.sum(grads[:, :, None] * split.transpose(0, 3, 1, 2, 4), axis=(3, 4))
    return query_back, key_back, value_back, kernel_grad, mixing_grad


def rms_norm(values, gain):
    return values * lax.rsqrt(jnp.mean(values * values, axis=-1, keepdims=True) + epsilon) * gain


def group_norm(values, gain):
    centred = values - jnp.mean(values, axis=-1, keepdims=True)
    return centred * lax.rsqrt(jnp.mean(centred * centred, axis=-1, keepdims=True) + epsilon) * gain


def swiglu(gate, upper):
    return jax.nn.silu(gate) * upper


def project(left, right):
    return jnp.dot(left, right, preferred_element_type=jnp.float32)


def contract_rows(left, right):
    return lax.dot_general(
        left, right, (((0,), (0,)), ((), ())), preferred_element_type=jnp.float32
    )


def contract_cols(left, right):
    return lax.dot_general(
        left, right, (((1,), (1,)), ((), ())), preferred_element_type=jnp.float32
    )


def shards(
    layer_input,
    piece_starts,
    query_weight,
    key_weight,
    value_weight,
    out_weight,
    gate_weight,
    up_weight,
    down_weight,
    attention_gain,
    feedforward_gain,
    head_gain,
    score_kernel,
    head_mix,
    output_grad,
):
    width_local = query_weight.shape[1]
    heads_local = width_local // HD
    tensor_index = lax.axis_index("tensor")
    kernel_local = lax.dynamic_slice_in_dim(
        score_kernel, tensor_index * heads_local, heads_local, 0
    )
    mixing_local = lax.dynamic_slice_in_dim(
        head_mix, tensor_index * (heads_local // 2), heads_local // 2, 0
    )
    gain_local = lax.dynamic_slice_in_dim(head_gain, tensor_index * width_local, width_local, 0)
    local_rows = layer_input.shape[0]
    inputs = layer_input.astype(jnp.float32)
    normed, first_pull = jax.vjp(rms_norm, inputs, attention_gain)
    rows_all = lax.all_gather(normed.astype(jnp.bfloat16), "tensor", axis=0, tiled=True)
    query_full, key_full, value_full, out_full = (
        lax.all_gather(query_weight, "dp", axis=0, tiled=True),
        lax.all_gather(key_weight, "dp", axis=0, tiled=True),
        lax.all_gather(value_weight, "dp", axis=0, tiled=True),
        lax.all_gather(out_weight, "dp", axis=1, tiled=True),
    )
    queries = project(rows_all, query_full).astype(jnp.bfloat16)
    key_rows = project(rows_all, key_full).astype(jnp.bfloat16)
    values = project(rows_all, value_full).astype(jnp.bfloat16)
    starts = piece_starts[0]
    heads_out, saved = seq_forward(queries, key_rows, values, starts, kernel_local, mixing_local)
    normed_heads, group_pull = jax.vjp(group_norm, heads_out, gain_local.reshape(heads_local, HD))
    mixed_rows = normed_heads.astype(jnp.bfloat16).reshape(LEN, width_local)
    attended = lax.psum_scatter(
        project(
            lax.slice_in_dim(mixed_rows, 0, local_rows * lax.axis_size("tensor"), axis=0), out_full
        ).astype(jnp.bfloat16),
        "tensor",
        scatter_dimension=0,
        tiled=True,
    ).astype(jnp.float32)
    hidden = inputs + attended
    ffn_in, second_pull = jax.vjp(rms_norm, hidden, feedforward_gain)
    ffn_all = lax.all_gather(ffn_in.astype(jnp.bfloat16), "tensor", axis=0, tiled=True)
    gate_full, up_full, down_full = (
        lax.all_gather(gate_weight, "dp", axis=0, tiled=True),
        lax.all_gather(up_weight, "dp", axis=0, tiled=True),
        lax.all_gather(down_weight, "dp", axis=1, tiled=True),
    )
    gate = project(ffn_all, gate_full)
    upper = project(ffn_all, up_full)
    activated, act_pull = jax.vjp(swiglu, gate, upper)
    act_low = activated.astype(jnp.bfloat16)
    ffn_term = lax.psum_scatter(
        project(
            lax.slice_in_dim(act_low, 0, local_rows * lax.axis_size("tensor"), axis=0), down_full
        ).astype(jnp.bfloat16),
        "tensor",
        scatter_dimension=0,
        tiled=True,
    ).astype(jnp.float32)
    layer_output = (hidden + ffn_term).astype(jnp.bfloat16)
    query_back, key_back, value_back, out_back, gate_back, up_back, down_back = (
        lax.all_gather(query_weight, "dp", axis=0, tiled=True),
        lax.all_gather(key_weight, "dp", axis=0, tiled=True),
        lax.all_gather(value_weight, "dp", axis=0, tiled=True),
        lax.all_gather(out_weight, "dp", axis=1, tiled=True),
        lax.all_gather(gate_weight, "dp", axis=0, tiled=True),
        lax.all_gather(up_weight, "dp", axis=0, tiled=True),
        lax.all_gather(down_weight, "dp", axis=1, tiled=True),
    )
    grads_all = lax.all_gather(output_grad, "tensor", axis=0, tiled=True)
    act_grads = contract_cols(grads_all, down_back)
    down_part = contract_rows(act_low, grads_all)
    gate_grads, up_grads = act_pull(act_grads)
    gate_low = gate_grads.astype(jnp.bfloat16)
    up_low = up_grads.astype(jnp.bfloat16)
    gate_part = contract_rows(ffn_all, gate_low)
    up_part = contract_rows(ffn_all, up_low)
    gate_grad, up_grad, down_grad = (
        lax.psum_scatter(
            gate_part.astype(jnp.bfloat16), "dp", scatter_dimension=0, tiled=True
        ).astype(jnp.float32),
        lax.psum_scatter(
            up_part.astype(jnp.bfloat16), "dp", scatter_dimension=0, tiled=True
        ).astype(jnp.float32),
        lax.psum_scatter(
            down_part.astype(jnp.bfloat16), "dp", scatter_dimension=1, tiled=True
        ).astype(jnp.float32),
    )
    gate_rows = lax.slice_in_dim(gate_low, 0, local_rows * lax.axis_size("tensor"), axis=0)
    up_rows = lax.slice_in_dim(up_low, 0, local_rows * lax.axis_size("tensor"), axis=0)
    ffn_in_grad = lax.psum_scatter(
        (contract_cols(gate_rows, gate_back) + contract_cols(up_rows, up_back)).astype(
            jnp.bfloat16
        ),
        "tensor",
        scatter_dimension=0,
        tiled=True,
    ).astype(jnp.float32)
    hidden_part, feedforward_gain_part = second_pull(ffn_in_grad)
    hidden_grad = output_grad.astype(jnp.float32) + hidden_part
    attn_grads = lax.all_gather(hidden_grad.astype(jnp.bfloat16), "tensor", axis=0, tiled=True)
    mixed_grads = contract_cols(attn_grads, out_back)
    out_part = contract_rows(mixed_rows, attn_grads)
    head_grads, head_gain_part = group_pull(mixed_grads.reshape(LEN, heads_local, HD))
    head_low = head_grads.astype(jnp.bfloat16)
    query_low, key_low, value_low, kernel_part, mixing_part = seq_backward(
        saved, starts, kernel_local, mixing_local, head_low
    )
    query_part = contract_rows(rows_all, query_low)
    key_part = contract_rows(rows_all, key_low)
    value_part = contract_rows(rows_all, value_low)
    query_grad, key_grad, value_grad, out_weight_grad = (
        lax.psum_scatter(
            query_part.astype(jnp.bfloat16), "dp", scatter_dimension=0, tiled=True
        ).astype(jnp.float32),
        lax.psum_scatter(
            key_part.astype(jnp.bfloat16), "dp", scatter_dimension=0, tiled=True
        ).astype(jnp.float32),
        lax.psum_scatter(
            value_part.astype(jnp.bfloat16), "dp", scatter_dimension=0, tiled=True
        ).astype(jnp.float32),
        lax.psum_scatter(
            out_part.astype(jnp.bfloat16), "dp", scatter_dimension=1, tiled=True
        ).astype(jnp.float32),
    )
    total = contract_cols(query_low, query_back)
    total = total + contract_cols(key_low, key_back)
    normed_grad = lax.psum_scatter(
        (
            total
            + contract_cols(
                lax.slice_in_dim(value_low, 0, local_rows * lax.axis_size("tensor"), axis=0),
                value_back,
            )
        ).astype(jnp.bfloat16),
        "tensor",
        scatter_dimension=0,
        tiled=True,
    ).astype(jnp.float32)
    input_part, attention_gain_part = first_pull(normed_grad)
    input_grad = (hidden_grad + input_part).astype(jnp.bfloat16)
    head_gain_full = lax.dynamic_update_slice_in_dim(
        jnp.zeros(head_gain.shape, jnp.float32),
        head_gain_part.reshape(-1),
        tensor_index * width_local,
        0,
    )
    kernel_full = lax.dynamic_update_slice_in_dim(
        jnp.zeros(score_kernel.shape, jnp.float32),
        kernel_part,
        tensor_index * heads_local,
        0,
    )
    mixing_full = lax.dynamic_update_slice_in_dim(
        jnp.zeros(head_mix.shape, jnp.float32),
        mixing_part,
        tensor_index * (heads_local // 2),
        0,
    )
    attention_gain_grad, feedforward_gain_grad, head_gain_grad, score_kernel_grad, head_mix_grad = (
        lax.psum(
            (attention_gain_part, feedforward_gain_part, head_gain_full, kernel_full, mixing_full),
            ("dp", "tensor"),
        )
    )
    return (
        layer_output,
        input_grad,
        query_grad,
        key_grad,
        value_grad,
        out_weight_grad,
        gate_grad,
        up_grad,
        down_grad,
        attention_gain_grad,
        feedforward_gain_grad,
        head_gain_grad,
        score_kernel_grad,
        head_mix_grad,
    )


def solution(mesh):
    placed = (
        P(("dp", "tensor"), None),
        P("dp", None),
        P("dp", "tensor"),
        P("dp", "tensor"),
        P("dp", "tensor"),
        P("tensor", "dp"),
        P("dp", "tensor"),
        P("dp", "tensor"),
        P("tensor", "dp"),
        P(),
        P(),
        P(),
        P(),
        P(),
        P(("dp", "tensor"), None),
    )
    return jax.shard_map(
        shards,
        mesh=mesh,
        in_specs=placed,
        out_specs=(
            P(("dp", "tensor"), None),
            P(("dp", "tensor"), None),
            P("dp", "tensor"),
            P("dp", "tensor"),
            P("dp", "tensor"),
            P("tensor", "dp"),
            P("dp", "tensor"),
            P("dp", "tensor"),
            P("tensor", "dp"),
            P(),
            P(),
            P(),
            P(),
            P(),
        ),
        check_vma=False,
    )
```

time: 7560 us -> 1550 us (0.21)
  other arithmetic: 5550 us -> 106 us
  local copies, waits for them, and re-layouts: 787 us -> 83.1 us
  Pallas kernels: 0 us -> 287 us
  matrix products: 282 us -> 168 us
    reduce_sum x20 -> x13, other arithmetic: 2160 us -> 13.4 us  [the longest x1 6.92 us: seq_backward(): jnp.sum(grads[:, :, None] * split.transpose(0, 3, 1, 2, 4), axis=(3, 4))]
    add x17 -> x2, other arithmetic: 1560 us -> 0.02 us  [the longest x1 0.02 us: group_norm(): jnp.mean(centred * centred, axis=-1, keepdims=True) + epsilon]
    dynamic_update_slice x12 -> x0, other arithmetic: 1110 us -> none  [lag_step(): rows = lax.dynamic_slice_in_dim(padded, lags - 1 - row_lag, block_rows, 1)]
    add_any x24 -> x0, local copies, waits for them, and re-layouts: 669 us -> none  [the longest x12 668 us: conv_probs(): lax.scan(jax.checkpoint(lag_step), start, (jnp.arange(lags, dtype=jnp.int...]
    mul x14 -> x2, other arithmetic: 545 us -> 0.11 us  [the longest x1 0.11 us: banded_taps(): kernel[:, :, index] * scale]
    pallas_call x0 -> x2, Pallas kernels: none -> 287 us  [the longest x1 177 us: attention_backward(): pl.pallas_call(functools.partial(backward_kernel, lags=lags, pics=starts....]
    dot_general x12 -> x0, matrix products: 113 us -> none  [the longest x2 31.5 us: sequence_backward(): jnp.einsum('hqk,qhd->khd', score_low, extended, preferred_element_type=jn...]
  transfers between devices with their start and end apart: 22 -> 22, of which waited for: 14 -> 16; matrix products, arithmetic and copies ran while one was open for 87% -> 19% of each run, Pallas kernels for 0% -> 19%
where the time goes in v1:
time: 1550 us
  waiting for transfers between devices  834 us (54%)
  Pallas kernels  287 us (19%)
  matrix products  168 us (11%)
  other arithmetic  106 us (7%)
  local copies, waits for them, and re-layouts  83.1 us (5%)
  blocking collectives  47.2 us (3%)
  between operations  18.3 us (1%)
    pallas_call x1, Pallas kernels, attention_backward(): pl.pallas_call(functools.partial(backward_kernel, lags=lags, pics=starts....  177 us
    pallas_call x1, Pallas kernels, attention_forward(): pl.pallas_call(functools.partial(forward_kernel, lags=lags, pics=starts.s...  110 us
    all_gather x1, waiting for transfers between devices, shards(): lax.all_gather(normed.astype(jnp.bfloat16), 'tensor', axis=0, tiled=True)  98.1 us
    all_gather x1, waiting for transfers between devices, shards(): lax.all_gather(ffn_in.astype(jnp.bfloat16), 'tensor', axis=0, tiled=True)  98.1 us
    all_gather x1, waiting for transfers between devices, shards(): grads_all = lax.all_gather(output_grad, 'tensor', axis=0, tiled=True)  97.5 us
    reduce_scatter x1, waiting for transfers between devices, shards(): lax.psum_scatter(project(lax.slice_in_dim(mixed_rows, 0, local_rows * lax...  93.3 us
    reduce_scatter x1, waiting for transfers between devices, shards(): lax.psum_scatter((total + contract_cols(lax.slice_in_dim(value_low, 0, lo...  92.5 us
    reduce_scatter x1, waiting for transfers between devices, shards(): lax.psum_scatter((contract_cols(gate_rows, gate_back) + contract_cols(up_...  90.1 us
  transfers between devices with their start and end apart: 22, of which 16 were waited for; matrix products, arithmetic and copies ran while one was open for 19% of the time, Pallas kernels for 19%

profile of v1, /device:TPU:0, one launch (start us, length us, event | category | flops | bytes accessed | tf_op | source)
XLA Modules:
  0.0 1545.5 jit_solution(845849911514920372)
XLA Ops:
  36.8 98.1 %all-gather.12.cloned.1.call-done = bf16[1664,1536]{1,0:T(8,128)(2,1)} async-done(((bf16[416,1536]{1,0:T(8,128)(2,1)}), bf16[1664,1536]{1,0:T(8,128)(2,1)}) %all-gather.12.cloned.1.call-update) | async-done | bytes 5111824 | tf_op jit(solution)/shard_map/all_gather | solution.py:530
  141.0 18.2 %all-gather.16.cloned.1.call-done = bf16[1536,384]{1,0:T(8,128)(2,1)} async-done(((bf16[192,384]{1,0:T(8,128)(2,1)}), bf16[1536,384]{1,0:T(8,128)(2,1)}) %all-gather.16.cloned.1.call-update) | async-done | bytes 1179664 | tf_op jit(solution)/shard_map/all_gather | solution.py:533
  173.2 11.8 all-gather.18.cloned.1.call-done
  192.8 110.1 %attention_forward.1 = (bf16[4,1664,1664]{2,1,0:T(8,128)(2,1)}, f32[4,1664,256]{2,1,0:T(8,128)}, f32[4,1664,128]{2,1,0:T(8,128)}) custom-call(s32[26]{0:T(128)} %pad_add_fusion.bounds_ref, s32[2]{0:T(128)} %bitcast.274, bf16[4,1680,128]{2,1,0:T(8,128)(2,1)} %pad.15.q_ref, bf16[4,128,1792]{2,1,0:T(8,128)(2,1)} %copy.156.kt_ref, ...), custom_call_target="tpu_custom_call" | custom-call | tf_op jit(solution)/shard_map/attention_forward/pallas_call | solution.py:368
  312.1 17.7 %fusion.4 = f32[2,2,1664,96]{3,1,2,0:T(2,128)S(1)} fusion(f32[2,2,1664,2,128]{4,3,2,1,0:T(2,128)} %reshape.480, f32[2,2,2]{1,2,0:T(2,128)S(1)} %copy.188), kind=kLoop, calls=%fused_computation.10 | loop fusion | flops 1916928 | bytes 7667744
  348.1 93.3 %reduce-scatter.12.cloned.1.call-done = bf16[416,1536]{1,0:T(8,128)(2,1)} async-done(((bf16[1664,1536]{1,0:T(8,128)(2,1)}), bf16[416,1536]{1,0:T(8,128)(2,1)}) %reduce-scatter.12.cloned.1.call-update) | async-done | bytes 1277968 | tf_op jit(solution)/shard_map/reduce_scatter | solution.py:544
  447.6 28.6 %all-gather.24.cloned.1.call-done = bf16[1536,1024]{1,0:T(8,128)(2,1)} async-done(((bf16[192,1024]{1,0:T(8,128)(2,1)}), bf16[1536,1024]{1,0:T(8,128)(2,1)}) %all-gather.24.cloned.1.call-update) | async-done | bytes 3145744 | tf_op jit(solution)/shard_map/all_gather | solution.py:556
  476.2 98.1 %all-gather.22.cloned.1.call-done = bf16[1664,1536]{1,0:T(8,128)(2,1)} async-done(((bf16[416,1536]{1,0:T(8,128)(2,1)}), bf16[1664,1536]{1,0:T(8,128)(2,1)}) %all-gather.22.cloned.1.call-update) | async-done | bytes 5111824 | tf_op jit(solution)/shard_map/all_gather | solution.py:554
  574.3 10.6 fusion.45
  584.9 22.0 %all-gather.26.cloned.1.call-done = bf16[1536,1024]{1,0:T(8,128)(2,1)} async-done(((bf16[192,1024]{1,0:T(8,128)(2,1)}), bf16[1536,1024]{1,0:T(8,128)(2,1)}) %all-gather.26.cloned.1.call-update) | async-done | bytes 3145744 | tf_op jit(solution)/shard_map/all_gather | solution.py:557
  606.9 10.4 fusion.46
  617.3 23.7 %all-gather.28.cloned.1.call-done = bf16[1024,1536]{0,1:T(8,128)(2,1)} async-done(((bf16[1024,192]{0,1:T(8,128)(2,1)}), bf16[1024,1536]{0,1:T(8,128)(2,1)}) %all-gather.28.cloned.1.call-update) | async-done | bytes 3145744 | tf_op jit(solution)/shard_map/all_gather | solution.py:558
  641.0 97.5 %all-gather.30.cloned.1.call-done = bf16[1664,1536]{1,0:T(8,128)(2,1)} async-done(((bf16[416,1536]{1,0:T(8,128)(2,1)}), bf16[1664,1536]{1,0:T(8,128)(2,1)}) %all-gather.30.cloned.1.call-update) | async-done | bytes 5111824 | tf_op jit(solution)/shard_map/all_gather | solution.py:582
  738.5 15.0 multiply_convert_fusion
  772.1 90.1 %reduce-scatter.16.cloned.1.call-done = bf16[416,1536]{1,0:T(8,128)(2,1)} async-done(((bf16[1664,1536]{1,0:T(8,128)(2,1)}), bf16[416,1536]{1,0:T(8,128)(2,1)}) %reduce-scatter.16.cloned.1.call-update) | async-done | bytes 1277968 | tf_op jit(solution)/shard_map/reduce_scatter | solution.py:603
  879.7 10.4 convolution_convert_fusion.3
  915.8 50.3 %all-gather.32.cloned.1.call-done = bf16[1664,1536]{1,0:T(8,128)(2,1)} async-done(((bf16[416,1536]{1,0:T(8,128)(2,1)}), bf16[1664,1536]{1,0:T(8,128)(2,1)}) %all-gather.32.cloned.1.call-update) | async-done | bytes 5111824 | tf_op jit(solution)/shard_map/all_gather | solution.py:613
  998.0 177.3 %attention_backward.1 = (f32[4,1680,128]{2,1,0:T(8,128)}, f32[4,128,1792]{2,1,0:T(8,128)}, f32[2,256,1664]{2,1,0:T(8,128)}, f32[4,256,768]{2,1,0:T(8,128)}) custom-call(s32[26]{0:T(128)} %pad_add_fusion.bounds_ref, s32[2]{0:T(128)} %bitcast.275, f32[8]{0:T(128)} %reshape.482.mix_ref, bf16[4,1680,128]{2,1,0:T(8,128)(2,1)} %pad.15.q_ref, ...), custom_call_target="tpu_custom_call" | custom-call | tf_op jit(solution)/shard_map/attention_backward/pallas_call | solution.py:402
  1257.8 16.3 %copy.178 = f32[2,2,1664,128]{3,1,2,0:T(2,128)S(1)} copy(bf16[2,2,1664,128]{3,2,1,0:T(8,128)(2,1)S(1)} %bitcast.237) | data formatting | bytes 5111808 | tf_op jit(solution)/shard_map/convert_element_type | solution.py:466
  1285.3 18.5 %reduce-scatter.24.cloned.1.call-done = bf16[192,384]{1,0:T(8,128)(2,1)} async-done(((bf16[1536,384]{1,0:T(8,128)(2,1)}), bf16[192,384]{1,0:T(8,128)(2,1)}) %reduce-scatter.24.cloned.1.call-update) | async-done | bytes 147472 | tf_op jit(solution)/shard_map/reduce_scatter | solution.py:631
  1305.4 38.2 %reduce-scatter.26.cloned.1.call-done = bf16[384,192]{0,1:T(8,128)(2,1)} async-done(((bf16[384,1536]{0,1:T(8,128)(2,1)}), bf16[384,192]{0,1:T(8,128)(2,1)}) %reduce-scatter.26.cloned.1.call-update) | async-done | bytes 147472 | tf_op jit(solution)/shard_map/reduce_scatter | solution.py:634
  1345.2 92.5 %reduce-scatter.18.cloned.1.call-done = bf16[416,1536]{1,0:T(8,128)(2,1)} async-done(((bf16[1664,1536]{1,0:T(8,128)(2,1)}), bf16[416,1536]{1,0:T(8,128)(2,1)}) %reduce-scatter.18.cloned.1.call-update) | async-done | bytes 1277968 | tf_op jit(solution)/shard_map/reduce_scatter | solution.py:640
  1439.9 47.2 %all-reduce.4 = (f32[1536]{0:T(1024)}, f32[1536]{0:T(1024)}, f32[1536]{0:T(1024)}, f32[16,6,11]{0,1,2:T(8,128)}, f32[8,2,2]{0,2,1:T(2,128)}) all-reduce(f32[1536]{0:T(1024)S(1)} %get-tuple-element.41, f32[1536]{0:T(1024)S(1)} %copy-done.67, f32[1536]{0:T(1024)S(1)} %dynamic_update_slice.9, ...), channel_id=1, replica_groups=mesh['dp'=8,'tensor'=4] {'dp','tensor'}, use_global_device_ids=true, to_apply=%region_20.21 | all-reduce | flops 5696 | bytes 45568 | tf_op jit(solution)/shard_map/psum | solution.py:673
  1487.2 46.2 %reduce-scatter.14.cloned.1.call-done = bf16[416,1536]{1,0:T(8,128)(2,1)} async-done(((bf16[1664,1536]{1,0:T(8,128)(2,1)}), bf16[416,1536]{1,0:T(8,128)(2,1)}) %reduce-scatter.14.cloned.1.call-update) | async-done | bytes 1277968 | tf_op jit(solution)/shard_map/reduce_scatter | solution.py:564
  (395 shorter events, 285.0 us)
Async XLA Ops:
  7.2 29.6 %all-gather.14.cloned.1.call-start = ((), (), s32[]{:S(2)}) async-start(), calls=%async_computation.12 | async-start | bytes 1327104 | tf_op jit(solution)/shard_map/all_gather | solution.py:532
  8.0 126.9 %all-gather.12.cloned.1.call-start = ((), (), s32[]{:S(2)}) async-start(), calls=%async_computation.11 | async-start | bytes 6389760 | tf_op jit(solution)/shard_map/all_gather | solution.py:530
  13.5 145.7 %all-gather.16.cloned.1.call-start = ((), (), s32[]{:S(2)}) async-start(), calls=%async_computation.13 | async-start | bytes 1327104 | tf_op jit(solution)/shard_map/all_gather | solution.py:533
  14.3 170.7 %all-gather.18.cloned.1.call-start = ((), (), s32[]{:S(2)}) async-start(), calls=%async_computation.14 | async-start | bytes 1327104 | tf_op jit(solution)/shard_map/all_gather | solution.py:534
  14.9 325.7 %all-gather.20.cloned.1.call-start = ((), (), s32[]{:S(2)}) async-start(), calls=%async_computation.15 | async-start | bytes 1327104 | tf_op jit(solution)/shard_map/all_gather | solution.py:535
  15.4 426.0 %reduce-scatter.12.cloned.1.call-start = ((), (), s32[]{:S(2)}) async-start(), calls=%async_computation.16 | async-start | bytes 6389760 | tf_op jit(solution)/shard_map/reduce_scatter | solution.py:544
  347.3 128.9 %all-gather.24.cloned.1.call-start = ((), (), s32[]{:S(2)}) async-start(), calls=%async_computation.18 | async-start | bytes 3538944 | tf_op jit(solution)/shard_map/all_gather | solution.py:556
  348.1 226.2 %all-gather.22.cloned.1.call-start = ((), (), s32[]{:S(2)}) async-start(), calls=%async_computation.17 | async-start | bytes 6389760 | tf_op jit(solution)/shard_map/all_gather | solution.py:554
  443.9 422.2 %copy-start.64 = (f32[416]{0:T(512)}, f32[416]{0:T(512)S(1)}, u32[]{:S(2)}) copy-start(f32[416]{0:T(512)S(1)} %fusion.38) | copy-start | bytes 4996
  445.5 161.5 %all-gather.26.cloned.1.call-start = ((), (), s32[]{:S(2)}) async-start(), calls=%async_computation.19 | async-start | bytes 3538944 | tf_op jit(solution)/shard_map/all_gather | solution.py:557
  446.2 194.8 %all-gather.28.cloned.1.call-start = ((), (), s32[]{:S(2)}) async-start(), calls=%async_computation.20 | async-start | bytes 3538944 | tf_op jit(solution)/shard_map/all_gather | solution.py:558
  446.8 291.7 %all-gather.30.cloned.1.call-start = ((), (), s32[]{:S(2)}) async-start(), calls=%async_computation.22 | async-start | bytes 6389760 | tf_op jit(solution)/shard_map/all_gather | solution.py:582
  447.5 414.8 %reduce-scatter.16.cloned.1.call-start = ((), (), s32[]{:S(2)}) async-start(), calls=%async_computation.23 | async-start | bytes 6389760 | tf_op jit(solution)/shard_map/reduce_scatter | solution.py:603
  772.1 194.0 %all-gather.32.cloned.1.call-start = ((), (), s32[]{:S(2)}) async-start(), calls=%async_computation.24 | async-start | bytes 6389760 | tf_op jit(solution)/shard_map/all_gather | solution.py:613
  869.5 370.5 %reduce-scatter.28.cloned.1.call-start = ((), (), s32[]{:S(2)}) async-start(), calls=%async_computation.30 | async-start | bytes 3538944 | tf_op jit(solution)/shard_map/reduce_scatter | solution.py:591
  879.6 362.5 %reduce-scatter.30.cloned.1.call-start = ((), (), s32[]{:S(2)}) async-start(), calls=%async_computation.31 | async-start | bytes 3538944 | tf_op jit(solution)/shard_map/reduce_scatter | solution.py:594
  890.1 354.1 %reduce-scatter.32.cloned.1.call-start = ((), (), s32[]{:S(2)}) async-start(), calls=%async_computation.32 | async-start | bytes 3538944 | tf_op jit(solution)/shard_map/reduce_scatter | solution.py:597
  900.4 381.6 %reduce-scatter.20.cloned.1.call-start = ((), (), s32[]{:S(2)}) async-start(), calls=%async_computation.26 | async-start | bytes 1327104 | tf_op jit(solution)/shard_map/reduce_scatter | solution.py:625
  1185.2 98.5 %reduce-scatter.22.cloned.1.call-start = ((), (), s32[]{:S(2)}) async-start(), calls=%async_computation.27 | async-start | bytes 1327104 | tf_op jit(solution)/shard_map/reduce_scatter | solution.py:628
  1193.9 109.8 %reduce-scatter.24.cloned.1.call-start = ((), (), s32[]{:S(2)}) async-start(), calls=%async_computation.28 | async-start | bytes 1327104 | tf_op jit(solution)/shard_map/reduce_scatter | solution.py:631
  1204.0 139.6 %reduce-scatter.26.cloned.1.call-start = ((), (), s32[]{:S(2)}) async-start(), calls=%async_computation.29 | async-start | bytes 1327104 | tf_op jit(solution)/shard_map/reduce_scatter | solution.py:634
  1211.5 226.2 %reduce-scatter.18.cloned.1.call-start = ((), (), s32[]{:S(2)}) async-start(), calls=%async_computation.25 | async-start | bytes 6389760 | tf_op jit(solution)/shard_map/reduce_scatter | solution.py:640
  1228.6 304.7 %reduce-scatter.14.cloned.1.call-start = ((), (), s32[]{:S(2)}) async-start(), calls=%async_computation.21 | async-start | bytes 6389760 | tf_op jit(solution)/shard_map/reduce_scatter | solution.py:564
  1281.1 252.2 %copy-start.7 = (bf16[416,1536]{1,0:T(8,128)(2,1)S(1)}, bf16[416,1536]{1,0:T(8,128)(2,1)}, u32[]{:S(2)}) copy-start(bf16[416,1536]{1,0:T(8,128)(2,1)} %reduce-scatter.12.cloned.1.call-done) | copy-start | bytes 3833860
  (81 other events, 2205.2 us)
Sparse Core Ops, SparseCore 0:
  9.9 26.7 all-gather.13
  38.9 95.8 all-gather.11
  136.7 22.4 all-gather.15
  160.9 24.0 all-gather.17
  186.8 24.2 all-gather.19
  347.4 93.9 reduce-scatter.11
  443.3 32.8 all-gather.23
  478.3 95.8 all-gather.21
  576.2 30.7 all-gather.25
  608.6 32.3 all-gather.27
  642.6 95.8 all-gather.29
  772.2 90.0 reduce-scatter.15
  869.6 96.3 all-gather.31
  969.3 44.6 reduce-scatter.27
  1017.6 46.3 reduce-scatter.29
  1067.2 46.2 reduce-scatter.31
  1185.3 38.0 reduce-scatter.19
  1226.5 36.8 reduce-scatter.21
  1266.9 36.7 reduce-scatter.23
  1306.8 36.7 reduce-scatter.25
  1346.0 91.6 reduce-scatter.17
  1440.1 93.1 reduce-scatter.13

commit v2 on v1

v2 whole, which is shorter than its diff:
```python
import functools
import math

import jax
import jax.numpy as jnp
from jax import lax
from jax.experimental import pallas as pl
from jax.experimental.pallas import tpu as pltpu
from jax.sharding import PartitionSpec as P

HD = 96
LEN = 1664
PIC = 256
TILE = 128
LANES = 128
FRONT = 64
ROWPAD = 16
COLS = LEN + 2 * FRONT
VMEM_BYTES = 56 * 1024 * 1024
epsilon = 1e-05


def dot_nn(left, right):
    return jnp.dot(left, right, preferred_element_type=jnp.float32)


def dot_nt(left, right):
    return lax.dot_general(left, right, (((1,), (1,)), ((), ())), preferred_element_type=jnp.float32)


def dot_tn(left, right):
    return lax.dot_general(left, right, (((0,), (0,)), ((), ())), preferred_element_type=jnp.float32)


def row_ends(rows, starts_ref, pics):
    ends = rows
    for piece in range(pics):
        first = starts_ref[piece]
        ends = jnp.where((rows >= first) & (rows < first + PIC), first + PIC - 1, ends)
    return ends


def stage_queries(qkv_ref, qpad_ref):
    for head in range(2):
        qpad_ref[head, :ROWPAD, :] = jnp.zeros((ROWPAD, LANES), jnp.bfloat16)
        qpad_ref[head, ROWPAD:, :] = qkv_ref[:, head * LANES : (head + 1) * LANES]


def stage_keys(qkv_ref, kpad_ref, kt_ref):
    for head in range(2):
        kpad_ref[head, :FRONT, :] = jnp.zeros((FRONT, LANES), jnp.bfloat16)
        kpad_ref[head, FRONT + LEN :, :] = jnp.zeros((FRONT, LANES), jnp.bfloat16)
        kpad_ref[head, FRONT : FRONT + LEN, :] = qkv_ref[:, (2 + head) * LANES : (3 + head) * LANES]

        def tile_step(tile, carry):
            first = pl.multiple_of(tile * TILE, TILE)
            rows = kpad_ref[head, pl.ds(first, TILE), :].astype(jnp.float32)
            kt_ref[head, :, pl.ds(first, TILE)] = jnp.transpose(rows).astype(jnp.bfloat16)
            return carry

        lax.fori_loop(0, COLS // TILE, tile_step, 0)


def filter_keys(kt_ref, thi_ref, tlo_ref, kcat_ref, lags):
    for head in range(2):

        def tile_step(tile, carry):
            first = pl.multiple_of(tile * TILE, TILE)
            window = kt_ref[head, :, pl.ds(first, 2 * TILE)]
            filtered = dot_nn(window, thi_ref[head]) + dot_nn(window, tlo_ref[head])
            for lag in range(lags):
                kcat_ref[head, lag * LANES : (lag + 1) * LANES, pl.ds(first, TILE)] = filtered[
                    :, lag * TILE : (lag + 1) * TILE
                ].astype(jnp.bfloat16)
            return carry

        lax.fori_loop(0, LEN // TILE, tile_step, 0)


def lagged(rows, lags):
    return jnp.concatenate(
        [rows[ROWPAD - lag : ROWPAD - lag + TILE] for lag in range(lags)], axis=1
    ).astype(jnp.bfloat16)


def centre(parts, weights):
    inside = lax.broadcasted_iota(jnp.int32, (TILE, LANES), 1) < HD
    mixed = parts[0] * weights[0] + parts[1] * weights[1]
    mean = jnp.sum(mixed, axis=1, keepdims=True) / HD
    centred = jnp.where(inside, mixed - mean, 0.0)
    spread = lax.rsqrt(jnp.sum(centred * centred, axis=1, keepdims=True) / HD + epsilon)
    return centred * spread, spread, inside


def forward_kernel(
    bounds_ref, starts_ref, mix_ref, gain_ref, qkv_ref, thi_ref, tlo_ref,
    e_ref, o_ref, inv_ref, z_ref,
    qpad_ref, kpad_ref, kt_ref, kcat_ref, c_ref, qcat_ref, top_ref, sum_ref,
    *, lags, pics, group,
):
    block = pl.program_id(0)
    blocks = pl.num_programs(0)
    first_row = pl.multiple_of(block * TILE, TILE)

    @pl.when(block == 0)
    def _():
        stage_queries(qkv_ref, qpad_ref)
        stage_keys(qkv_ref, kpad_ref, kt_ref)
        filter_keys(kt_ref, thi_ref, tlo_ref, kcat_ref, lags)

    full = bounds_ref[block]
    last = bounds_ref[blocks + block]
    for head in range(2):
        rows = qpad_ref[head, pl.ds(first_row, TILE + ROWPAD), :].astype(jnp.float32)
        qcat_ref[head] = lagged(rows, lags)
        top_ref[head] = jnp.full((TILE, LANES), -1e30, jnp.float32)
        sum_ref[head] = jnp.zeros((TILE, LANES), jnp.float32)
        o_ref[head] = jnp.zeros(o_ref.shape[1:], jnp.float32)

    def full_tiles(first, width):
        for head in range(2):
            logits = dot_nn(qcat_ref[head], kcat_ref[head, :, pl.ds(first, width)])
            c_ref[head, :, pl.ds(first, width)] = logits
            top = top_ref[head]
            for part in range(width // LANES):
                top = jnp.maximum(top, logits[:, part * LANES : (part + 1) * LANES])
            top_ref[head] = top

    def full_step(pair, carry):
        full_tiles(pl.multiple_of(pair * 2 * TILE, 2 * TILE), 2 * TILE)
        return carry

    lax.fori_loop(0, full // 2, full_step, 0)

    @pl.when(full % 2 == 1)
    def _():
        full_tiles(pl.multiple_of((full - 1) * TILE, TILE), TILE)

    source_rows = first_row - ROWPAD + lax.broadcasted_iota(jnp.int32, (TILE + ROWPAD, 1), 0)
    source_ends = row_ends(source_rows, starts_ref, pics)
    target_rows = first_row + lax.broadcasted_iota(jnp.int32, (TILE, 1), 0)
    target_ends = row_ends(target_rows, starts_ref, pics)

    def mixed_step(tile, carry):
        first = pl.multiple_of(tile * TILE, TILE)
        columns = first - FRONT + lax.broadcasted_iota(jnp.int32, (1, 2 * TILE), 1)
        source_allowed = columns <= source_ends
        target_allowed = first + lax.broadcasted_iota(jnp.int32, (1, TILE), 1) <= target_ends
        for head in range(2):
            raw = dot_nn(qpad_ref[head, pl.ds(first_row, TILE + ROWPAD), :], kt_ref[head, :, pl.ds(first, 2 * TILE)])
            raw = jnp.where(source_allowed, raw, 0.0)
            high = raw.astype(jnp.bfloat16)
            low = (raw - high.astype(jnp.float32)).astype(jnp.bfloat16)
            taps = dot_nn(high, thi_ref[head]) + dot_nn(low, thi_ref[head]) + dot_nn(high, tlo_ref[head])
            logits = taps[ROWPAD:, :TILE]
            for lag in range(1, lags):
                logits = logits + taps[ROWPAD - lag : ROWPAD - lag + TILE, lag * TILE : (lag + 1) * TILE]
            logits = jnp.where(target_allowed, logits, -1e30)
            c_ref[head, :, pl.ds(first, TILE)] = logits
            top_ref[head] = jnp.maximum(top_ref[head], logits)
        return carry

    lax.fori_loop(full, last + 1, mixed_step, 0)

    for head in range(2):
        top_ref[head] = jnp.broadcast_to(
            jnp.max(top_ref[head], axis=1, keepdims=True), (TILE, LANES)
        )

    def soft_tiles(first, width):
        for head in range(2):
            parts = []
            total = sum_ref[head]
            for part in range(width // LANES):
                logits = c_ref[head, :, pl.ds(first + part * LANES, LANES)]
                value = jnp.exp(logits - top_ref[head])
                total = total + value
                parts.append(value.astype(jnp.bfloat16))
            sum_ref[head] = total
            weights = parts[0] if len(parts) == 1 else jnp.concatenate(parts, axis=1)
            e_ref[head, :, pl.ds(first, width)] = weights
            o_ref[head] += dot_nn(weights, qkv_ref[pl.ds(first, width), 4 * LANES :])

    def soft_step(pair, carry):
        soft_tiles(pl.multiple_of(pair * 2 * TILE, 2 * TILE), 2 * TILE)
        return carry

    lax.fori_loop(0, (last + 1) // 2, soft_step, 0)

    @pl.when(last % 2 == 0)
    def _():
        soft_tiles(pl.multiple_of(last * TILE, TILE), TILE)

    for head in range(2):
        inverse = 1.0 / jnp.sum(sum_ref[head], axis=1, keepdims=True)
        inv_ref[head] = jnp.broadcast_to(inverse, (TILE, LANES))
        o_ref[head] = o_ref[head] * inverse
    for out_head in range(2):
        lanes = slice(out_head * LANES, (out_head + 1) * LANES)
        weights = [mix_ref[group * 4 + out_head * 2 + head] for head in range(2)]
        normal, _, _ = centre([o_ref[head, :, lanes] for head in range(2)], weights)
        z_ref[:, lanes] = (normal * gain_ref[:, lanes]).astype(jnp.bfloat16)


def fold_rows(values):
    return jnp.sum(values.reshape(TILE // 8, 8, LANES), axis=0)


def backward_kernel(
    bounds_ref, starts_ref, mix_ref, gain_ref, qkv_ref, thi_ref, tlo_ref, ttr_ref,
    e_ref, o_ref, inv_ref, dz_ref, *refs, lags, pics, group,
):
    (
        low_ref, gram_ref, dgain_ref, dmix_ref,
        qpad_ref, kpad_ref, kt_ref, vt_ref, kcat_ref,
        dq_ref, dkt_ref, dvt_ref, dkcat_ref, dqcat_ref, qcatt_ref, x_ref, xt_ref, delta_ref,
    ) = refs[-18:]
    block = pl.program_id(0)
    blocks = pl.num_programs(0)
    first_row = pl.multiple_of(block * TILE, TILE)

    @pl.when(block == 0)
    def _():
        stage_queries(qkv_ref, qpad_ref)
        stage_keys(qkv_ref, kpad_ref, kt_ref)
        filter_keys(kt_ref, thi_ref, tlo_ref, kcat_ref, lags)

        def tile_step(tile, carry):
            first = pl.multiple_of(tile * TILE, TILE)
            for head in range(2):
                rows = qkv_ref[pl.ds(first, TILE), (4 + head) * LANES : (5 + head) * LANES].astype(jnp.float32)
                vt_ref[head * LANES : (head + 1) * LANES, pl.ds(first, TILE)] = jnp.transpose(rows).astype(jnp.bfloat16)
            return carry

        lax.fori_loop(0, LEN // TILE, tile_step, 0)
        dkcat_ref[...] = jnp.zeros(dkcat_ref.shape, jnp.float32)
        dq_ref[...] = jnp.zeros(dq_ref.shape, jnp.float32)
        dkt_ref[...] = jnp.zeros(dkt_ref.shape, jnp.float32)
        dvt_ref[...] = jnp.zeros(dvt_ref.shape, jnp.float32)
        gram_ref[...] = jnp.zeros(gram_ref.shape, jnp.float32)
        dgain_ref[...] = jnp.zeros(dgain_ref.shape, jnp.float32)
        dmix_ref[...] = jnp.zeros(dmix_ref.shape, jnp.float32)

    full = bounds_ref[block]
    last = bounds_ref[blocks + block]
    out_grads = []
    for out_head in range(2):
        lanes = slice(out_head * LANES, (out_head + 1) * LANES)
        parts = [o_ref[head, :, lanes] for head in range(2)]
        weights = [mix_ref[group * 4 + out_head * 2 + head] for head in range(2)]
        normal, spread, inside = centre(parts, weights)
        grads = dz_ref[:, lanes].astype(jnp.float32)
        dgain_ref[0, :, lanes] += fold_rows(grads * normal)
        grads = grads * gain_ref[:, lanes]
        mean = jnp.sum(grads, axis=1, keepdims=True) / HD
        slope = jnp.sum(grads * normal, axis=1, keepdims=True) / HD
        grads = jnp.where(inside, (grads - mean - normal * slope) * spread, 0.0)
        grads = grads.astype(jnp.bfloat16).astype(jnp.float32)
        for head in range(2):
            dmix_ref[0, 2 * out_head + head] += fold_rows(grads * parts[head])
        out_grads.append(grads)
    for head in range(2):
        rows = qpad_ref[head, pl.ds(first_row, TILE + ROWPAD), :].astype(jnp.float32)
        for lag in range(lags):
            turned = jnp.transpose(rows[ROWPAD - lag : ROWPAD - lag + TILE])
            qcatt_ref[head, lag * HD : (lag + 1) * HD, :] = turned[:HD].astype(jnp.bfloat16)
        dqcat_ref[head] = jnp.zeros(dqcat_ref.shape[1:], jnp.float32)
        inverse = inv_ref[head]
        delta = jnp.zeros((TILE, 1), jnp.float32)
        for out_head in range(2):
            weight = mix_ref[group * 4 + out_head * 2 + head]
            scaled = out_grads[out_head] * (inverse * weight)
            lanes = slice(out_head * LANES, (out_head + 1) * LANES)
            delta = delta + jnp.sum(scaled * o_ref[head, :, lanes], axis=1, keepdims=True)
            x_ref[head, :, lanes] = scaled.astype(jnp.bfloat16)
            xt_ref[head, lanes, :] = jnp.transpose(scaled).astype(jnp.bfloat16)
        delta_ref[head] = jnp.broadcast_to(delta, (TILE, LANES))

    def score_grads(head, first, width):
        prob_grads = dot_nn(x_ref[head], vt_ref[:, pl.ds(first, width)])
        weights = e_ref[head, :, pl.ds(first, width)]
        dvt_ref[:, pl.ds(first, width)] += dot_nn(xt_ref[head], weights)
        delta = delta_ref[head]
        parts = [
            weights[:, part * LANES : (part + 1) * LANES].astype(jnp.float32)
            * (prob_grads[:, part * LANES : (part + 1) * LANES] - delta)
            for part in range(width // LANES)
        ]
        return parts[0] if len(parts) == 1 else jnp.concatenate(parts, axis=1)

    def full_tiles(first, width):
        for head in range(2):
            grads = score_grads(head, first, width).astype(jnp.bfloat16)
            dqcat_ref[head] += dot_nt(grads, kcat_ref[head, :, pl.ds(first, width)])
            dkcat_ref[head, :, pl.ds(first, width)] += dot_nn(qcatt_ref[head], grads)

    def full_step(pair, carry):
        full_tiles(pl.multiple_of(pair * 2 * TILE, 2 * TILE), 2 * TILE)
        return carry

    lax.fori_loop(0, full // 2, full_step, 0)

    @pl.when(full % 2 == 1)
    def _():
        full_tiles(pl.multiple_of((full - 1) * TILE, TILE), TILE)

    source_rows = first_row - ROWPAD + lax.broadcasted_iota(jnp.int32, (TILE + ROWPAD, 1), 0)
    source_ends = row_ends(source_rows, starts_ref, pics)
    turned_rows = first_row - ROWPAD + lax.broadcasted_iota(jnp.int32, (1, TILE + ROWPAD), 1)
    turned_ends = row_ends(turned_rows, starts_ref, pics)

    def mixed_step(tile, carry):
        first = pl.multiple_of(tile * TILE, TILE)
        columns = first - FRONT + lax.broadcasted_iota(jnp.int32, (1, 2 * TILE), 1)
        turned_columns = first - FRONT + lax.broadcasted_iota(jnp.int32, (2 * TILE, 1), 0)
        for head in range(2):
            rows_low = qpad_ref[head, pl.ds(first_row, TILE + ROWPAD), :]
            grads = score_grads(head, first, TILE)
            padded = jnp.concatenate(
                [jnp.zeros((ROWPAD, TILE), jnp.float32), grads, jnp.zeros((8, TILE), jnp.float32)], axis=0
            )
            shifted = jnp.concatenate(
                [padded[lag : lag + TILE + ROWPAD] for lag in range(lags)], axis=1
            ).astype(jnp.bfloat16)
            raw_grads = jnp.where(columns <= source_ends, dot_nn(shifted, ttr_ref[head]), 0.0).astype(jnp.bfloat16)
            dq_ref[head, pl.ds(first_row, TILE + ROWPAD), :] += dot_nt(
                raw_grads, kt_ref[head, :, pl.ds(first, 2 * TILE)]
            )
            dkt_ref[head, :, pl.ds(first, 2 * TILE)] += dot_tn(rows_low, raw_grads)
            turned = dot_nt(kpad_ref[head, pl.ds(first, 2 * TILE), :], rows_low)
            turned = jnp.where(turned_columns <= turned_ends, turned, 0.0).astype(jnp.bfloat16)
            gram_ref[head] += dot_nn(turned, shifted)
        return carry

    lax.fori_loop(full, last + 1, mixed_step, 0)

    for head in range(2):
        total = jnp.zeros((TILE + ROWPAD, LANES), jnp.float32)
        for lag in range(lags):
            part = dqcat_ref[head, :, lag * LANES : (lag + 1) * LANES]
            pieces = [jnp.zeros((ROWPAD, LANES), jnp.float32), part, jnp.zeros((8, LANES), jnp.float32)]
            total = total + jnp.concatenate(pieces, axis=0)[lag : lag + TILE + ROWPAD]
        dq_ref[head, pl.ds(first_row, TILE + ROWPAD), :] += total

    @pl.when(block == blocks - 1)
    def _():
        for head in range(2):

            def tile_step(tile, carry):
                first = pl.multiple_of(tile * TILE, TILE)
                filtered = jnp.concatenate(
                    [dkcat_ref[head, lag * HD : (lag + 1) * HD, pl.ds(first, TILE)] for lag in range(lags)], axis=1
                ).astype(jnp.bfloat16)
                dkt_ref[head, :HD, pl.ds(first, 2 * TILE)] += dot_nn(filtered, ttr_ref[head])
                gram_ref[head] += dot_nn(kpad_ref[head, pl.ds(first, 2 * TILE), :HD], filtered)
                return carry

            lax.fori_loop(0, LEN // TILE, tile_step, 0)
            low_ref[:, head * LANES : (head + 1) * LANES] = dq_ref[head, ROWPAD:, :].astype(jnp.bfloat16)

            def turn_step(tile, carry):
                first = pl.multiple_of(tile * TILE, TILE)
                half = TILE // 2
                lanes = slice((2 + head) * LANES, (3 + head) * LANES)
                front = jnp.transpose(dkt_ref[head, :, pl.ds(first, TILE)]).astype(jnp.bfloat16)
                back = jnp.transpose(dkt_ref[head, :, pl.ds(first + TILE, TILE)]).astype(jnp.bfloat16)
                low_ref[pl.ds(first, half), lanes] = front[half:]
                low_ref[pl.ds(first + half, half), lanes] = back[:half]
                lanes = slice((4 + head) * LANES, (5 + head) * LANES)
                turned = jnp.transpose(dvt_ref[head * LANES : (head + 1) * LANES, pl.ds(first, TILE)])
                low_ref[pl.ds(first, TILE), lanes] = turned.astype(jnp.bfloat16)
                return carry

            lax.fori_loop(0, LEN // TILE, turn_step, 0)


def banded_taps(kernel, scale):
    heads, lags, taps = kernel.shape
    source = lax.broadcasted_iota(jnp.int32, (2 * TILE, TILE), 0)
    target = lax.broadcasted_iota(jnp.int32, (2 * TILE, TILE), 1)
    tap = target + FRONT + taps // 2 - source
    banded = jnp.zeros((heads, 2 * TILE, lags, TILE), jnp.float32)
    for index in range(taps):
        banded = jnp.where(
            (tap == index)[None, :, None, :], (kernel[:, :, index] * scale)[:, None, :, None], banded
        )
    return banded.reshape(heads, 2 * TILE, lags * TILE)


def gather_taps(gram, lags, taps, scale):
    heads = gram.shape[0]
    source = lax.broadcasted_iota(jnp.int32, (2 * TILE, TILE), 0)
    target = lax.broadcasted_iota(jnp.int32, (2 * TILE, TILE), 1)
    tap = target + FRONT + taps // 2 - source
    split = gram.reshape(heads, 2 * TILE, lags, TILE)
    sums = [
        jnp.sum(jnp.where((tap == index)[None, :, None, :], split, 0.0), axis=(1, 3)) for index in range(taps)
    ]
    return jnp.stack(sums, axis=2) * scale


def tile_bounds(starts):
    blocks = LEN // TILE
    firsts = jnp.arange(blocks, dtype=jnp.int32) * TILE
    full = jnp.maximum((row_ends(firsts - 5, starts, starts.shape[0]) - 4) // TILE, 0)
    last = row_ends(firsts + TILE - 1, starts, starts.shape[0]) // TILE
    return jnp.concatenate([full, last])


SMEM = pl.BlockSpec(memory_space=pltpu.SMEM)


def pair_spec(group, *shape):
    return pl.BlockSpec((2,) + shape, lambda block: (group,) + (0,) * len(shape))


def row_spec(*shape):
    return pl.BlockSpec((2,) + shape, lambda block: (0, block) + (0,) * (len(shape) - 1))


def wide_spec(group, rows, width):
    return pl.BlockSpec((rows, width), lambda block: (0, group))


def tile_spec(width):
    return pl.BlockSpec((TILE, width), lambda block: (block, 0))


def attention_forward(group, bounds, starts, mixing, gain, qkv, thi, tlo, lags):
    return pl.pallas_call(
        functools.partial(forward_kernel, lags=lags, pics=starts.shape[0], group=group),
        grid=(LEN // TILE,),
        in_specs=[
            SMEM, SMEM, SMEM,
            wide_spec(group, 1, 2 * LANES),
            wide_spec(group, LEN, 6 * LANES),
            pair_spec(group, 2 * TILE, lags * TILE),
            pair_spec(group, 2 * TILE, lags * TILE),
        ],
        out_specs=[
            row_spec(TILE, LEN), row_spec(TILE, 2 * LANES), row_spec(TILE, LANES),
            tile_spec(2 * LANES),
        ],
        out_shape=[
            jax.ShapeDtypeStruct((2, LEN, LEN), jnp.bfloat16),
            jax.ShapeDtypeStruct((2, LEN, 2 * LANES), jnp.float32),
            jax.ShapeDtypeStruct((2, LEN, LANES), jnp.float32),
            jax.ShapeDtypeStruct((LEN, 2 * LANES), jnp.bfloat16),
        ],
        scratch_shapes=[
            pltpu.VMEM((2, LEN + ROWPAD, LANES), jnp.bfloat16),
            pltpu.VMEM((2, COLS, LANES), jnp.bfloat16),
            pltpu.VMEM((2, LANES, COLS), jnp.bfloat16),
            pltpu.VMEM((2, lags * LANES, LEN), jnp.bfloat16),
            pltpu.VMEM((2, TILE, LEN), jnp.float32),
            pltpu.VMEM((2, TILE, lags * LANES), jnp.bfloat16),
            pltpu.VMEM((2, TILE, LANES), jnp.float32),
            pltpu.VMEM((2, TILE, LANES), jnp.float32),
        ],
        compiler_params=pltpu.CompilerParams(vmem_limit_bytes=VMEM_BYTES),
        cost_estimate=pl.CostEstimate(flops=70_000_000_000, transcendentals=0, bytes_accessed=20_000_000),
        name="attention_forward",
    )(bounds, starts, mixing.reshape(-1), gain, qkv, thi, tlo)


def attention_backward(group, bounds, starts, mixing, gain, qkv, thi, tlo, ttr, e, o, inv, dz, low, lags):
    width = qkv.shape[1]
    joined = [] if low is None else [low]
    return pl.pallas_call(
        functools.partial(backward_kernel, lags=lags, pics=starts.shape[0], group=group),
        grid=(LEN // TILE,),
        in_specs=[
            SMEM, SMEM, SMEM,
            wide_spec(group, 1, 2 * LANES),
            wide_spec(group, LEN, 6 * LANES),
            pair_spec(group, 2 * TILE, lags * TILE),
            pair_spec(group, 2 * TILE, lags * TILE),
            pair_spec(group, lags * TILE, 2 * TILE),
            row_spec(TILE, LEN), row_spec(TILE, 2 * LANES), row_spec(TILE, LANES),
            tile_spec(2 * LANES),
        ] + [pl.BlockSpec(memory_space=pl.ANY)] * len(joined),
        out_specs=[
            wide_spec(group, LEN, 6 * LANES),
            pair_spec(0, 2 * TILE, lags * TILE),
            pl.BlockSpec((1, 8, 2 * LANES), lambda block: (0, 0, 0)),
            pl.BlockSpec((1, 4, 8, LANES), lambda block: (0, 0, 0, 0)),
        ],
        out_shape=[
            jax.ShapeDtypeStruct((LEN, width), jnp.bfloat16),
            jax.ShapeDtypeStruct((2, 2 * TILE, lags * TILE), jnp.float32),
            jax.ShapeDtypeStruct((1, 8, 2 * LANES), jnp.float32),
            jax.ShapeDtypeStruct((1, 4, 8, LANES), jnp.float32),
        ],
        scratch_shapes=[
            pltpu.VMEM((2, LEN + ROWPAD, LANES), jnp.bfloat16),
            pltpu.VMEM((2, COLS, LANES), jnp.bfloat16),
            pltpu.VMEM((2, LANES, COLS), jnp.bfloat16),
            pltpu.VMEM((2 * LANES, LEN), jnp.bfloat16),
            pltpu.VMEM((2, lags * LANES, LEN), jnp.bfloat16),
            pltpu.VMEM((2, LEN + ROWPAD, LANES), jnp.float32),
            pltpu.VMEM((2, LANES, COLS), jnp.float32),
            pltpu.VMEM((2 * LANES, LEN), jnp.float32),
            pltpu.VMEM((2, lags * HD, LEN), jnp.float32),
            pltpu.VMEM((2, TILE, lags * LANES), jnp.float32),
            pltpu.VMEM((2, lags * HD, TILE), jnp.bfloat16),
            pltpu.VMEM((2, TILE, 2 * LANES), jnp.bfloat16),
            pltpu.VMEM((2, 2 * LANES, TILE), jnp.bfloat16),
            pltpu.VMEM((2, TILE, LANES), jnp.float32),
        ],
        compiler_params=pltpu.CompilerParams(vmem_limit_bytes=VMEM_BYTES),
        cost_estimate=pl.CostEstimate(flops=115_000_000_000, transcendentals=0, bytes_accessed=20_000_000),
        input_output_aliases={12: 0} if joined else {},
        name="attention_backward",
    )(bounds, starts, mixing.reshape(-1), gain, qkv, thi, tlo, ttr, e, o, inv, dz, *joined)


def pad_heads(columns, heads):
    rows = columns.shape[0]
    split = columns.reshape(rows, heads, HD)
    return jnp.pad(split, ((0, 0), (0, 0), (0, LANES - HD)))


def drop_pads(columns, heads):
    rows = columns.shape[0]
    return columns.reshape(rows, heads, LANES)[:, :, :HD].reshape(rows, heads * HD)


def join_pairs(queries, key_rows, values, heads):
    rows = queries.shape[0]
    parts = [pad_heads(part, heads).reshape(rows, heads // 2, 2, LANES) for part in (queries, key_rows, values)]
    return jnp.stack(parts, axis=2).reshape(rows, heads * 3 * LANES)


def split_pairs(columns, heads):
    rows = columns.shape[0]
    split = columns.reshape(rows, heads // 2, 3, 2, LANES)[..., :HD]
    return [split[:, :, part].reshape(rows, heads * HD) for part in range(3)]


def rms_norm(values, gain):
    return values * lax.rsqrt(jnp.mean(values * values, axis=-1, keepdims=True) + epsilon) * gain


def swiglu(gate, upper):
    return jax.nn.silu(gate) * upper


def shift(values, step):
    size = lax.axis_size("tensor")
    return lax.ppermute(values, "tensor", [(index, (index + step) % size) for index in range(size)])


def swap(values):
    size = lax.axis_size("tensor")
    return lax.ppermute(values, "tensor", [(index, index ^ 1) for index in range(size)])


def line_gather(rows, chunks):
    size = lax.axis_size("tensor")
    index = lax.axis_index("tensor")
    count = rows.shape[0]
    part = count // chunks
    gathered = jnp.zeros((size * count,) + rows.shape[1:], rows.dtype)
    gathered = lax.dynamic_update_slice_in_dim(gathered, rows, index * count, 0)
    rising = [rows[chunk * part : (chunk + 1) * part] for chunk in range(chunks)]
    falling = list(rising)
    from_below, from_above = [], []
    for step in range(1, size):
        upward = [(i, i + 1) for i in range(size - 1) if i >= step - 1]
        downward = [(i + 1, i) for i in range(size - 1) if i + 1 <= size - step]
        for chunk in range(chunks):
            rising[chunk] = lax.ppermute(rising[chunk], "tensor", upward)
            falling[chunk] = lax.ppermute(falling[chunk], "tensor", downward)
        from_below.append(list(rising))
        from_above.append(list(falling))
    for step in range(1, size):
        first = ((index - step) % size) * count
        for chunk in range(chunks):
            piece = jnp.where(index >= step, from_below[step - 1][chunk], from_above[size - step - 1][chunk])
            gathered = lax.dynamic_update_slice_in_dim(gathered, piece, first + chunk * part, 0)
    return gathered


def line_scatter(parts, count):
    size = lax.axis_size("tensor")
    index = lax.axis_index("tensor")

    def block(values, position):
        first = jnp.clip(position, 0, size - 1) * count
        return lax.dynamic_slice_in_dim(values, first, count, 0).astype(jnp.float32)

    rising = [None] * len(parts)
    falling = [None] * len(parts)
    for step in range(1, size):
        upward = [(i, i + 1) for i in range(size - 1) if i <= step - 1]
        downward = [(i + 1, i) for i in range(size - 1) if size - 2 - i <= step - 1]
        for chunk, values in enumerate(parts):
            up = block(values, size - step + index)
            down = block(values, step + index - size)
            if step > 1:
                up = up + rising[chunk].astype(jnp.float32)
                down = down + falling[chunk].astype(jnp.float32)
            rising[chunk] = lax.ppermute(up.astype(jnp.bfloat16), "tensor", upward)
            falling[chunk] = lax.ppermute(down.astype(jnp.bfloat16), "tensor", downward)
    sums = [
        block(values, index) + (rising[chunk].astype(jnp.float32) + falling[chunk].astype(jnp.float32))
        for chunk, values in enumerate(parts)
    ]
    return jnp.concatenate(sums, axis=1)


def sum_all(values):
    for axis in ("tensor", "dp"):
        size = lax.axis_size(axis)
        step = 1
        while step < size:
            values = values + lax.ppermute(values, axis, [(i, i ^ step) for i in range(size)])
            step *= 2
    return values


def after(values, *others):
    return lax.optimization_barrier((values,) + others)[0]


def shards(
    layer_input,
    piece_starts,
    query_weight,
    key_weight,
    value_weight,
    out_weight,
    gate_weight,
    up_weight,
    down_weight,
    attention_gain,
    feedforward_gain,
    head_gain,
    score_kernel,
    head_mix,
    output_grad,
):
    size = lax.axis_size("tensor")
    index = lax.axis_index("tensor")
    width_local = query_weight.shape[1]
    heads = width_local // HD
    pairs = heads // 2
    wide = 2 * LANES
    hidden_local = gate_weight.shape[1]
    count = layer_input.shape[0]
    lags, taps = score_kernel.shape[1:]
    score_scale = 1.0 / math.sqrt(HD)

    inputs = layer_input.astype(jnp.float32)
    normed, first_pull = jax.vjp(rms_norm, inputs, attention_gain)
    normed_low = normed.astype(jnp.bfloat16)
    rows_all = line_gather(normed_low, 2)

    query_weight, key_weight, value_weight = after((query_weight, key_weight, value_weight), normed_low)
    qkv_full = lax.all_gather(
        join_pairs(query_weight, key_weight, value_weight, heads), "dp", axis=0, tiled=True
    )
    kernel_local = lax.dynamic_slice_in_dim(score_kernel, index * heads, heads, 0)
    mixing_local = lax.dynamic_slice_in_dim(head_mix, index * pairs, pairs, 0)
    gain_local = lax.dynamic_slice_in_dim(head_gain, index * width_local, width_local, 0)
    gain_pad = pad_heads(gain_local[None], heads).reshape(1, heads * LANES)
    starts = piece_starts[0]
    bounds = tile_bounds(starts)
    banded = banded_taps(kernel_local, score_scale)
    taps_high = banded.astype(jnp.bfloat16)
    taps_low = (banded - taps_high.astype(jnp.float32)).astype(jnp.bfloat16)
    taps_turned = taps_high.transpose(0, 2, 1)

    out_own = pad_heads(after(out_weight, rows_all).T, heads).reshape(-1, heads * LANES)
    out_parts = [out_own] + [shift(out_own, step) for step in range(1, size)]
    out_full = lax.all_gather(
        jnp.concatenate(
            [part[:, pair * wide : (pair + 1) * wide] for pair in range(pairs) for part in out_parts], axis=1
        ),
        "dp", axis=0, tiled=True,
    )
    qkv = dot_nn(rows_all, qkv_full).astype(jnp.bfloat16)
    qkv, taps_high, taps_low, taps_turned = lax.optimization_barrier((qkv, taps_high, taps_low, taps_turned))
    gate_up_own = after(jnp.concatenate([gate_weight, up_weight], axis=1), rows_all)
    down_own = after(down_weight.T, rows_all)
    gate_up = [gate_up_own] + [shift(gate_up_own, step) for step in range(2, size, 2)]
    down = [down_own] + [shift(down_own, step) for step in range(2, size, 2)]
    grads_swapped = swap(after(output_grad, rows_all))

    saved = []
    token_parts = []
    for pair in range(pairs):
        weights, parts_out, inverse, normed_heads = attention_forward(
            pair, bounds, starts, mixing_local, gain_pad, qkv, taps_high, taps_low, lags
        )
        saved.append((weights, parts_out, inverse))
        if pair == 0:
            gate_up, down, grads_swapped = after((gate_up, down, grads_swapped), normed_heads)
        for step in range(size):
            first = ((index + step) % size) * count
            part = lax.dynamic_slice_in_dim(normed_heads, first, count, 0)
            token_parts.append(part if step == 0 else shift(part, step))
    token_heads = jnp.concatenate(token_parts, axis=1)
    grads_two = jnp.concatenate([output_grad, grads_swapped], axis=0)

    gate_up_full = lax.all_gather(
        jnp.concatenate([part[:, :hidden_local] for part in gate_up] + [part[:, hidden_local:] for part in gate_up], axis=1),
        "dp", axis=0, tiled=True,
    )
    down_full = lax.all_gather(jnp.concatenate(down, axis=1), "dp", axis=0, tiled=True)
    hidden_width = down_full.shape[1]
    gate_full = gate_up_full[:, :hidden_width]
    up_full = gate_up_full[:, hidden_width:]

    hidden = inputs + dot_nt(token_heads, out_full)
    ffn_in, second_pull = jax.vjp(rms_norm, hidden, feedforward_gain)
    ffn_low = ffn_in.astype(jnp.bfloat16)
    ffn_two = jnp.concatenate([ffn_low, swap(ffn_low)], axis=0)
    gate = dot_nn(ffn_two, gate_full)
    upper = dot_nn(ffn_two, up_full)
    activated, act_pull = jax.vjp(swiglu, gate, upper)
    act_low = activated.astype(jnp.bfloat16)
    down_part = dot_tn(grads_two, act_low).astype(jnp.bfloat16)
    down_sum = lax.psum_scatter(down_part, "dp", scatter_dimension=0, tiled=True)
    act_grads = dot_nn(after(grads_two, down_part), down_full)
    gate_grads, up_grads = act_pull(act_grads)
    gate_low = gate_grads.astype(jnp.bfloat16)
    up_low = up_grads.astype(jnp.bfloat16)

    def ffn_back(rows):
        return dot_nt(gate_low[rows], gate_full) + dot_nt(up_low[rows], up_full)

    ffn_back_sent = ffn_back(slice(count, None)).astype(jnp.bfloat16)
    ffn_back_kept = ffn_back(slice(0, count))
    ffn_two_later, gate_later, up_later = after((ffn_two, gate_low, up_low), ffn_back_kept, ffn_back_sent)
    gate_up_part = dot_tn(ffn_two_later, jnp.concatenate([gate_later, up_later], axis=1)).astype(jnp.bfloat16)
    gate_up_sum = lax.psum_scatter(gate_up_part, "dp", scatter_dimension=0, tiled=True)
    ffn_in_grad = ffn_back_kept + after(swap(ffn_back_sent), gate_up_part).astype(jnp.float32)
    hidden_part, feedforward_gain_part = second_pull(ffn_in_grad)
    hidden_grad = output_grad.astype(jnp.float32) + hidden_part
    hidden_low = hidden_grad.astype(jnp.bfloat16)

    head_back = dot_nn(hidden_low, out_full).astype(jnp.bfloat16)
    head_grads = []
    for pair in range(pairs):
        rows = jnp.zeros((LEN, wide), jnp.bfloat16)
        for step in range(size):
            first = (pair * size + step) * wide
            part = head_back[:, first : first + wide]
            part = part if step == 0 else shift(part, -step)
            rows = lax.dynamic_update_slice_in_dim(rows, part, ((index + step) % size) * count, 0)
        head_grads.append(rows)

    act_later, hidden_later = after((act_low, hidden_low), head_back)
    out_part = dot_tn(hidden_later, token_heads).astype(jnp.bfloat16)
    ffn_out_sent = dot_nt(act_later[count:], down_full).astype(jnp.bfloat16)
    ffn_term = dot_nt(act_later[:count], down_full) + swap(ffn_out_sent).astype(jnp.float32)
    layer_output = (hidden + ffn_term).astype(jnp.bfloat16)

    head_grads[0] = after(head_grads[0], out_part, ffn_out_sent)
    def owned(groups, stride):
        joined = jnp.concatenate(groups[0], axis=1).astype(jnp.float32)
        for step in range(1, len(groups)):
            joined = joined + shift(jnp.concatenate(groups[step], axis=1), -step * stride).astype(jnp.float32)
        return joined

    def columns(values, first, width):
        return values[:, first * width : (first + 1) * width]

    low = None
    grams, gain_parts, mixing_parts = [], [], []
    for pair in range(pairs):
        if pair == pairs - 1:
            head_grads[pair], gate_up_sum, down_sum = lax.optimization_barrier(
                (head_grads[pair], gate_up_sum, down_sum)
            )
        low, gram, gain_part, mixing_part = attention_backward(
            pair, bounds, starts, mixing_local, gain_pad, qkv, taps_high, taps_low, taps_turned,
            *saved[pair], head_grads[pair], low, lags,
        )
        if pair == 0:
            out_sum = lax.psum_scatter(after(out_part, gram), "dp", scatter_dimension=0, tiled=True)
        grams.append(gram)
        gain_parts.append(gain_part)
        mixing_parts.append(mixing_part)
    gram = jnp.concatenate(grams, axis=0)
    gain_parts = jnp.concatenate(gain_parts, axis=0)
    mixing_parts = jnp.concatenate(mixing_parts, axis=0)
    parts = hidden_width // hidden_local
    ffn_sum = owned(
        [
            [columns(gate_up_sum, part, hidden_local), columns(gate_up_sum, parts + part, hidden_local),
             columns(down_sum, part, hidden_local)]
            for part in range(parts)
        ],
        2,
    )
    low, ffn_sum, out_sum = lax.optimization_barrier((low, ffn_sum, out_sum))
    gate_grad, up_grad, down_grad = [columns(ffn_sum, part, hidden_local) for part in range(3)]
    down_grad = down_grad.T

    half = qkv_full.shape[0] // 2
    normed_parts = [
        dot_nt(low, qkv_full[chunk * half : (chunk + 1) * half]).astype(jnp.bfloat16) for chunk in range(2)
    ]
    attention_gain_part = jnp.concatenate(
        [
            jnp.sum(
                part.astype(jnp.float32) * rows_all[:, chunk * half : (chunk + 1) * half].astype(jnp.float32), axis=0
            )
            for chunk, part in enumerate(normed_parts)
        ]
    ) / attention_gain
    normed_grad = line_scatter(normed_parts, count)
    qkv_part = dot_tn(after(rows_all, *normed_parts), low).astype(jnp.bfloat16)
    qkv_sum = lax.psum_scatter(qkv_part, "dp", scatter_dimension=0, tiled=True).astype(jnp.float32)
    input_part = first_pull(normed_grad)[0]
    input_grad = (hidden_grad + input_part).astype(jnp.bfloat16)
    query_grad, key_grad, value_grad = split_pairs(qkv_sum, heads)
    out_total = owned(
        [[columns(out_sum, pair * size + step, wide) for pair in range(pairs)] for step in range(size)], 1
    )
    out_weight_grad = drop_pads(out_total, heads).T

    kernel_part = gather_taps(gram, lags, taps, score_scale)
    mixing_part = jnp.sum(mixing_parts, axis=(2, 3)).reshape(mixing_local.shape)
    head_gain_part = drop_pads(jnp.sum(gain_parts, axis=1).reshape(1, heads * LANES), heads).reshape(-1)

    def placed(part, whole, first):
        return lax.dynamic_update_slice_in_dim(jnp.zeros(whole.shape, jnp.float32), part, first, 0)

    small = (
        attention_gain_part,
        feedforward_gain_part,
        placed(head_gain_part, head_gain, index * width_local),
        placed(kernel_part, score_kernel, index * heads),
        placed(mixing_part, head_mix, index * pairs),
    )
    packed = jnp.concatenate([part.reshape(-1) for part in small])
    packed = jnp.pad(packed, (0, -packed.shape[0] % 1024)).reshape(-1, LANES)
    packed = sum_all(packed).reshape(-1)
    sums = []
    first = 0
    for part in small:
        sums.append(packed[first : first + part.size].reshape(part.shape))
        first += part.size
    return (
        layer_output,
        input_grad,
        query_grad,
        key_grad,
        value_grad,
        out_weight_grad,
        gate_grad,
        up_grad,
        down_grad,
        *sums,
    )


def solution(mesh):
    placed = (
        P(("dp", "tensor"), None),
        P("dp", None),
        P("dp", "tensor"),
        P("dp", "tensor"),
        P("dp", "tensor"),
        P("tensor", "dp"),
        P("dp", "tensor"),
        P("dp", "tensor"),
        P("tensor", "dp"),
        P(),
        P(),
        P(),
        P(),
        P(),
        P(("dp", "tensor"), None),
    )
    return jax.shard_map(
        shards,
        mesh=mesh,
        in_specs=placed,
        out_specs=(
            P(("dp", "tensor"), None),
            P(("dp", "tensor"), None),
            P("dp", "tensor"),
            P("dp", "tensor"),
            P("dp", "tensor"),
            P("tensor", "dp"),
            P("dp", "tensor"),
            P("dp", "tensor"),
            P("tensor", "dp"),
            P(),
            P(),
            P(),
            P(),
            P(),
        ),
        check_vma=False,
    )
```

time: 1550 us -> 952 us (0.61)
  waiting for transfers between devices: 834 us -> 164 us
  starting transfers between devices: 1.46 us -> 117 us
  blocking collectives: 47.2 us -> 0 us
  Pallas kernels: 287 us -> 330 us
  other arithmetic: 106 us -> 65.9 us
    all_gather x11 -> x4, waiting for transfers between devices: 450 us -> 0.02 us  [the longest x1 0.02 us: shards(): lax.all_gather(jnp.concatenate(down, axis=1), 'dp', axis=0, tiled=True)]
    reduce_scatter x11 -> x4, waiting for transfers between devices: 379 us -> 0.04 us  [the longest x1 0.02 us: shards(): lax.psum_scatter(after(out_part, gram), 'dp', scatter_dimension=0, tiled=...]
    ppermute x0 -> x54, waiting for transfers between devices: none -> 164 us  [the longest x4 55.2 us: swap(): lax.ppermute(values, 'tensor', [(index, index ^ 1) for index in range(siz...]
    ppermute x0 -> x54, starting transfers between devices: none -> 116 us  [the longest x21 38.7 us: shift(): lax.ppermute(values, 'tensor', [(index, (index + step) % size) for index...]
    psum x1 -> x0, blocking collectives: 47.2 us -> none  [shards(): lax.psum((attention_gain_part, feedforward_gain_part, head_gain_full, ker...]
    pallas_call x1 -> x2, Pallas kernels: 177 us -> 206 us  [attention_backward(): pl.pallas_call(functools.partial(backward_kernel, lags=lags, pics=starts....]
    convert_element_type x3 -> x0, local copies, waits for them, and re-layouts: 19.6 us -> none  [the longest x1 16.3 us: seq_backward(): grads = og.reshape(heads // 2, 2, LEN, LANES).astype(jnp.float32)]
    reduce_sum x5 -> x2, other arithmetic: 19.4 us -> 1.56 us  [the longest x1 0.83 us: shards(): mixing_part = jnp.sum(mixing_parts, axis=(2, 3)).reshape(mixing_local.shape)]
  transfers between devices with their start and end apart: 22 -> 62, of which waited for: 16 -> 21; matrix products, arithmetic and copies ran while one was open for 19% -> 28% of each run, Pallas kernels for 19% -> 35%
where the time goes in v2:
time: 952 us; the launch traced here: 941 us
  Pallas kernels  330 us (35%)
  waiting for transfers between devices  164 us (17%)
  matrix products  161 us (17%)
  starting transfers between devices  117 us (12%)
  local copies, waits for them, and re-layouts  85.2 us (9%)
  other arithmetic  65.9 us (7%)
  between operations  19 us (2%)
    pallas_call x2, Pallas kernels, attention_backward(): pl.pallas_call(functools.partial(backward_kernel, lags=lags, pics=starts....  206 us
    pallas_call x2, Pallas kernels, attention_forward(): pl.pallas_call(functools.partial(forward_kernel, lags=lags, pics=starts.s...  123 us
    dot_general x9, matrix products, dot_nt(): lax.dot_general(left, right, (((1,), (1,)), ((), ())), preferred_element_...  64.3 us
    ppermute x4, waiting for transfers between devices, swap(): lax.ppermute(values, 'tensor', [(index, index ^ 1) for index in range(siz...  55.2 us
    dot_general x5, matrix products, dot_nn(): return jnp.dot(left, right, preferred_element_type=jnp.float32)  50.7 us
    dot_general x4, matrix products, dot_tn(): lax.dot_general(left, right, (((0,), (0,)), ((), ())), preferred_element_...  46 us
    ppermute x21, starting transfers between devices, shift(): lax.ppermute(values, 'tensor', [(index, (index + step) % size) for index...  38.7 us
    ppermute x6, starting transfers between devices, line_scatter(): rising[chunk] = lax.ppermute(up.astype(jnp.bfloat16), 'tensor', upward)  36.1 us
  transfers between devices with their start and end apart: 62, of which 21 were waited for; matrix products, arithmetic and copies ran while one was open for 28% of the time, Pallas kernels for 35%

profile of v2, /device:TPU:0, one launch (start us, length us, event | category | flops | bytes accessed | tf_op | source)
XLA Modules:
  0.0 941.4 jit_solution(8571180890694781222)
XLA Ops:
  34.9 12.4 %collective-permute-done.5 = bf16[208,1536]{1,0:T(8,128)(2,1)} collective-permute-done((bf16[208,1536]{1,0:T(8,128)(2,1)S(1)}, bf16[208,1536]{1,0:T(8,128)(2,1)}, u32[]{:S(2)}, u32[]{:S(2)}) %collective-permute-start.5) | collective-permute-done | bytes 639008 | tf_op jit(solution)/shard_map/ppermute | solution.py:573
  66.6 8.1 collective-permute-done.6
  93.7 7.6 collective-permute-done.7
  112.2 10.1 %collective-permute-start.19 = (bf16[192,512]{1,0:T(8,128)(2,1)S(1)}, bf16[192,512]{1,0:T(8,128)(2,1)S(1)}, u32[]{:S(2)}, u32[]{:S(2)}) collective-permute-start(bf16[192,512]{1,0:T(8,128)(2,1)S(1)} %bitcast.179), channel_id=1, source_target_pairs={{0,2},{1,3},{2,0},{3,1},{4,6},{5,7},{6,4},{7,5},{8,10},{9,11},{10,... | collective-permute-start | bytes 589832 | tf_op jit(solution)/shard_map/ppermute | solution.py:550
  147.5 12.8 %convolution_convert_fusion.4.qkv_ref = bf16[1664,1536]{1,0:T(8,128)(2,1)} fusion(bf16[1664,1536]{1,0:T(8,128)(2,1)} %select_dynamic-update-slice_fusion, bf16[1536,1536]{1,0:T(8,128)(2,1)} %all-gather.5.cloned.1.call-done), kind=kOutput, calls=%fused_computation.5 | convolution fusion | flops 7854292992 | bytes 14942208 | tf_op jit(solution)/shard_map/dot_general | solution.py:24
  160.3 61.2 %attention_forward.2 = (bf16[2,1664,1664]{2,1,0:T(8,128)(2,1)}, f32[2,1664,256]{2,1,0:T(8,128)}, f32[2,1664,128]{2,1,0:T(8,128)}, bf16[1664,256]{1,0:T(8,128)(2,1)}) custom-call(s32[26]{0:T(128)} %pad_add_fusion.bounds_ref, s32[2]{0:T(128)} %bitcast.216, f32[8]{0:T(128)} %reshape.422.mix_ref, f32[1,512]{1,0:T(1,128)} %bitcast.212, ...), custom_call_target="tpu_custom_call" | custom-call | flops 70000001024 | bytes 20000000 | tf_op jit(solution)/shard_map/attention_forward/pallas_call | solution.py:430
  230.0 61.9 %attention_forward.3 = (bf16[2,1664,1664]{2,1,0:T(8,128)(2,1)}, f32[2,1664,256]{2,1,0:T(8,128)}, f32[2,1664,128]{2,1,0:T(8,128)}, bf16[1664,256]{1,0:T(8,128)(2,1)}) custom-call(s32[26]{0:T(128)} %pad_add_fusion.bounds_ref, s32[2]{0:T(128)} %bitcast.217, f32[8]{0:T(128)} %reshape.422.mix_ref, f32[1,512]{1,0:T(1,128)} %bitcast.213, ...), custom_call_target="tpu_custom_call" | custom-call | flops 70000001024 | bytes 20000000 | tf_op jit(solution)/shard_map/attention_forward/pallas_call | solution.py:430
  330.6 26.6 %collective-permute-done.21 = bf16[416,1536]{1,0:T(8,128)(2,1)S(1)} collective-permute-done((bf16[416,1536]{1,0:T(8,128)(2,1)S(1)}, bf16[416,1536]{1,0:T(8,128)(2,1)S(1)}, u32[]{:S(2)}, u32[]{:S(2)}) %collective-permute-start.21) | collective-permute-done | bytes 1277984 | tf_op jit(solution)/shard_map/ppermute | solution.py:555
  359.9 10.1 %fusion.17 = f32[832,2048]{1,0:T(8,128)} fusion(bf16[1536,4096]{1,0:T(8,128)(2,1)} %all-gather.9.cloned.1.call-done, bf16[416,1536]{1,0:T(8,128)(2,1)} %copy-done.38, bf16[416,1536]{1,0:T(8,128)(2,1)} %copy-done.11), kind=kOutput, calls=%fused_computation.33 | convolution fusion | flops 5239603200 | bytes 15663104 | tf_op jit(solution)/shard_map/dot_general | solution.py:24
  370.0 10.3 %multiply_convert_fusion.1 = (bf16[832,2048]{1,0:T(8,128)(2,1)}, f32[832,2048]{1,0:T(8,128)}) fusion(f32[832,2048]{1,0:T(8,128)} %fusion.17, bf16[1536,4096]{1,0:T(8,128)(2,1)S(1)} %copy-done.82, bf16[416,1536]{1,0:T(8,128)(2,1)S(1)} %copy-done.39, bf16[416,1536]{1,0:T(8,128)(2,1)S(1)} %copy-done.12), kind=kOutput, calls=%fused_computation.13 | convolution fusion | flops 5249826816 | bytes 25886720 | tf_op jit(solution)/shard_map/dot_general | solution.py:24
  380.4 10.6 %convolution_convert_fusion.1 = bf16[1536,2048]{1,0:T(8,128)(2,1)} fusion(bf16[832,1536]{1,0:T(8,128)(2,1)S(1)} %copy-done.52, bf16[832,2048]{1,0:T(8,128)(2,1)} %get-tuple-element.84), kind=kOutput, calls=%fused_computation.2 | convolution fusion | flops 5237637120 | bytes 12255232 | tf_op jit(solution)/shard_map/dot_general | solution.py:32
  391.5 14.5 %fusion.2 = (bf16[832,2048]{1,0:T(8,128)(2,1)}, bf16[832,2048]{1,0:T(8,128)(2,1)S(1)}) fusion(f32[832,2048]{1,0:T(8,128)} %fusion.17, f32[832,2048]{1,0:T(8,128)} %get-tuple-element.240, bf16[832,1536]{1,0:T(8,128)(2,1)} %copy-done.51, bf16[1536,2048]{1,0:T(8,128)(2,1)} %all-gather.11.cloned.1.call-done), kind=kOutput, calls=%fused_computation.8 | convolution fusion | flops 5258346496 | bytes 29294592 | tf_op jit(solution)/shard_map/dot_general | solution.py:24
  427.8 18.0 %convolution_convert_fusion = bf16[1536,4096]{1,0:T(8,128)(2,1)} fusion(bf16[832,1536]{1,0:T(8,128)(2,1)S(1)} %copy-done.17, bf16[832,2048]{1,0:T(8,128)(2,1)S(1)} %get-tuple-element.82, bf16[832,2048]{1,0:T(8,128)(2,1)} %get-tuple-element.81), kind=kOutput, calls=%fused_computation | convolution fusion | flops 10488905728 | bytes 21954560 | tf_op jit(solution)/shard_map/dot_general | solution.py:32
  447.7 28.5 %collective-permute-done.25 = bf16[416,1536]{1,0:T(8,128)(2,1)} collective-permute-done((bf16[416,1536]{1,0:T(8,128)(2,1)}, bf16[416,1536]{1,0:T(8,128)(2,1)}, u32[]{:S(2)}, u32[]{:S(2)}) %collective-permute-start.25) | collective-permute-done | bytes 1277984 | tf_op jit(solution)/shard_map/ppermute | solution.py:555
  523.4 102.8 %attention_backward.2 = (bf16[1664,1536]{1,0:T(8,128)(2,1)}, f32[2,256,768]{2,1,0:T(8,128)}, f32[1,8,256]{2,1,0:T(8,128)}, f32[1,4,8,128]{3,2,1,0:T(8,128)}) custom-call(s32[26]{0:T(128)} %pad_add_fusion.bounds_ref, s32[2]{0:T(128)} %bitcast.218, f32[8]{0:T(128)} %reshape.422.mix_ref, f32[1,512]{1,0:T(1,128)} %bitcast.214, ...), custom_call_target="tpu_custom_call" | custom-call | flops 115000000512 | bytes 20000000 | tf_op jit(solution)/shard_map/attention_backward/pallas_call | solution.py:469
  633.4 9.2 add_convert_fusion
  646.9 103.7 %attention_backward.3 = (bf16[1664,1536]{1,0:T(8,128)(2,1)}, f32[2,256,768]{2,1,0:T(8,128)}, f32[1,8,256]{2,1,0:T(8,128)}, f32[1,4,8,128]{3,2,1,0:T(8,128)}) custom-call(s32[26]{0:T(128)} %pad_add_fusion.bounds_ref, s32[2]{0:T(128)} %bitcast.219, f32[8]{0:T(128)} %reshape.422.mix_ref, f32[1,512]{1,0:T(1,128)} %bitcast.215, ...), custom_call_target="tpu_custom_call", output_to_operand_aliasing={{0}: (12, {})} | custom-call | flops 115000000512 | bytes 20000000 | tf_op jit(solution)/shard_map/attention_backward/pallas_call | solution.py:469
  764.6 11.9 %multiply_reduce_fusion.1 = (f32[768]{0:T(1024)S(1)}, f32[768]{0:T(1024)}, bf16[1664,768]{1,0:T(8,128)(2,1)}) fusion(bf16[1664,1536]{1,0:T(8,128)(2,1)} %select_dynamic-update-slice_fusion, bf16[1664,768]{1,0:T(8,128)(2,1)S(1)} %convolution_convert_fusion.5, bf16[1664,1536]{1,0:T(8,128)(2,1)} %get-tuple-element.101, ...), kind=kOutput, calls=%fused_computation.17 | convolution fusion | flops 3937368576 | bytes 17700864 | tf_op jit(solution)/shard_map/dot_general | solution.py:28
  776.6 10.6 %convolution_convert_fusion.2 = bf16[1536,1536]{1,0:T(8,128)(2,1)} fusion(bf16[1664,1536]{1,0:T(8,128)(2,1)S(1)} %bitcast.151, bf16[1664,1536]{1,0:T(8,128)(2,1)S(1)} %bitcast.225), kind=kOutput, calls=%fused_computation.3 | convolution fusion | flops 7854096384 | bytes 14942208 | tf_op jit(solution)/shard_map/dot_general | solution.py:32
  820.3 7.7 collective-permute-done.49
  833.6 8.0 collective-permute-done.40
  857.2 10.9 %collective-permute-done.41 = bf16[416,768]{1,0:T(8,128)(2,1)S(1)} collective-permute-done((bf16[416,768]{1,0:T(8,128)(2,1)S(1)}, bf16[416,768]{1,0:T(8,128)(2,1)S(1)}, u32[]{:S(2)}, u32[]{:S(2)}) %collective-permute-start.41) | collective-permute-done | bytes 639008 | tf_op jit(solution)/shard_map/ppermute | solution.py:603
  886.2 13.2 %collective-permute-start.42 = (bf16[416,768]{1,0:T(8,128)(2,1)}, bf16[416,768]{1,0:T(8,128)(2,1)}, u32[]{:S(2)}, u32[]{:S(2)}) collective-permute-start(bf16[416,768]{1,0:T(8,128)(2,1)} %get-tuple-element.165), channel_id=1, source_target_pairs={{0,1},{1,2},{2,3},{4,5},{5,6},{6,7},{8,9},{9,10},{10,11},{12,13},{... | collective-permute-start | bytes 1916936 | tf_op jit(solution)/shard_map/ppermute | solution.py:603
  913.7 9.9 %collective-permute-done.45 = bf16[416,768]{1,0:T(8,128)(2,1)} collective-permute-done((bf16[416,768]{1,0:T(8,128)(2,1)S(1)}, bf16[416,768]{1,0:T(8,128)(2,1)}, u32[]{:S(2)}, u32[]{:S(2)}) %collective-permute-start.45) | collective-permute-done | bytes 639008 | tf_op jit(solution)/shard_map/ppermute | solution.py:604
  (541 shorter events, 341.7 us)
Async XLA Ops:
  7.2 140.3 %all-gather.5.cloned.1.call-start = ((), (), s32[]{:S(2)}) async-start(), calls=%async_computation.4 | async-start | bytes 5308416 | tf_op jit(solution)/shard_map/all_gather | solution.py:660
  14.7 42.1 %collective-permute-start = (bf16[208,1536]{1,0:T(8,128)(2,1)S(1)}, bf16[208,1536]{1,0:T(8,128)(2,1)}, u32[]{:S(2)}, u32[]{:S(2)}) collective-permute-start(bf16[208,1536]{1,0:T(8,128)(2,1)S(1)} %get-tuple-element.184), channel_id=1, source_target_pairs={{0,1},{1,2},{2,3},{4,5},{5,6},{6,7},{8,9},{9,10},{10,11},{12,13},{... | collective-permute-start | bytes 1916936 | tf_op jit(solution)/shard_map/ppermute | solution.py:572
  22.5 35.8 %collective-permute-start.4 = (bf16[208,1536]{1,0:T(8,128)(2,1)S(1)}, bf16[208,1536]{1,0:T(8,128)(2,1)}, u32[]{:S(2)}, u32[]{:S(2)}) collective-permute-start(bf16[208,1536]{1,0:T(8,128)(2,1)S(1)} %get-tuple-element.183), channel_id=1, source_target_pairs={{0,1},{1,2},{2,3},{4,5},{5,6},{6,7},{8,9},{9,10},{10,11},{12,13},{... | collective-permute-start | bytes 1916936 | tf_op jit(solution)/shard_map/ppermute | solution.py:572
  30.7 286.9 %all-gather.7.cloned.1.call-start = ((), (), s32[]{:S(2)}) async-start(), calls=%async_computation.5 | async-start | bytes 7077888 | tf_op jit(solution)/shard_map/all_gather | solution.py:676
  56.8 33.3 %collective-permute-start.8 = (bf16[208,1536]{1,0:T(8,128)(2,1)}, bf16[208,1536]{1,0:T(8,128)(2,1)}, u32[]{:S(2)}, u32[]{:S(2)}) collective-permute-start(bf16[208,1536]{1,0:T(8,128)(2,1)} %collective-permute-done), channel_id=1, source_target_pairs={{1,2},{2,3},{5,6},{6,7},{9,10},{10,11},{13,14},{14,15},{17,18},{18... | collective-permute-start | bytes 1916936 | tf_op jit(solution)/shard_map/ppermute | solution.py:572
  134.7 225.2 %all-gather.9.cloned.1.call-start = ((), (), s32[]{:S(2)}) async-start(), calls=%async_computation.6 | async-start | bytes 14155776 | tf_op jit(solution)/shard_map/all_gather | solution.py:706
  139.9 81.6 %collective-permute-start.22 = (bf16[192,2048]{1,0:T(8,128)(2,1)S(1)}, bf16[192,2048]{1,0:T(8,128)(2,1)}, u32[]{:S(2)}, u32[]{:S(2)}) collective-permute-start(bf16[192,2048]{1,0:T(8,128)(2,1)S(1)} %pad_maximum_fusion.3), channel_id=1, source_target_pairs={{0,2},{1,3},{2,0},{3,1},{4,6},{5,7},{6,4},{7,5},{8,10},{9,11},{10,... | collective-permute-start | bytes 2359304 | tf_op jit(solution)/shard_map/ppermute | solution.py:550
  143.5 78.0 %collective-permute-start.24 = (bf16[416,1536]{1,0:T(8,128)(2,1)S(1)}, bf16[416,1536]{1,0:T(8,128)(2,1)S(1)}, u32[]{:S(2)}, u32[]{:S(2)}) collective-permute-start(bf16[416,1536]{1,0:T(8,128)(2,1)S(1)} %copy-done.13), channel_id=1, source_target_pairs={{0,1},{1,0},{2,3},{3,2},{4,5},{5,4},{6,7},{7,6},{8,9},{9,8},{10,11... | collective-permute-start | bytes 3833864 | tf_op jit(solution)/shard_map/ppermute | solution.py:555
  146.5 75.0 %collective-permute-start.23 = (bf16[192,1024]{1,0:T(8,128)(2,1)}, bf16[192,1024]{1,0:T(8,128)(2,1)}, u32[]{:S(2)}, u32[]{:S(2)}) collective-permute-start(bf16[192,1024]{1,0:T(8,128)(2,1)} %bitcast.41), channel_id=1, source_target_pairs={{0,2},{1,3},{2,0},{3,1},{4,6},{5,7},{6,4},{7,5},{8,10},{9,11},{10,... | collective-permute-start | bytes 1179656 | tf_op jit(solution)/shard_map/ppermute | solution.py:550
  224.5 167.0 %all-gather.11.cloned.1.call-start = ((), (), s32[]{:S(2)}) async-start(), calls=%async_computation.7 | async-start | bytes 7077888 | tf_op jit(solution)/shard_map/all_gather | solution.py:710
  225.5 68.7 %collective-permute-start.12 = (bf16[416,256]{1,0:T(8,128)(2,1)S(1)}, bf16[416,256]{1,0:T(8,128)(2,1)S(1)}, u32[]{:S(2)}, u32[]{:S(2)}) collective-permute-start(bf16[416,256]{1,0:T(8,128)(2,1)S(1)} %get-tuple-element.194), channel_id=1, source_target_pairs={{0,1},{1,2},{2,3},{3,0},{4,5},{5,6},{6,7},{7,4},{8,9},{9,10},{10,1... | collective-permute-start | bytes 638984 | tf_op jit(solution)/shard_map/ppermute | solution.py:550
  225.8 69.0 %collective-permute-start.13 = (bf16[416,256]{1,0:T(8,128)(2,1)S(1)}, bf16[416,256]{1,0:T(8,128)(2,1)S(1)}, u32[]{:S(2)}, u32[]{:S(2)}) collective-permute-start(bf16[416,256]{1,0:T(8,128)(2,1)S(1)} %get-tuple-element.193), channel_id=1, source_target_pairs={{0,2},{1,3},{2,0},{3,1},{4,6},{5,7},{6,4},{7,5},{8,10},{9,11},{10,... | collective-permute-start | bytes 638984 | tf_op jit(solution)/shard_map/ppermute | solution.py:550
  230.0 412.7 %reduce-scatter.7.cloned.1.call-start = ((), (), s32[]{:S(2)}) async-start(), calls=%async_computation.9 | async-start | bytes 7077888 | tf_op jit(solution)/shard_map/reduce_scatter | solution.py:724
  391.0 251.6 %reduce-scatter.5.cloned.1.call-start = ((), (), s32[]{:S(2)}) async-start(), calls=%async_computation.8 | async-start | bytes 14155776 | tf_op jit(solution)/shard_map/reduce_scatter | solution.py:737
  445.8 311.2 %reduce-scatter.9.cloned.1.call-start = ((), (), s32[]{:S(2)}) async-start(), calls=%async_computation.10 | async-start | bytes 7077888 | tf_op jit(solution)/shard_map/reduce_scatter | solution.py:782
  492.3 134.0 %collective-permute-start.27 = (bf16[416,256]{1,0:T(8,128)(2,1)}, bf16[416,256]{1,0:T(8,128)(2,1)}, u32[]{:S(2)}, u32[]{:S(2)}) collective-permute-start(bf16[416,256]{1,0:T(8,128)(2,1)} %get-tuple-element.178), channel_id=1, source_target_pairs={{0,3},{1,0},{2,1},{3,2},{4,7},{5,4},{6,5},{7,6},{8,11},{9,8},{10,9... | collective-permute-start | bytes 638984 | tf_op jit(solution)/shard_map/ppermute | solution.py:550
  496.2 132.3 %collective-permute-start.28 = (bf16[416,256]{1,0:T(8,128)(2,1)}, bf16[416,256]{1,0:T(8,128)(2,1)}, u32[]{:S(2)}, u32[]{:S(2)}) collective-permute-start(bf16[416,256]{1,0:T(8,128)(2,1)} %get-tuple-element.177), channel_id=1, source_target_pairs={{0,2},{1,3},{2,0},{3,1},{4,6},{5,7},{6,4},{7,5},{8,10},{9,11},{10,... | collective-permute-start | bytes 638984 | tf_op jit(solution)/shard_map/ppermute | solution.py:550
  511.2 118.2 %collective-permute-start.29 = (bf16[416,256]{1,0:T(8,128)(2,1)}, bf16[416,256]{1,0:T(8,128)(2,1)}, u32[]{:S(2)}, u32[]{:S(2)}) collective-permute-start(bf16[416,256]{1,0:T(8,128)(2,1)} %get-tuple-element.176), channel_id=1, source_target_pairs={{0,1},{1,2},{2,3},{3,0},{4,5},{5,6},{6,7},{7,4},{8,9},{9,10},{10,1... | collective-permute-start | bytes 638984 | tf_op jit(solution)/shard_map/ppermute | solution.py:550
  520.5 112.9 %collective-permute-start.26 = (bf16[416,1536]{1,0:T(8,128)(2,1)}, bf16[416,1536]{1,0:T(8,128)(2,1)}, u32[]{:S(2)}, u32[]{:S(2)}) collective-permute-start(bf16[416,1536]{1,0:T(8,128)(2,1)} %convolution_convert_fusion.7), channel_id=1, source_target_pairs={{0,1},{1,0},{2,3},{3,2},{4,5},{5,4},{6,7},{7,6},{8,9},{9,8},{10,11... | collective-permute-start | bytes 3833864 | tf_op jit(solution)/shard_map/ppermute | solution.py:555
  626.2 302.5 %reduce-scatter.11.cloned.1.call-start = ((), (), s32[]{:S(2)}) async-start(), calls=%async_computation.11 | async-start | bytes 5308416 | tf_op jit(solution)/shard_map/reduce_scatter | solution.py:816
  646.9 106.9 %collective-permute-start.33 = (bf16[192,3072]{1,0:T(8,128)(2,1)}, bf16[192,3072]{1,0:T(8,128)(2,1)}, u32[]{:S(2)}, u32[]{:S(2)}) collective-permute-start(bf16[192,3072]{1,0:T(8,128)(2,1)} %pad_maximum_fusion.2), channel_id=1, source_target_pairs={{0,2},{1,3},{2,0},{3,1},{4,6},{5,7},{6,4},{7,5},{8,10},{9,11},{10,... | collective-permute-start | bytes 3538952 | tf_op jit(solution)/shard_map/ppermute | solution.py:550
  819.6 36.9 %collective-permute-start.43 = (bf16[416,768]{1,0:T(8,128)(2,1)S(1)}, bf16[416,768]{1,0:T(8,128)(2,1)S(1)}, u32[]{:S(2)}, u32[]{:S(2)}) collective-permute-start(bf16[416,768]{1,0:T(8,128)(2,1)S(1)} %get-tuple-element.168), channel_id=1, source_target_pairs={{3,2},{7,6},{11,10},{15,14},{19,18},{23,22},{27,26},{31,30}} | collective-permute-start | bytes 1916936 | tf_op jit(solution)/shard_map/ppermute | solution.py:604
  847.5 38.6 %collective-permute-start.46 = (bf16[192,512]{1,0:T(8,128)(2,1)S(1)}, bf16[192,512]{1,0:T(8,128)(2,1)S(1)}, u32[]{:S(2)}, u32[]{:S(2)}) collective-permute-start(bf16[192,512]{1,0:T(8,128)(2,1)S(1)} %pad_maximum_fusion.6), channel_id=1, source_target_pairs={{0,3},{1,0},{2,1},{3,2},{4,7},{5,4},{6,5},{7,6},{8,11},{9,8},{10,9... | collective-permute-start | bytes 589832 | tf_op jit(solution)/shard_map/ppermute | solution.py:550
  847.6 51.8 %collective-permute-start.47 = (bf16[192,512]{1,0:T(8,128)(2,1)S(1)}, bf16[192,512]{1,0:T(8,128)(2,1)S(1)}, u32[]{:S(2)}, u32[]{:S(2)}) collective-permute-start(bf16[192,512]{1,0:T(8,128)(2,1)S(1)} %pad_maximum_fusion.7), channel_id=1, source_target_pairs={{0,2},{1,3},{2,0},{3,1},{4,6},{5,7},{6,4},{7,5},{8,10},{9,11},{10,... | collective-permute-start | bytes 589832 | tf_op jit(solution)/shard_map/ppermute | solution.py:550
  (131 other events, 2361.8 us)
Sparse Core Ops, SparseCore 0:
  30.8 39.4 all-gather.4
  134.8 49.1 all-gather.6
  224.6 71.9 all-gather.8
  299.0 45.4 all-gather.10
  391.2 62.6 reduce-scatter.6
  457.6 92.4 reduce-scatter.4
  626.4 60.8 reduce-scatter.8
  787.4 55.6 reduce-scatter.10

commit v3 on v2

--- a/solution.py
+++ b/solution.py
@@ -16,6 +16,7 @@
 FRONT = 64
 ROWPAD = 16
 COLS = LEN + 2 * FRONT
+GROUP = 8
 VMEM_BYTES = 56 * 1024 * 1024
 epsilon = 1e-05
 
@@ -40,6 +41,36 @@
     return ends
 
 
+def over_tiles(tiles, work):
+    def wide_step(group, carry):
+        work(pl.multiple_of(group * GROUP * TILE, GROUP * TILE), GROUP * TILE)
+        return carry
+
+    lax.fori_loop(0, tiles // GROUP, wide_step, 0)
+    left = tiles % GROUP
+    size = GROUP // 2
+    while size:
+        first = tiles - left % (2 * size)
+
+        @pl.when((left // size) % 2 == 1)
+        def _():
+            work(pl.multiple_of(first * TILE, TILE), size * TILE)
+
+        size //= 2
+
+
+def over_edges(first, end, work):
+    def pair_step(pair, carry):
+        work(pl.multiple_of((first + 2 * pair) * TILE, TILE), 2 * TILE)
+        return carry
+
+    lax.fori_loop(0, (end - first) // 2, pair_step, 0)
+
+    @pl.when((end - first) % 2 == 1)
+    def _():
+        work(pl.multiple_of((end - 1) * TILE, TILE), TILE)
+
+
 def stage_queries(qkv_ref, qpad_ref):
     for head in range(2):
         qpad_ref[head, :ROWPAD, :] = jnp.zeros((ROWPAD, LANES), jnp.bfloat16)
@@ -61,20 +92,21 @@
         lax.fori_loop(0, COLS // TILE, tile_step, 0)
 
 
-def filter_keys(kt_ref, thi_ref, tlo_ref, kcat_ref, lags):
+def filter_keys(kt_ref, thi_ref, tlo_ref, stack_ref, kcat_ref, lags):
+    tiles = LEN // TILE
     for head in range(2):
-
-        def tile_step(tile, carry):
-            first = pl.multiple_of(tile * TILE, TILE)
-            window = kt_ref[head, :, pl.ds(first, 2 * TILE)]
-            filtered = dot_nn(window, thi_ref[head]) + dot_nn(window, tlo_ref[head])
-            for lag in range(lags):
-                kcat_ref[head, lag * LANES : (lag + 1) * LANES, pl.ds(first, TILE)] = filtered[
-                    :, lag * TILE : (lag + 1) * TILE
-                ].astype(jnp.bfloat16)
-            return carry
-
-        lax.fori_loop(0, LEN // TILE, tile_step, 0)
+        for tile in range(tiles):
+            stack_ref[tile * TILE : (tile + 1) * TILE, :] = kt_ref[head, :, tile * TILE : (tile + 2) * TILE]
+        for first in range(0, lags, 2):
+            width = min(2, lags - first) * TILE
+            lanes = slice(first * TILE, first * TILE + width)
+            filtered = dot_nn(stack_ref[...], thi_ref[head, :, lanes]) + dot_nn(stack_ref[...], tlo_ref[head, :, lanes])
+            for tile in range(tiles):
+                for part in range(width // TILE):
+                    lag = first + part
+                    kcat_ref[head, lag * LANES : (lag + 1) * LANES, tile * TILE : (tile + 1) * TILE] = filtered[
+                        tile * TILE : (tile + 1) * TILE, part * TILE : (part + 1) * TILE
+                    ].astype(jnp.bfloat16)
 
 
 def lagged(rows, lags):
@@ -95,7 +127,7 @@
 def forward_kernel(
     bounds_ref, starts_ref, mix_ref, gain_ref, qkv_ref, thi_ref, tlo_ref,
     e_ref, o_ref, inv_ref, z_ref,
-    qpad_ref, kpad_ref, kt_ref, kcat_ref, c_ref, qcat_ref, top_ref, sum_ref,
+    qpad_ref, kpad_ref, kt_ref, stack_ref, kcat_ref, c_ref, qcat_ref, top_ref, sum_ref,
     *, lags, pics, group,
 ):
     block = pl.program_id(0)
@@ -106,7 +138,7 @@
     def _():
         stage_queries(qkv_ref, qpad_ref)
         stage_keys(qkv_ref, kpad_ref, kt_ref)
-        filter_keys(kt_ref, thi_ref, tlo_ref, kcat_ref, lags)
+        filter_keys(kt_ref, thi_ref, tlo_ref, stack_ref, kcat_ref, lags)
 
     full = bounds_ref[block]
     last = bounds_ref[blocks + block]
@@ -126,41 +158,35 @@
                 top = jnp.maximum(top, logits[:, part * LANES : (part + 1) * LANES])
             top_ref[head] = top
 
-    def full_step(pair, carry):
-        full_tiles(pl.multiple_of(pair * 2 * TILE, 2 * TILE), 2 * TILE)
-        return carry
-
-    lax.fori_loop(0, full // 2, full_step, 0)
-
-    @pl.when(full % 2 == 1)
-    def _():
-        full_tiles(pl.multiple_of((full - 1) * TILE, TILE), TILE)
+    over_tiles(full, full_tiles)
 
     source_rows = first_row - ROWPAD + lax.broadcasted_iota(jnp.int32, (TILE + ROWPAD, 1), 0)
     source_ends = row_ends(source_rows, starts_ref, pics)
     target_rows = first_row + lax.broadcasted_iota(jnp.int32, (TILE, 1), 0)
     target_ends = row_ends(target_rows, starts_ref, pics)
 
-    def mixed_step(tile, carry):
-        first = pl.multiple_of(tile * TILE, TILE)
-        columns = first - FRONT + lax.broadcasted_iota(jnp.int32, (1, 2 * TILE), 1)
+    def mixed_tiles(first, width):
+        parts = width // TILE
+        columns = first - FRONT + lax.broadcasted_iota(jnp.int32, (1, width + TILE), 1)
         source_allowed = columns <= source_ends
-        target_allowed = first + lax.broadcasted_iota(jnp.int32, (1, TILE), 1) <= target_ends
         for head in range(2):
-            raw = dot_nn(qpad_ref[head, pl.ds(first_row, TILE + ROWPAD), :], kt_ref[head, :, pl.ds(first, 2 * TILE)])
-            raw = jnp.where(source_allowed, raw, 0.0)
-            high = raw.astype(jnp.bfloat16)
-            low = (raw - high.astype(jnp.float32)).astype(jnp.bfloat16)
-            taps = dot_nn(high, thi_ref[head]) + dot_nn(low, thi_ref[head]) + dot_nn(high, tlo_ref[head])
-            logits = taps[ROWPAD:, :TILE]
-            for lag in range(1, lags):
-                logits = logits + taps[ROWPAD - lag : ROWPAD - lag + TILE, lag * TILE : (lag + 1) * TILE]
-            logits = jnp.where(target_allowed, logits, -1e30)
-            c_ref[head, :, pl.ds(first, TILE)] = logits
-            top_ref[head] = jnp.maximum(top_ref[head], logits)
-        return carry
-
-    lax.fori_loop(full, last + 1, mixed_step, 0)
+            raw = dot_nn(qpad_ref[head, pl.ds(first_row, TILE + ROWPAD), :], kt_ref[head, :, pl.ds(first, width + TILE)])
+            raw = jnp.where(source_allowed, raw, 0.0).astype(jnp.bfloat16)
+            stacked = [raw[:, part * TILE : (part + 2) * TILE] for part in range(parts)]
+            taps = dot_nn(stacked[0] if parts == 1 else jnp.concatenate(stacked, axis=0), thi_ref[head])
+            top = top_ref[head]
+            for part in range(parts):
+                base = part * (TILE + ROWPAD) + ROWPAD
+                logits = taps[base : base + TILE, :TILE]
+                for lag in range(1, lags):
+                    logits = logits + taps[base - lag : base - lag + TILE, lag * TILE : (lag + 1) * TILE]
+                targets = first + part * TILE + lax.broadcasted_iota(jnp.int32, (1, TILE), 1)
+                logits = jnp.where(targets <= target_ends, logits, -1e30)
+                c_ref[head, :, pl.ds(first + part * TILE, TILE)] = logits
+                top = jnp.maximum(top, logits)
+            top_ref[head] = top
+
+    over_edges(full, last + 1, mixed_tiles)
 
     for head in range(2):
         top_ref[head] = jnp.broadcast_to(
@@ -181,15 +207,7 @@
             e_ref[head, :, pl.ds(first, width)] = weights
             o_ref[head] += dot_nn(weights, qkv_ref[pl.ds(first, width), 4 * LANES :])
 
-    def soft_step(pair, carry):
-        soft_tiles(pl.multiple_of(pair * 2 * TILE, 2 * TILE), 2 * TILE)
-        return carry
-
-    lax.fori_loop(0, (last + 1) // 2, soft_step, 0)
-
-    @pl.when(last % 2 == 0)
-    def _():
-        soft_tiles(pl.multiple_of(last * TILE, TILE), TILE)
+    over_tiles(last + 1, soft_tiles)
 
     for head in range(2):
         inverse = 1.0 / jnp.sum(sum_ref[head], axis=1, keepdims=True)
@@ -212,9 +230,9 @@
 ):
     (
         low_ref, gram_ref, dgain_ref, dmix_ref,
-        qpad_ref, kpad_ref, kt_ref, vt_ref, kcat_ref,
-        dq_ref, dkt_ref, dvt_ref, dkcat_ref, dqcat_ref, qcatt_ref, x_ref, xt_ref, delta_ref,
-    ) = refs[-18:]
+        qpad_ref, kpad_ref, kt_ref, vt_ref, stack_ref, kcat_ref,
+        dq_ref, dkt_ref, dvt_ref, dkcat_ref, spread_ref, rowst_ref, dqcat_ref, qcatt_ref, x_ref, xt_ref, delta_ref,
+    ) = refs[-21:]
     block = pl.program_id(0)
     blocks = pl.num_programs(0)
     first_row = pl.multiple_of(block * TILE, TILE)
@@ -223,7 +241,7 @@
     def _():
         stage_queries(qkv_ref, qpad_ref)
         stage_keys(qkv_ref, kpad_ref, kt_ref)
-        filter_keys(kt_ref, thi_ref, tlo_ref, kcat_ref, lags)
+        filter_keys(kt_ref, thi_ref, tlo_ref, stack_ref, kcat_ref, lags)
 
         def tile_step(tile, carry):
             first = pl.multiple_of(tile * TILE, TILE)
@@ -261,6 +279,7 @@
         out_grads.append(grads)
     for head in range(2):
         rows = qpad_ref[head, pl.ds(first_row, TILE + ROWPAD), :].astype(jnp.float32)
+        rowst_ref[head] = jnp.transpose(rows).astype(jnp.bfloat16)
         for lag in range(lags):
             turned = jnp.transpose(rows[ROWPAD - lag : ROWPAD - lag + TILE])
             qcatt_ref[head, lag * HD : (lag + 1) * HD, :] = turned[:HD].astype(jnp.bfloat16)
@@ -292,47 +311,52 @@
         for head in range(2):
             grads = score_grads(head, first, width).astype(jnp.bfloat16)
             dqcat_ref[head] += dot_nt(grads, kcat_ref[head, :, pl.ds(first, width)])
-            dkcat_ref[head, :, pl.ds(first, width)] += dot_nn(qcatt_ref[head], grads)
-
-    def full_step(pair, carry):
-        full_tiles(pl.multiple_of(pair * 2 * TILE, 2 * TILE), 2 * TILE)
-        return carry
-
-    lax.fori_loop(0, full // 2, full_step, 0)
-
-    @pl.when(full % 2 == 1)
-    def _():
-        full_tiles(pl.multiple_of((full - 1) * TILE, TILE), TILE)
+            filtered = dot_nn(qcatt_ref[head], grads)
+            for part in range(width // TILE):
+                for lag in range(lags):
+                    dkcat_ref[head, first // TILE + part, :HD, lag * TILE : (lag + 1) * TILE] += filtered[
+                        lag * HD : (lag + 1) * HD, part * TILE : (part + 1) * TILE
+                    ]
+
+    over_tiles(full, full_tiles)
 
     source_rows = first_row - ROWPAD + lax.broadcasted_iota(jnp.int32, (TILE + ROWPAD, 1), 0)
     source_ends = row_ends(source_rows, starts_ref, pics)
     turned_rows = first_row - ROWPAD + lax.broadcasted_iota(jnp.int32, (1, TILE + ROWPAD), 1)
     turned_ends = row_ends(turned_rows, starts_ref, pics)
 
-    def mixed_step(tile, carry):
-        first = pl.multiple_of(tile * TILE, TILE)
-        columns = first - FRONT + lax.broadcasted_iota(jnp.int32, (1, 2 * TILE), 1)
-        turned_columns = first - FRONT + lax.broadcasted_iota(jnp.int32, (2 * TILE, 1), 0)
+    def mixed_tiles(first, width):
+        parts = width // TILE
+        columns = first - FRONT + lax.broadcasted_iota(jnp.int32, (1, width + TILE), 1)
+        turned_columns = first - FRONT + lax.broadcasted_iota(jnp.int32, (width + TILE, 1), 0)
         for head in range(2):
-            rows_low = qpad_ref[head, pl.ds(first_row, TILE + ROWPAD), :]
-            grads = score_grads(head, first, TILE)
-            padded = jnp.concatenate(
-                [jnp.zeros((ROWPAD, TILE), jnp.float32), grads, jnp.zeros((8, TILE), jnp.float32)], axis=0
-            )
-            shifted = jnp.concatenate(
-                [padded[lag : lag + TILE + ROWPAD] for lag in range(lags)], axis=1
-            ).astype(jnp.bfloat16)
-            raw_grads = jnp.where(columns <= source_ends, dot_nn(shifted, ttr_ref[head]), 0.0).astype(jnp.bfloat16)
-            dq_ref[head, pl.ds(first_row, TILE + ROWPAD), :] += dot_nt(
-                raw_grads, kt_ref[head, :, pl.ds(first, 2 * TILE)]
-            )
-            dkt_ref[head, :, pl.ds(first, 2 * TILE)] += dot_tn(rows_low, raw_grads)
-            turned = dot_nt(kpad_ref[head, pl.ds(first, 2 * TILE), :], rows_low)
+            grads = score_grads(head, first, width)
+            above = jnp.zeros((ROWPAD, TILE), jnp.float32)
+            below = jnp.zeros((8, TILE), jnp.float32)
+            shifted = []
+            for part in range(parts):
+                padded = jnp.concatenate([above, grads[:, part * TILE : (part + 1) * TILE], below], axis=0)
+                shifted.append(
+                    jnp.concatenate([padded[lag : lag + TILE + ROWPAD] for lag in range(lags)], axis=1).astype(jnp.bfloat16)
+                )
+            stacked = shifted[0] if parts == 1 else jnp.concatenate(shifted, axis=0)
+            spread = dot_nn(stacked, ttr_ref[head])
+            if parts == 2:
+                upper = spread[: TILE + ROWPAD]
+                lower = spread[TILE + ROWPAD :]
+                spread = jnp.concatenate([upper[:, :TILE], upper[:, TILE:] + lower[:, :TILE], lower[:, TILE:]], axis=1)
+            raw_grads = jnp.where(columns <= source_ends, spread, 0.0).astype(jnp.bfloat16)
+            window = kpad_ref[head, pl.ds(first, width + TILE), :]
+            dq_ref[head, pl.ds(first_row, TILE + ROWPAD), :] += dot_nn(raw_grads, window)
+            dkt_ref[head, :, pl.ds(first, width + TILE)] += dot_nn(rowst_ref[head], raw_grads)
+            turned = dot_nn(window, rowst_ref[head])
             turned = jnp.where(turned_columns <= turned_ends, turned, 0.0).astype(jnp.bfloat16)
-            gram_ref[head] += dot_nn(turned, shifted)
-        return carry
-
-    lax.fori_loop(full, last + 1, mixed_step, 0)
+            total = dot_nn(turned[: 2 * TILE], shifted[0])
+            for part in range(1, parts):
+                total = total + dot_nn(turned[part * TILE : (part + 2) * TILE], shifted[part])
+            gram_ref[head] += total
+
+    over_edges(full, last + 1, mixed_tiles)
 
     for head in range(2):
         total = jnp.zeros((TILE + ROWPAD, LANES), jnp.float32)
@@ -346,16 +370,13 @@
     def _():
         for head in range(2):
 
-            def tile_step(tile, carry):
-                first = pl.multiple_of(tile * TILE, TILE)
-                filtered = jnp.concatenate(
-                    [dkcat_ref[head, lag * HD : (lag + 1) * HD, pl.ds(first, TILE)] for lag in range(lags)], axis=1
-                ).astype(jnp.bfloat16)
-                dkt_ref[head, :HD, pl.ds(first, 2 * TILE)] += dot_nn(filtered, ttr_ref[head])
-                gram_ref[head] += dot_nn(kpad_ref[head, pl.ds(first, 2 * TILE), :HD], filtered)
-                return carry
-
-            lax.fori_loop(0, LEN // TILE, tile_step, 0)
+            filtered = dkcat_ref[head].reshape(LEN, lags * TILE).astype(jnp.bfloat16)
+            windows = dot_nn(filtered, ttr_ref[head])
+            for tile in range(LEN // TILE):
+                rows = slice(tile * TILE, (tile + 1) * TILE)
+                dkt_ref[head, :, tile * TILE : (tile + 2) * TILE] += windows[rows]
+                spread_ref[:, rows] = kpad_ref[head, tile * TILE : (tile + 2) * TILE, :]
+            gram_ref[head] += dot_nn(spread_ref[...], filtered)
             low_ref[:, head * LANES : (head + 1) * LANES] = dq_ref[head, ROWPAD:, :].astype(jnp.bfloat16)
 
             def turn_step(tile, carry):
@@ -451,6 +472,7 @@
             pltpu.VMEM((2, LEN + ROWPAD, LANES), jnp.bfloat16),
             pltpu.VMEM((2, COLS, LANES), jnp.bfloat16),
             pltpu.VMEM((2, LANES, COLS), jnp.bfloat16),
+            pltpu.VMEM((LEN, 2 * TILE), jnp.bfloat16),
             pltpu.VMEM((2, lags * LANES, LEN), jnp.bfloat16),
             pltpu.VMEM((2, TILE, LEN), jnp.float32),
             pltpu.VMEM((2, TILE, lags * LANES), jnp.bfloat16),
@@ -496,11 +518,14 @@
             pltpu.VMEM((2, COLS, LANES), jnp.bfloat16),
             pltpu.VMEM((2, LANES, COLS), jnp.bfloat16),
             pltpu.VMEM((2 * LANES, LEN), jnp.bfloat16),
+            pltpu.VMEM((LEN, 2 * TILE), jnp.bfloat16),
             pltpu.VMEM((2, lags * LANES, LEN), jnp.bfloat16),
             pltpu.VMEM((2, LEN + ROWPAD, LANES), jnp.float32),
             pltpu.VMEM((2, LANES, COLS), jnp.float32),
             pltpu.VMEM((2 * LANES, LEN), jnp.float32),
-            pltpu.VMEM((2, lags * HD, LEN), jnp.float32),
+            pltpu.VMEM((2, LEN // TILE, LANES, lags * TILE), jnp.float32),
+            pltpu.VMEM((2 * TILE, LEN), jnp.bfloat16),
+            pltpu.VMEM((2, LANES, TILE + ROWPAD), jnp.bfloat16),
             pltpu.VMEM((2, TILE, lags * LANES), jnp.float32),
             pltpu.VMEM((2, lags * HD, TILE), jnp.bfloat16),
             pltpu.VMEM((2, TILE, 2 * LANES), jnp.bfloat16),
@@ -581,36 +606,26 @@
     return gathered
 
 
-def line_scatter(parts, count):
+def token_scatter(parts, count):
     size = lax.axis_size("tensor")
     index = lax.axis_index("tensor")
-
-    def block(values, position):
-        first = jnp.clip(position, 0, size - 1) * count
-        return lax.dynamic_slice_in_dim(values, first, count, 0).astype(jnp.float32)
-
-    rising = [None] * len(parts)
-    falling = [None] * len(parts)
-    for step in range(1, size):
-        upward = [(i, i + 1) for i in range(size - 1) if i <= step - 1]
-        downward = [(i + 1, i) for i in range(size - 1) if size - 2 - i <= step - 1]
-        for chunk, values in enumerate(parts):
-            up = block(values, size - step + index)
-            down = block(values, step + index - size)
-            if step > 1:
-                up = up + rising[chunk].astype(jnp.float32)
-                down = down + falling[chunk].astype(jnp.float32)
-            rising[chunk] = lax.ppermute(up.astype(jnp.bfloat16), "tensor", upward)
-            falling[chunk] = lax.ppermute(down.astype(jnp.bfloat16), "tensor", downward)
-    sums = [
-        block(values, index) + (rising[chunk].astype(jnp.float32) + falling[chunk].astype(jnp.float32))
-        for chunk, values in enumerate(parts)
-    ]
-    return jnp.concatenate(sums, axis=1)
+    sums, arrivals = [], []
+    for values in parts:
+
+        def block(step):
+            return lax.dynamic_slice_in_dim(values, ((index + step) % size) * count, count, 0)
+
+        received = [shift(block(step), step) for step in range(1, size)]
+        total = block(0).astype(jnp.float32)
+        for part in received:
+            total = total + part.astype(jnp.float32)
+        sums.append(total)
+        arrivals.append(received[0])
+    return jnp.concatenate(sums, axis=1), arrivals
 
 
 def sum_all(values):
-    for axis in ("tensor", "dp"):
+    for axis in ("dp", "tensor"):
         size = lax.axis_size(axis)
         step = 1
         while step < size:
@@ -673,14 +688,16 @@
 
     out_own = pad_heads(after(out_weight, rows_all).T, heads).reshape(-1, heads * LANES)
     out_parts = [out_own] + [shift(out_own, step) for step in range(1, size)]
+    qkv = dot_nn(rows_all, qkv_full).astype(jnp.bfloat16)
+    qkv, taps_high, taps_low, taps_turned, out_parts = lax.optimization_barrier(
+        (qkv, taps_high, taps_low, taps_turned, out_parts)
+    )
     out_full = lax.all_gather(
         jnp.concatenate(
             [part[:, pair * wide : (pair + 1) * wide] for pair in range(pairs) for part in out_parts], axis=1
         ),
         "dp", axis=0, tiled=True,
     )
-    qkv = dot_nn(rows_all, qkv_full).astype(jnp.bfloat16)
-    qkv, taps_high, taps_low, taps_turned = lax.optimization_barrier((qkv, taps_high, taps_low, taps_turned))
     gate_up_own = after(jnp.concatenate([gate_weight, up_weight], axis=1), rows_all)
     down_own = after(down_weight.T, rows_all)
     gate_up = [gate_up_own] + [shift(gate_up_own, step) for step in range(2, size, 2)]
@@ -715,27 +732,40 @@
     hidden = inputs + dot_nt(token_heads, out_full)
     ffn_in, second_pull = jax.vjp(rms_norm, hidden, feedforward_gain)
     ffn_low = ffn_in.astype(jnp.bfloat16)
+    lead = count // 4 // 16 * 16
     ffn_two = jnp.concatenate([ffn_low, swap(ffn_low)], axis=0)
-    gate = dot_nn(ffn_two, gate_full)
-    upper = dot_nn(ffn_two, up_full)
-    activated, act_pull = jax.vjp(swiglu, gate, upper)
-    act_low = activated.astype(jnp.bfloat16)
+    halves = (ffn_low, ffn_two[count:])
+    gates, uppers, acts = [], [], []
+    for rows in halves:
+        gates.append(dot_nn(rows, gate_full))
+        uppers.append(dot_nn(rows, up_full))
+        acts.append(swiglu(gates[-1], uppers[-1]).astype(jnp.bfloat16))
+    act_low = jnp.concatenate(acts, axis=0)
     down_part = dot_tn(grads_two, act_low).astype(jnp.bfloat16)
     down_sum = lax.psum_scatter(down_part, "dp", scatter_dimension=0, tiled=True)
     act_grads = dot_nn(after(grads_two, down_part), down_full)
-    gate_grads, up_grads = act_pull(act_grads)
-    gate_low = gate_grads.astype(jnp.bfloat16)
-    up_low = up_grads.astype(jnp.bfloat16)
-
-    def ffn_back(rows):
-        return dot_nt(gate_low[rows], gate_full) + dot_nt(up_low[rows], up_full)
-
-    ffn_back_sent = ffn_back(slice(count, None)).astype(jnp.bfloat16)
-    ffn_back_kept = ffn_back(slice(0, count))
-    ffn_two_later, gate_later, up_later = after((ffn_two, gate_low, up_low), ffn_back_kept, ffn_back_sent)
-    gate_up_part = dot_tn(ffn_two_later, jnp.concatenate([gate_later, up_later], axis=1)).astype(jnp.bfloat16)
+    gate_lows, up_lows = [], []
+    for half in range(2):
+        gate_grads, up_grads = jax.vjp(swiglu, gates[half], uppers[half])[1](act_grads[half * count : (half + 1) * count])
+        gate_lows.append(gate_grads.astype(jnp.bfloat16))
+        up_lows.append(up_grads.astype(jnp.bfloat16))
+
+    def ffn_back(gate_low, up_low):
+        return dot_nt(gate_low, gate_full) + dot_nt(up_low, up_full)
+
+    ffn_back_sent = ffn_back(gate_lows[1], up_lows[1]).astype(jnp.bfloat16)
+    back_lead = swap(ffn_back_sent[:lead])
+    back_rest = swap(ffn_back_sent[lead:])
+    kept_gate, kept_up = after((gate_lows[0], up_lows[0]), back_lead)
+    ffn_back_kept = ffn_back(kept_gate, kept_up)
+    ffn_two_later, gate_later, up_later = after((ffn_two, gate_lows, up_lows), ffn_back_kept)
+    gate_up_grads = jnp.concatenate(
+        [jnp.concatenate(gate_later, axis=0), jnp.concatenate(up_later, axis=0)], axis=1
+    )
+    gate_up_part = dot_tn(ffn_two_later, gate_up_grads).astype(jnp.bfloat16)
     gate_up_sum = lax.psum_scatter(gate_up_part, "dp", scatter_dimension=0, tiled=True)
-    ffn_in_grad = ffn_back_kept + after(swap(ffn_back_sent), gate_up_part).astype(jnp.float32)
+    back_other = jnp.concatenate([back_lead, after(back_rest, gate_up_part)], axis=0)
+    ffn_in_grad = ffn_back_kept + back_other.astype(jnp.float32)
     hidden_part, feedforward_gain_part = second_pull(ffn_in_grad)
     hidden_grad = output_grad.astype(jnp.float32) + hidden_part
     hidden_low = hidden_grad.astype(jnp.bfloat16)
@@ -803,20 +833,24 @@
     normed_parts = [
         dot_nt(low, qkv_full[chunk * half : (chunk + 1) * half]).astype(jnp.bfloat16) for chunk in range(2)
     ]
+    normed_grad, arrivals = token_scatter(normed_parts, count)
+    rows_later, low_later, parts_later, gram, gain_parts, mixing_parts = after(
+        (rows_all, low, normed_parts, gram, gain_parts, mixing_parts), arrivals[0]
+    )
+    qkv_part = dot_tn(rows_later, low_later).astype(jnp.bfloat16)
+    qkv_sum = lax.psum_scatter(qkv_part, "dp", scatter_dimension=0, tiled=True).astype(jnp.float32)
     attention_gain_part = jnp.concatenate(
         [
             jnp.sum(
-                part.astype(jnp.float32) * rows_all[:, chunk * half : (chunk + 1) * half].astype(jnp.float32), axis=0
+                part.astype(jnp.float32) * rows_later[:, chunk * half : (chunk + 1) * half].astype(jnp.float32), axis=0
             )
-            for chunk, part in enumerate(normed_parts)
+            for chunk, part in enumerate(parts_later)
         ]
     ) / attention_gain
-    normed_grad = line_scatter(normed_parts, count)
-    qkv_part = dot_tn(after(rows_all, *normed_parts), low).astype(jnp.bfloat16)
-    qkv_sum = lax.psum_scatter(qkv_part, "dp", scatter_dimension=0, tiled=True).astype(jnp.float32)
     input_part = first_pull(normed_grad)[0]
     input_grad = (hidden_grad + input_part).astype(jnp.bfloat16)
     query_grad, key_grad, value_grad = split_pairs(qkv_sum, heads)
+    out_sum = after(out_sum, arrivals[1])
     out_total = owned(
         [[columns(out_sum, pair * size + step, wide) for pair in range(pairs)] for step in range(size)], 1
     )

time: 952 us -> 864 us (0.908)
  Pallas kernels: 330 us -> 245 us
  starting transfers between devices: 117 us -> 107 us
    pallas_call x2, Pallas kernels: 206 us -> 164 us  [attention_backward(): pl.pallas_call(functools.partial(backward_kernel, lags=lags, pics=starts....]
    pallas_call x2, Pallas kernels: 123 us -> 81.2 us  [attention_forward(): pl.pallas_call(functools.partial(forward_kernel, lags=lags, pics=starts.s...]
    ppermute x12 -> x0, starting transfers between devices: 41.4 us -> none  [the longest x6 36.1 us: line_scatter(): rising[chunk] = lax.ppermute(up.astype(jnp.bfloat16), 'tensor', upward)]
    ppermute x12 -> x0, waiting for transfers between devices: 40.2 us -> none  [the longest x6 25.7 us: line_scatter(): rising[chunk] = lax.ppermute(up.astype(jnp.bfloat16), 'tensor', upward)]
    ppermute x21 -> x27, waiting for transfers between devices: 29 us -> 64.4 us  [shift(): lax.ppermute(values, 'tensor', [(index, (index + step) % size) for index...]
    ppermute x21 -> x27, starting transfers between devices: 38.7 us -> 67.9 us  [shift(): lax.ppermute(values, 'tensor', [(index, (index + step) % size) for index...]
    ppermute x4 -> x5, waiting for transfers between devices: 55.2 us -> 44.4 us  [swap(): lax.ppermute(values, 'tensor', [(index, index ^ 1) for index in range(siz...]
    ppermute x6, waiting for transfers between devices: 29.7 us -> 39.5 us  [line_gather(): falling[chunk] = lax.ppermute(falling[chunk], 'tensor', downward)]
  transfers between devices with their start and end apart: 62 -> 57, of which waited for: 21 -> 19; matrix products, arithmetic and copies ran while one was open for 28% -> 35% of each run, Pallas kernels for 35% -> 29%
where the time goes in v3:
time: 864 us; the launch traced here: 852 us
  Pallas kernels  245 us (28%)
  waiting for transfers between devices  159 us (18%)
  matrix products  154 us (18%)
  starting transfers between devices  107 us (12%)
  local copies, waits for them, and re-layouts  92.9 us (11%)
  other arithmetic  75 us (9%)
  between operations  18.8 us (2%)
    pallas_call x2, Pallas kernels, attention_backward(): pl.pallas_call(functools.partial(backward_kernel, lags=lags, pics=starts....  164 us
    pallas_call x2, Pallas kernels, attention_forward(): pl.pallas_call(functools.partial(forward_kernel, lags=lags, pics=starts.s...  81.2 us
    ppermute x27, starting transfers between devices, shift(): lax.ppermute(values, 'tensor', [(index, (index + step) % size) for index...  67.9 us
    ppermute x27, waiting for transfers between devices, shift(): lax.ppermute(values, 'tensor', [(index, (index + step) % size) for index...  64.4 us
    dot_general x9, matrix products, dot_nt(): lax.dot_general(left, right, (((1,), (1,)), ((), ())), preferred_element_...  58.3 us
    dot_general x7, matrix products, dot_nn(): return jnp.dot(left, right, preferred_element_type=jnp.float32)  48.6 us
    dot_general x4, matrix products, dot_tn(): lax.dot_general(left, right, (((0,), (0,)), ((), ())), preferred_element_...  47.1 us
    ppermute x5, waiting for transfers between devices, swap(): lax.ppermute(values, 'tensor', [(index, index ^ 1) for index in range(siz...  44.4 us
  transfers between devices with their start and end apart: 57, of which 19 were waited for; matrix products, arithmetic and copies ran while one was open for 35% of the time, Pallas kernels for 29%

profile of v3, /device:TPU:0, one launch (start us, length us, event | category | flops | bytes accessed | tf_op | source)
XLA Modules:
  0.0 851.9 jit_solution(14621251440516497280)
XLA Ops:
  63.0 12.1 %collective-permute-done.6 = bf16[208,1536]{1,0:T(8,128)(2,1)} collective-permute-done((bf16[208,1536]{1,0:T(8,128)(2,1)}, bf16[208,1536]{1,0:T(8,128)(2,1)}, u32[]{:S(2)}, u32[]{:S(2)}) %collective-permute-start.6) | collective-permute-done | bytes 639008 | tf_op jit(solution)/shard_map/ppermute | solution.py:598
  76.3 12.4 %collective-permute-done.2 = bf16[208,1536]{1,0:T(8,128)(2,1)} collective-permute-done((bf16[208,1536]{1,0:T(8,128)(2,1)}, bf16[208,1536]{1,0:T(8,128)(2,1)}, u32[]{:S(2)}, u32[]{:S(2)}) %collective-permute-start.2) | collective-permute-done | bytes 639008 | tf_op jit(solution)/shard_map/ppermute | solution.py:598
  99.0 15.1 %collective-permute-done.3 = bf16[208,1536]{1,0:T(8,128)(2,1)} collective-permute-done((bf16[208,1536]{1,0:T(8,128)(2,1)}, bf16[208,1536]{1,0:T(8,128)(2,1)}, u32[]{:S(2)}, u32[]{:S(2)}) %collective-permute-start.3) | collective-permute-done | bytes 639008 | tf_op jit(solution)/shard_map/ppermute | solution.py:598
  129.4 12.8 %convolution_convert_fusion.4.qkv_ref = bf16[1664,1536]{1,0:T(8,128)(2,1)} fusion(bf16[1664,1536]{1,0:T(8,128)(2,1)} %select_dynamic-update-slice_fusion, bf16[1536,1536]{1,0:T(8,128)(2,1)} %all-gather.5.cloned.1.call-done), kind=kOutput, calls=%fused_computation.4 | convolution fusion | flops 7854292992 | bytes 14942208 | tf_op jit(solution)/shard_map/dot_general | solution.py:25
  161.3 40.6 %attention_forward.2 = (bf16[2,1664,1664]{2,1,0:T(8,128)(2,1)}, f32[2,1664,256]{2,1,0:T(8,128)}, f32[2,1664,128]{2,1,0:T(8,128)}, bf16[1664,256]{1,0:T(8,128)(2,1)}) custom-call(s32[26]{0:T(128)} %pad_add_fusion.bounds_ref, s32[2]{0:T(128)} %bitcast.225, f32[8]{0:T(128)} %reshape.422.mix_ref, f32[1,512]{1,0:T(1,128)} %bitcast.221, ...), custom_call_target="tpu_custom_call" | custom-call | flops 70000001024 | bytes 20000000 | tf_op jit(solution)/shard_map/attention_forward/pallas_call | solution.py:451
  201.9 9.8 %collective-permute-done.21 = bf16[192,2048]{1,0:T(8,128)(2,1)S(1)} collective-permute-done((bf16[192,2048]{1,0:T(8,128)(2,1)S(1)}, bf16[192,2048]{1,0:T(8,128)(2,1)S(1)}, u32[]{:S(2)}, u32[]{:S(2)}) %collective-permute-start.21) | collective-permute-done | bytes 786464 | tf_op jit(solution)/shard_map/ppermute | solution.py:575
  220.0 40.7 %attention_forward.3 = (bf16[2,1664,1664]{2,1,0:T(8,128)(2,1)}, f32[2,1664,256]{2,1,0:T(8,128)}, f32[2,1664,128]{2,1,0:T(8,128)}, bf16[1664,256]{1,0:T(8,128)(2,1)}) custom-call(s32[26]{0:T(128)} %pad_add_fusion.bounds_ref, s32[2]{0:T(128)} %bitcast.226, f32[8]{0:T(128)} %reshape.422.mix_ref, f32[1,512]{1,0:T(1,128)} %bitcast.222, ...), custom_call_target="tpu_custom_call" | custom-call | flops 70000001024 | bytes 20000000 | tf_op jit(solution)/shard_map/attention_forward/pallas_call | solution.py:451
  309.0 20.5 %collective-permute-done.24 = bf16[416,1536]{1,0:T(8,128)(2,1)} collective-permute-done((bf16[416,1536]{1,0:T(8,128)(2,1)}, bf16[416,1536]{1,0:T(8,128)(2,1)}, u32[]{:S(2)}, u32[]{:S(2)}) %collective-permute-start.24) | collective-permute-done | bytes 1277984 | tf_op jit(solution)/shard_map/ppermute | solution.py:580
  333.8 7.2 multiply_convert_fusion.3
  349.0 10.4 %convolution_convert_fusion.1 = bf16[1536,2048]{1,0:T(8,128)(2,1)} fusion(bf16[832,1536]{1,0:T(8,128)(2,1)} %constant_dynamic-update-slice_fusion.6, bf16[416,2048]{1,0:T(8,128)(2,1)S(1)} %get-tuple-element.271, bf16[416,2048]{1,0:T(8,128)(2,1)S(1)} %get-tuple-element.273), kind=kOutput, calls=%fused_computation.1 | convolution fusion | flops 5244452864 | bytes 12255232 | tf_op jit(solution)/shard_map/dot_general | solution.py:33
  359.6 9.0 %fusion.96 = f32[832,2048]{1,0:T(8,128)S(1)} fusion(bf16[832,1536]{1,0:T(8,128)(2,1)} %constant_dynamic-update-slice_fusion.6, bf16[1536,2048]{1,0:T(8,128)(2,1)} %all-gather.11.cloned.1.call-done), kind=kOutput, calls=%fused_computation.258 | convolution fusion | flops 5234491392 | bytes 15663104 | tf_op jit(solution)/shard_map/dot_general | solution.py:25
  403.0 19.4 %convolution_convert_fusion = bf16[1536,4096]{1,0:T(8,128)(2,1)} fusion(bf16[832,1536]{1,0:T(8,128)(2,1)S(1)} %pad_maximum_fusion.2, bf16[416,2048]{1,0:T(8,128)(2,1)} %get-tuple-element.105, bf16[416,2048]{1,0:T(8,128)(2,1)} %get-tuple-element.104, bf16[416,2048]{1,0:T(8,128)(2,1)} %copy-done.45, bf16[416,2048]{1,0:T(8,128)(2,1)} %get-tuple-element.102), kind=kOutput, calls=%fused_computation | convolution fusion | flops 10502537216 | bytes 21954560 | tf_op jit(solution)/shard_map/dot_general | solution.py:33
  429.1 16.6 %collective-permute-done.26 = bf16[320,1536]{1,0:T(8,128)(2,1)S(1)} collective-permute-done((bf16[320,1536]{1,0:T(8,128)(2,1)S(1)}, bf16[320,1536]{1,0:T(8,128)(2,1)S(1)}, u32[]{:S(2)}, u32[]{:S(2)}) %collective-permute-start.26) | collective-permute-done | bytes 983072 | tf_op jit(solution)/shard_map/ppermute | solution.py:580
  478.3 7.1 collective-permute-start.27
  487.3 81.6 %attention_backward.2 = (bf16[1664,1536]{1,0:T(8,128)(2,1)}, f32[2,256,768]{2,1,0:T(8,128)}, f32[1,8,256]{2,1,0:T(8,128)}, f32[1,4,8,128]{3,2,1,0:T(8,128)}) custom-call(s32[26]{0:T(128)} %pad_add_fusion.bounds_ref, s32[2]{0:T(128)} %bitcast.227, f32[8]{0:T(128)} %reshape.422.mix_ref, f32[1,512]{1,0:T(1,128)} %bitcast.223, ...), custom_call_target="tpu_custom_call" | custom-call | flops 115000000512 | bytes 20000000 | tf_op jit(solution)/shard_map/attention_backward/pallas_call | solution.py:491
  577.1 82.5 %attention_backward.3 = (bf16[1664,1536]{1,0:T(8,128)(2,1)}, f32[2,256,768]{2,1,0:T(8,128)}, f32[1,8,256]{2,1,0:T(8,128)}, f32[1,4,8,128]{3,2,1,0:T(8,128)}) custom-call(s32[26]{0:T(128)} %pad_add_fusion.bounds_ref, s32[2]{0:T(128)} %bitcast.228, f32[8]{0:T(128)} %reshape.422.mix_ref, f32[1,512]{1,0:T(1,128)} %bitcast.224, ...), custom_call_target="tpu_custom_call", output_to_operand_aliasing={{0}: (12, {})} | custom-call | flops 115000000512 | bytes 20000000 | tf_op jit(solution)/shard_map/attention_backward/pallas_call | solution.py:491
  667.2 7.4 convolution_convert_fusion.6
  678.3 9.4 %convolution_convert_fusion.5 = bf16[1664,768]{1,0:T(8,128)(2,1)} fusion(bf16[1664,1536]{1,0:T(8,128)(2,1)} %get-tuple-element.131, bf16[1536,1536]{1,0:T(8,128)(2,1)} %all-gather.5.cloned.1.call-done), kind=kOutput, calls=%fused_computation.54 | convolution fusion | flops 3927146496 | bytes 10027008 | tf_op jit(solution)/shard_map/dot_general | solution.py:29
  687.7 7.5 collective-permute-done.35
  695.3 10.4 %convolution_convert_fusion.2 = bf16[1536,1536]{1,0:T(8,128)(2,1)} fusion(bf16[1664,1536]{1,0:T(8,128)(2,1)S(1)} %bitcast.158, bf16[1664,1536]{1,0:T(8,128)(2,1)S(1)} %bitcast.234), kind=kOutput, calls=%fused_computation.2 | convolution fusion | flops 7854096384 | bytes 14942208 | tf_op jit(solution)/shard_map/dot_general | solution.py:33
  708.5 8.1 add_convert_fusion
  753.8 15.2 %collective-permute-done.36 = bf16[416,768]{1,0:T(8,128)(2,1)} collective-permute-done((bf16[416,768]{1,0:T(8,128)(2,1)}, bf16[416,768]{1,0:T(8,128)(2,1)}, u32[]{:S(2)}, u32[]{:S(2)}) %collective-permute-start.36) | collective-permute-done | bytes 639008 | tf_op jit(solution)/shard_map/ppermute | solution.py:575
  771.0 31.4 %collective-permute-start.43 = (bf16[192,512]{1,0:T(8,128)(2,1)S(1)}, bf16[192,512]{1,0:T(8,128)(2,1)S(1)}, u32[]{:S(2)}, u32[]{:S(2)}) collective-permute-start(bf16[192,512]{1,0:T(8,128)(2,1)S(1)} %pad_maximum_fusion.10), channel_id=1, source_target_pairs={{0,1},{1,2},{2,3},{3,0},{4,5},{5,6},{6,7},{7,4},{8,9},{9,10},{10,1... | collective-permute-start | bytes 589832 | tf_op jit(solution)/shard_map/ppermute | solution.py:575
  803.6 14.7 %collective-permute-done.39 = bf16[416,768]{1,0:T(8,128)(2,1)} collective-permute-done((bf16[416,768]{1,0:T(8,128)(2,1)}, bf16[416,768]{1,0:T(8,128)(2,1)}, u32[]{:S(2)}, u32[]{:S(2)}) %collective-permute-start.39) | collective-permute-done | bytes 639008 | tf_op jit(solution)/shard_map/ppermute | solution.py:575
  (553 shorter events, 331.3 us)
Async XLA Ops:
  7.2 122.3 %all-gather.5.cloned.1.call-start = ((), (), s32[]{:S(2)}) async-start(), calls=%async_computation.4 | async-start | bytes 5308416 | tf_op jit(solution)/shard_map/all_gather | solution.py:675
  15.9 45.6 %collective-permute-start.4 = (bf16[208,1536]{1,0:T(8,128)(2,1)}, bf16[208,1536]{1,0:T(8,128)(2,1)}, u32[]{:S(2)}, u32[]{:S(2)}) collective-permute-start(bf16[208,1536]{1,0:T(8,128)(2,1)} %get-tuple-element.215), channel_id=1, source_target_pairs={{0,1},{1,2},{2,3},{4,5},{5,6},{6,7},{8,9},{9,10},{10,11},{12,13},{... | collective-permute-start | bytes 1916936 | tf_op jit(solution)/shard_map/ppermute | solution.py:597
  32.0 256.7 %all-gather.7.cloned.1.call-start = ((), (), s32[]{:S(2)}) async-start(), calls=%async_computation.5 | async-start | bytes 7077888 | tf_op jit(solution)/shard_map/all_gather | solution.py:695
  150.7 152.7 %all-gather.9.cloned.1.call-start = ((), (), s32[]{:S(2)}) async-start(), calls=%async_computation.6 | async-start | bytes 14155776 | tf_op jit(solution)/shard_map/all_gather | solution.py:723
  160.2 51.5 %collective-permute-start.21 = (bf16[192,2048]{1,0:T(8,128)(2,1)S(1)}, bf16[192,2048]{1,0:T(8,128)(2,1)S(1)}, u32[]{:S(2)}, u32[]{:S(2)}) collective-permute-start(bf16[192,2048]{1,0:T(8,128)(2,1)S(1)} %pad_maximum_fusion.5), channel_id=1, source_target_pairs={{0,2},{1,3},{2,0},{3,1},{4,6},{5,7},{6,4},{7,5},{8,10},{9,11},{10,... | collective-permute-start | bytes 2359304 | tf_op jit(solution)/shard_map/ppermute | solution.py:575
  161.2 53.8 %collective-permute-start.23 = (bf16[416,1536]{1,0:T(8,128)(2,1)S(1)}, bf16[416,1536]{1,0:T(8,128)(2,1)S(1)}, u32[]{:S(2)}, u32[]{:S(2)}) collective-permute-start(bf16[416,1536]{1,0:T(8,128)(2,1)S(1)} %copy-done.11), channel_id=1, source_target_pairs={{0,1},{1,0},{2,3},{3,2},{4,5},{5,4},{6,7},{7,6},{8,9},{9,8},{10,11... | collective-permute-start | bytes 3833864 | tf_op jit(solution)/shard_map/ppermute | solution.py:580
  217.4 142.1 %all-gather.11.cloned.1.call-start = ((), (), s32[]{:S(2)}) async-start(), calls=%async_computation.7 | async-start | bytes 7077888 | tf_op jit(solution)/shard_map/all_gather | solution.py:727
  218.3 46.4 %collective-permute-start.16 = (bf16[416,256]{1,0:T(8,128)(2,1)S(1)}, bf16[416,256]{1,0:T(8,128)(2,1)S(1)}, u32[]{:S(2)}, u32[]{:S(2)}) collective-permute-start(bf16[416,256]{1,0:T(8,128)(2,1)S(1)} %get-tuple-element.225), channel_id=1, source_target_pairs={{0,2},{1,3},{2,0},{3,1},{4,6},{5,7},{6,4},{7,5},{8,10},{9,11},{10,... | collective-permute-start | bytes 638984 | tf_op jit(solution)/shard_map/ppermute | solution.py:575
  218.3 45.7 %collective-permute-start.15 = (bf16[416,256]{1,0:T(8,128)(2,1)S(1)}, bf16[416,256]{1,0:T(8,128)(2,1)S(1)}, u32[]{:S(2)}, u32[]{:S(2)}) collective-permute-start(bf16[416,256]{1,0:T(8,128)(2,1)S(1)} %get-tuple-element.226), channel_id=1, source_target_pairs={{0,1},{1,2},{2,3},{3,0},{4,5},{5,6},{6,7},{7,4},{8,9},{9,10},{10,1... | collective-permute-start | bytes 638984 | tf_op jit(solution)/shard_map/ppermute | solution.py:575
  219.8 351.3 %reduce-scatter.7.cloned.1.call-start = ((), (), s32[]{:S(2)}) async-start(), calls=%async_computation.9 | async-start | bytes 7077888 | tf_op jit(solution)/shard_map/reduce_scatter | solution.py:745
  359.4 211.6 %reduce-scatter.5.cloned.1.call-start = ((), (), s32[]{:S(2)}) async-start(), calls=%async_computation.8 | async-start | bytes 14155776 | tf_op jit(solution)/shard_map/reduce_scatter | solution.py:766
  422.5 244.7 %reduce-scatter.9.cloned.1.call-start = ((), (), s32[]{:S(2)}) async-start(), calls=%async_computation.10 | async-start | bytes 7077888 | tf_op jit(solution)/shard_map/reduce_scatter | solution.py:812
  456.9 113.1 %collective-permute-start.30 = (bf16[416,256]{1,0:T(8,128)(2,1)}, bf16[416,256]{1,0:T(8,128)(2,1)}, u32[]{:S(2)}, u32[]{:S(2)}) collective-permute-start(bf16[416,256]{1,0:T(8,128)(2,1)} %get-tuple-element.208), channel_id=1, source_target_pairs={{0,1},{1,2},{2,3},{3,0},{4,5},{5,6},{6,7},{7,4},{8,9},{9,10},{10,1... | collective-permute-start | bytes 638984 | tf_op jit(solution)/shard_map/ppermute | solution.py:575
  457.0 112.1 %collective-permute-start.29 = (bf16[416,256]{1,0:T(8,128)(2,1)}, bf16[416,256]{1,0:T(8,128)(2,1)}, u32[]{:S(2)}, u32[]{:S(2)}) collective-permute-start(bf16[416,256]{1,0:T(8,128)(2,1)} %get-tuple-element.209), channel_id=1, source_target_pairs={{0,2},{1,3},{2,0},{3,1},{4,6},{5,7},{6,4},{7,5},{8,10},{9,11},{10,... | collective-permute-start | bytes 638984 | tf_op jit(solution)/shard_map/ppermute | solution.py:575
  476.7 92.4 %collective-permute-start.28 = (bf16[416,256]{1,0:T(8,128)(2,1)}, bf16[416,256]{1,0:T(8,128)(2,1)S(1)}, u32[]{:S(2)}, u32[]{:S(2)}) collective-permute-start(bf16[416,256]{1,0:T(8,128)(2,1)} %get-tuple-element.210), channel_id=1, source_target_pairs={{0,3},{1,0},{2,1},{3,2},{4,7},{5,4},{6,5},{7,6},{8,11},{9,8},{10,9... | collective-permute-start | bytes 638984 | tf_op jit(solution)/shard_map/ppermute | solution.py:575
  478.3 230.2 %collective-permute-start.27 = (bf16[416,1536]{1,0:T(8,128)(2,1)}, bf16[416,1536]{1,0:T(8,128)(2,1)}, u32[]{:S(2)}, u32[]{:S(2)}) collective-permute-start(bf16[416,1536]{1,0:T(8,128)(2,1)} %convolution_convert_fusion.7), channel_id=1, source_target_pairs={{0,1},{1,0},{2,3},{3,2},{4,5},{5,4},{6,7},{7,6},{8,9},{9,8},{10,11... | collective-permute-start | bytes 3833864 | tf_op jit(solution)/shard_map/ppermute | solution.py:580
  569.0 270.4 %reduce-scatter.11.cloned.1.call-start = ((), (), s32[]{:S(2)}) async-start(), calls=%async_computation.11 | async-start | bytes 5308416 | tf_op jit(solution)/shard_map/reduce_scatter | solution.py:841
  573.2 90.8 %collective-permute-start.34 = (bf16[192,3072]{1,0:T(8,128)(2,1)S(1)}, bf16[192,3072]{1,0:T(8,128)(2,1)}, u32[]{:S(2)}, u32[]{:S(2)}) collective-permute-start(bf16[192,3072]{1,0:T(8,128)(2,1)S(1)} %pad_maximum_fusion.4), channel_id=1, source_target_pairs={{0,2},{1,3},{2,0},{3,1},{4,6},{5,7},{6,4},{7,5},{8,10},{9,11},{10,... | collective-permute-start | bytes 3538952 | tf_op jit(solution)/shard_map/ppermute | solution.py:575
  720.3 48.7 %collective-permute-start.36 = (bf16[416,768]{1,0:T(8,128)(2,1)}, bf16[416,768]{1,0:T(8,128)(2,1)}, u32[]{:S(2)}, u32[]{:S(2)}) collective-permute-start(bf16[416,768]{1,0:T(8,128)(2,1)} %get-tuple-element.197), channel_id=1, source_target_pairs={{0,2},{1,3},{2,0},{3,1},{4,6},{5,7},{6,4},{7,5},{8,10},{9,11},{10,... | collective-permute-start | bytes 1916936 | tf_op jit(solution)/shard_map/ppermute | solution.py:575
  720.3 82.1 %collective-permute-start.40 = (bf16[416,768]{1,0:T(8,128)(2,1)}, bf16[416,768]{1,0:T(8,128)(2,1)}, u32[]{:S(2)}, u32[]{:S(2)}) collective-permute-start(bf16[416,768]{1,0:T(8,128)(2,1)} %get-tuple-element.199), channel_id=1, source_target_pairs={{0,3},{1,0},{2,1},{3,2},{4,7},{5,4},{6,5},{7,6},{8,11},{9,8},{10,9... | collective-permute-start | bytes 1916936 | tf_op jit(solution)/shard_map/ppermute | solution.py:575
  721.2 97.2 %collective-permute-start.39 = (bf16[416,768]{1,0:T(8,128)(2,1)}, bf16[416,768]{1,0:T(8,128)(2,1)}, u32[]{:S(2)}, u32[]{:S(2)}) collective-permute-start(bf16[416,768]{1,0:T(8,128)(2,1)} %get-tuple-element.200), channel_id=1, source_target_pairs={{0,2},{1,3},{2,0},{3,1},{4,6},{5,7},{6,4},{7,5},{8,10},{9,11},{10,... | collective-permute-start | bytes 1916936 | tf_op jit(solution)/shard_map/ppermute | solution.py:575
  729.4 107.9 %collective-permute-start.41 = (bf16[192,512]{1,0:T(8,128)(2,1)}, bf16[192,512]{1,0:T(8,128)(2,1)}, u32[]{:S(2)}, u32[]{:S(2)}) collective-permute-start(bf16[192,512]{1,0:T(8,128)(2,1)} %pad_maximum_fusion.8), channel_id=1, source_target_pairs={{0,3},{1,0},{2,1},{3,2},{4,7},{5,4},{6,5},{7,6},{8,11},{9,8},{10,9... | collective-permute-start | bytes 589832 | tf_op jit(solution)/shard_map/ppermute | solution.py:575
  753.5 83.8 %collective-permute-start.42 = (bf16[192,512]{1,0:T(8,128)(2,1)S(1)}, bf16[192,512]{1,0:T(8,128)(2,1)S(1)}, u32[]{:S(2)}, u32[]{:S(2)}) collective-permute-start(bf16[192,512]{1,0:T(8,128)(2,1)S(1)} %pad_maximum_fusion.9), channel_id=1, source_target_pairs={{0,2},{1,3},{2,0},{3,1},{4,6},{5,7},{6,4},{7,5},{8,10},{9,11},{10,... | collective-permute-start | bytes 589832 | tf_op jit(solution)/shard_map/ppermute | solution.py:575
  771.0 66.3 %collective-permute-start.43 = (bf16[192,512]{1,0:T(8,128)(2,1)S(1)}, bf16[192,512]{1,0:T(8,128)(2,1)S(1)}, u32[]{:S(2)}, u32[]{:S(2)}) collective-permute-start(bf16[192,512]{1,0:T(8,128)(2,1)S(1)} %pad_maximum_fusion.10), channel_id=1, source_target_pairs={{0,1},{1,2},{2,3},{3,0},{4,5},{5,6},{6,7},{7,4},{8,9},{9,10},{10,1... | collective-permute-start | bytes 589832 | tf_op jit(solution)/shard_map/ppermute | solution.py:575
  (136 other events, 2414.1 us)
Sparse Core Ops, SparseCore 0:
  32.1 39.4 all-gather.4
  150.8 45.4 all-gather.6
  217.5 70.6 all-gather.8
  290.6 45.5 all-gather.10
  359.6 60.3 reduce-scatter.6
  423.7 92.3 reduce-scatter.4
  569.1 65.8 reduce-scatter.8
  705.8 53.9 reduce-scatter.10

commit v4 on v3

--- a/solution.py
+++ b/solution.py
@@ -784,8 +784,7 @@
     act_later, hidden_later = after((act_low, hidden_low), head_back)
     out_part = dot_tn(hidden_later, token_heads).astype(jnp.bfloat16)
     ffn_out_sent = dot_nt(act_later[count:], down_full).astype(jnp.bfloat16)
-    ffn_term = dot_nt(act_later[:count], down_full) + swap(ffn_out_sent).astype(jnp.float32)
-    layer_output = (hidden + ffn_term).astype(jnp.bfloat16)
+    ffn_out_other = swap(ffn_out_sent)
 
     head_grads[0] = after(head_grads[0], out_part, ffn_out_sent)
     def owned(groups, stride):
@@ -835,7 +834,7 @@
     ]
     normed_grad, arrivals = token_scatter(normed_parts, count)
     rows_later, low_later, parts_later, gram, gain_parts, mixing_parts = after(
-        (rows_all, low, normed_parts, gram, gain_parts, mixing_parts), arrivals[0]
+        (rows_all, low, normed_parts, gram, gain_parts, mixing_parts), arrivals[0], arrivals[1]
     )
     qkv_part = dot_tn(rows_later, low_later).astype(jnp.bfloat16)
     qkv_sum = lax.psum_scatter(qkv_part, "dp", scatter_dimension=0, tiled=True).astype(jnp.float32)
@@ -851,6 +850,9 @@
     input_grad = (hidden_grad + input_part).astype(jnp.bfloat16)
     query_grad, key_grad, value_grad = split_pairs(qkv_sum, heads)
     out_sum = after(out_sum, arrivals[1])
+    act_last, ffn_out_other = after((act_low[:count], ffn_out_other), attention_gain_part)
+    ffn_term = dot_nt(act_last, down_full) + ffn_out_other.astype(jnp.float32)
+    layer_output = (hidden + ffn_term).astype(jnp.bfloat16)
     out_total = owned(
         [[columns(out_sum, pair * size + step, wide) for pair in range(pairs)] for step in range(size)], 1
     )

time: 864 us -> 856 us (level)
  waiting for transfers between devices: 159 us -> 203 us
  starting transfers between devices: 107 us -> 81.1 us
  other arithmetic: 75 us -> 62.7 us
    ppermute x5, waiting for transfers between devices: 44.4 us -> 77.8 us  [swap(): lax.ppermute(values, 'tensor', [(index, index ^ 1) for index in range(siz...]
    ppermute x27, starting transfers between devices: 67.9 us -> 41.3 us  [shift(): lax.ppermute(values, 'tensor', [(index, (index + step) % size) for index...]
    ppermute x27, waiting for transfers between devices: 64.4 us -> 75.9 us  [shift(): lax.ppermute(values, 'tensor', [(index, (index + step) % size) for index...]
    unnamed x234 -> x242, local copies, waits for them, and re-layouts: 30.6 us -> 34.6 us
  transfers between devices with their start and end apart: 57 -> 57, of which waited for: 19 -> 23; matrix products, arithmetic and copies ran while one was open for 35% -> 29% of each run, Pallas kernels for 29% -> 30%
where the time goes in v4:
time: 856 us; the launch traced here: 850 us
  Pallas kernels  251 us (29%)
  waiting for transfers between devices  203 us (24%)
  matrix products  148 us (17%)
  local copies, waits for them, and re-layouts  85.4 us (10%)
  starting transfers between devices  81.1 us (9%)
  other arithmetic  62.7 us (7%)
  between operations  19.2 us (2%)
    pallas_call x2, Pallas kernels, attention_backward(): pl.pallas_call(functools.partial(backward_kernel, lags=lags, pics=starts....  168 us
    pallas_call x2, Pallas kernels, attention_forward(): pl.pallas_call(functools.partial(forward_kernel, lags=lags, pics=starts.s...  82.8 us
    ppermute x5, waiting for transfers between devices, swap(): lax.ppermute(values, 'tensor', [(index, index ^ 1) for index in range(siz...  77.8 us
    ppermute x27, waiting for transfers between devices, shift(): lax.ppermute(values, 'tensor', [(index, (index + step) % size) for index...  75.9 us
    dot_general x9, matrix products, dot_nt(): lax.dot_general(left, right, (((1,), (1,)), ((), ())), preferred_element_...  52.2 us
    dot_general x7, matrix products, dot_nn(): return jnp.dot(left, right, preferred_element_type=jnp.float32)  48.4 us
    dot_general x4, matrix products, dot_tn(): lax.dot_general(left, right, (((0,), (0,)), ((), ())), preferred_element_...  47.2 us
    ppermute x27, starting transfers between devices, shift(): lax.ppermute(values, 'tensor', [(index, (index + step) % size) for index...  41.3 us
  transfers between devices with their start and end apart: 57, of which 23 were waited for; matrix products, arithmetic and copies ran while one was open for 29% of the time, Pallas kernels for 30%

profile of v4, /device:TPU:0, one launch (start us, length us, event | category | flops | bytes accessed | tf_op | source)
XLA Modules:
  0.0 850.3 jit_solution(15432286296674703337)
XLA Ops:
  62.9 12.1 %collective-permute-done.6 = bf16[208,1536]{1,0:T(8,128)(2,1)} collective-permute-done((bf16[208,1536]{1,0:T(8,128)(2,1)}, bf16[208,1536]{1,0:T(8,128)(2,1)}, u32[]{:S(2)}, u32[]{:S(2)}) %collective-permute-start.6) | collective-permute-done | bytes 639008 | tf_op jit(solution)/shard_map/ppermute | solution.py:598
  76.3 12.4 %collective-permute-done.2 = bf16[208,1536]{1,0:T(8,128)(2,1)} collective-permute-done((bf16[208,1536]{1,0:T(8,128)(2,1)}, bf16[208,1536]{1,0:T(8,128)(2,1)}, u32[]{:S(2)}, u32[]{:S(2)}) %collective-permute-start.2) | collective-permute-done | bytes 639008 | tf_op jit(solution)/shard_map/ppermute | solution.py:598
  98.8 15.3 %collective-permute-done.3 = bf16[208,1536]{1,0:T(8,128)(2,1)} collective-permute-done((bf16[208,1536]{1,0:T(8,128)(2,1)}, bf16[208,1536]{1,0:T(8,128)(2,1)}, u32[]{:S(2)}, u32[]{:S(2)}) %collective-permute-start.3) | collective-permute-done | bytes 639008 | tf_op jit(solution)/shard_map/ppermute | solution.py:598
  129.4 12.9 %convolution_convert_fusion.4.qkv_ref = bf16[1664,1536]{1,0:T(8,128)(2,1)} fusion(bf16[1664,1536]{1,0:T(8,128)(2,1)} %select_dynamic-update-slice_fusion, bf16[1536,1536]{1,0:T(8,128)(2,1)} %all-gather.5.cloned.1.call-done), kind=kOutput, calls=%fused_computation.4 | convolution fusion | flops 7854292992 | bytes 14942208 | tf_op jit(solution)/shard_map/dot_general | solution.py:25
  161.2 41.3 %attention_forward.2 = (bf16[2,1664,1664]{2,1,0:T(8,128)(2,1)}, f32[2,1664,256]{2,1,0:T(8,128)}, f32[2,1664,128]{2,1,0:T(8,128)}, bf16[1664,256]{1,0:T(8,128)(2,1)}) custom-call(s32[26]{0:T(128)} %pad_add_fusion.bounds_ref, s32[2]{0:T(128)} %bitcast.226, f32[8]{0:T(128)} %reshape.422.mix_ref, f32[1,512]{1,0:T(1,128)} %bitcast.222, ...), custom_call_target="tpu_custom_call" | custom-call | flops 70000001024 | bytes 20000000 | tf_op jit(solution)/shard_map/attention_forward/pallas_call | solution.py:451
  202.5 9.0 %collective-permute-done.21 = bf16[192,2048]{1,0:T(8,128)(2,1)S(1)} collective-permute-done((bf16[192,2048]{1,0:T(8,128)(2,1)S(1)}, bf16[192,2048]{1,0:T(8,128)(2,1)S(1)}, u32[]{:S(2)}, u32[]{:S(2)}) %collective-permute-start.21) | collective-permute-done | bytes 786464 | tf_op jit(solution)/shard_map/ppermute | solution.py:575
  220.0 41.4 %attention_forward.3 = (bf16[2,1664,1664]{2,1,0:T(8,128)(2,1)}, f32[2,1664,256]{2,1,0:T(8,128)}, f32[2,1664,128]{2,1,0:T(8,128)}, bf16[1664,256]{1,0:T(8,128)(2,1)}) custom-call(s32[26]{0:T(128)} %pad_add_fusion.bounds_ref, s32[2]{0:T(128)} %bitcast.227, f32[8]{0:T(128)} %reshape.422.mix_ref, f32[1,512]{1,0:T(1,128)} %bitcast.223, ...), custom_call_target="tpu_custom_call" | custom-call | flops 70000001024 | bytes 20000000 | tf_op jit(solution)/shard_map/attention_forward/pallas_call | solution.py:451
  308.7 20.6 %collective-permute-done.24 = bf16[416,1536]{1,0:T(8,128)(2,1)} collective-permute-done((bf16[416,1536]{1,0:T(8,128)(2,1)}, bf16[416,1536]{1,0:T(8,128)(2,1)}, u32[]{:S(2)}, u32[]{:S(2)}) %collective-permute-start.24) | collective-permute-done | bytes 1277984 | tf_op jit(solution)/shard_map/ppermute | solution.py:580
  333.5 7.2 multiply_convert_fusion.3
  348.7 10.4 %convolution_convert_fusion.1 = bf16[1536,2048]{1,0:T(8,128)(2,1)} fusion(bf16[832,1536]{1,0:T(8,128)(2,1)} %constant_dynamic-update-slice_fusion.6, bf16[416,2048]{1,0:T(8,128)(2,1)S(1)} %get-tuple-element.275, bf16[416,2048]{1,0:T(8,128)(2,1)S(1)} %get-tuple-element.135), kind=kOutput, calls=%fused_computation.1 | convolution fusion | flops 5244452864 | bytes 12255232 | tf_op jit(solution)/shard_map/dot_general | solution.py:33
  359.2 8.9 %fusion.94 = f32[832,2048]{1,0:T(8,128)S(1)} fusion(bf16[832,1536]{1,0:T(8,128)(2,1)} %constant_dynamic-update-slice_fusion.6, bf16[1536,2048]{1,0:T(8,128)(2,1)} %all-gather.11.cloned.1.call-done), kind=kOutput, calls=%fused_computation.258 | convolution fusion | flops 5234491392 | bytes 15663104 | tf_op jit(solution)/shard_map/dot_general | solution.py:25
  402.5 19.5 %convolution_convert_fusion = bf16[1536,4096]{1,0:T(8,128)(2,1)} fusion(bf16[832,1536]{1,0:T(8,128)(2,1)S(1)} %pad_maximum_fusion.2, bf16[416,2048]{1,0:T(8,128)(2,1)} %get-tuple-element.107, bf16[416,2048]{1,0:T(8,128)(2,1)} %get-tuple-element.106, bf16[416,2048]{1,0:T(8,128)(2,1)} %copy-done.53, bf16[416,2048]{1,0:T(8,128)(2,1)} %get-tuple-element.104), kind=kOutput, calls=%fused_computation | convolution fusion | flops 10502537216 | bytes 21954560 | tf_op jit(solution)/shard_map/dot_general | solution.py:33
  427.2 18.9 %collective-permute-done.26 = bf16[320,1536]{1,0:T(8,128)(2,1)S(1)} collective-permute-done((bf16[320,1536]{1,0:T(8,128)(2,1)S(1)}, bf16[320,1536]{1,0:T(8,128)(2,1)S(1)}, u32[]{:S(2)}, u32[]{:S(2)}) %collective-permute-start.26) | collective-permute-done | bytes 983072 | tf_op jit(solution)/shard_map/ppermute | solution.py:580
  481.1 83.9 %attention_backward.2 = (bf16[1664,1536]{1,0:T(8,128)(2,1)}, f32[2,256,768]{2,1,0:T(8,128)}, f32[1,8,256]{2,1,0:T(8,128)}, f32[1,4,8,128]{3,2,1,0:T(8,128)}) custom-call(s32[26]{0:T(128)} %pad_add_fusion.bounds_ref, s32[2]{0:T(128)} %bitcast.228, f32[8]{0:T(128)} %reshape.422.mix_ref, f32[1,512]{1,0:T(1,128)} %bitcast.224, ...), custom_call_target="tpu_custom_call" | custom-call | flops 115000000512 | bytes 20000000 | tf_op jit(solution)/shard_map/attention_backward/pallas_call | solution.py:491
  567.5 7.5 collective-permute-start.34
  575.0 84.2 %attention_backward.3 = (bf16[1664,1536]{1,0:T(8,128)(2,1)}, f32[2,256,768]{2,1,0:T(8,128)}, f32[1,8,256]{2,1,0:T(8,128)}, f32[1,4,8,128]{3,2,1,0:T(8,128)}) custom-call(s32[26]{0:T(128)} %pad_add_fusion.bounds_ref, s32[2]{0:T(128)} %bitcast.229, f32[8]{0:T(128)} %reshape.422.mix_ref, f32[1,512]{1,0:T(1,128)} %bitcast.225, ...), custom_call_target="tpu_custom_call", output_to_operand_aliasing={{0}: (12, {})} | custom-call | flops 115000000512 | bytes 20000000 | tf_op jit(solution)/shard_map/attention_backward/pallas_call | solution.py:491
  661.0 7.5 convolution_convert_fusion.6
  681.9 8.4 collective-permute-done.35
  691.2 10.4 %collective-permute-done.36 = bf16[416,768]{1,0:T(8,128)(2,1)} collective-permute-done((bf16[416,768]{1,0:T(8,128)(2,1)S(1)}, bf16[416,768]{1,0:T(8,128)(2,1)}, u32[]{:S(2)}, u32[]{:S(2)}) %collective-permute-start.36) | collective-permute-done | bytes 639008 | tf_op jit(solution)/shard_map/ppermute | solution.py:575
  701.7 10.5 %convolution_convert_fusion.2 = bf16[1536,1536]{1,0:T(8,128)(2,1)} fusion(bf16[1664,1536]{1,0:T(8,128)(2,1)S(1)} %bitcast.159, bf16[1664,1536]{1,0:T(8,128)(2,1)S(1)} %bitcast.239), kind=kOutput, calls=%fused_computation.2 | convolution fusion | flops 7854096384 | bytes 14942208 | tf_op jit(solution)/shard_map/dot_general | solution.py:33
  732.1 30.2 %collective-permute-done.27 = bf16[416,1536]{1,0:T(8,128)(2,1)} collective-permute-done((bf16[416,1536]{1,0:T(8,128)(2,1)}, bf16[416,1536]{1,0:T(8,128)(2,1)}, u32[]{:S(2)}, u32[]{:S(2)}) %collective-permute-start.27) | collective-permute-done | bytes 1277984 | tf_op jit(solution)/shard_map/ppermute | solution.py:580
  763.3 17.0 %collective-permute-done.38 = bf16[416,768]{1,0:T(8,128)(2,1)} collective-permute-done((bf16[416,768]{1,0:T(8,128)(2,1)}, bf16[416,768]{1,0:T(8,128)(2,1)}, u32[]{:S(2)}, u32[]{:S(2)}) %collective-permute-start.38) | collective-permute-done | bytes 639008 | tf_op jit(solution)/shard_map/ppermute | solution.py:575
  785.8 9.2 %collective-permute-done.40 = bf16[416,768]{1,0:T(8,128)(2,1)} collective-permute-done((bf16[416,768]{1,0:T(8,128)(2,1)}, bf16[416,768]{1,0:T(8,128)(2,1)}, u32[]{:S(2)}, u32[]{:S(2)}) %collective-permute-start.40) | collective-permute-done | bytes 639008 | tf_op jit(solution)/shard_map/ppermute | solution.py:575
  798.9 8.4 fusion.38
  (563 shorter events, 323.8 us)
Async XLA Ops:
  7.2 122.2 %all-gather.5.cloned.1.call-start = ((), (), s32[]{:S(2)}) async-start(), calls=%async_computation.4 | async-start | bytes 5308416 | tf_op jit(solution)/shard_map/all_gather | solution.py:675
  16.0 45.5 %collective-permute-start.4 = (bf16[208,1536]{1,0:T(8,128)(2,1)}, bf16[208,1536]{1,0:T(8,128)(2,1)}, u32[]{:S(2)}, u32[]{:S(2)}) collective-permute-start(bf16[208,1536]{1,0:T(8,128)(2,1)} %get-tuple-element.219), channel_id=1, source_target_pairs={{0,1},{1,2},{2,3},{4,5},{5,6},{6,7},{8,9},{9,10},{10,11},{12,13},{... | collective-permute-start | bytes 1916936 | tf_op jit(solution)/shard_map/ppermute | solution.py:597
  32.0 256.4 %all-gather.7.cloned.1.call-start = ((), (), s32[]{:S(2)}) async-start(), calls=%async_computation.5 | async-start | bytes 7077888 | tf_op jit(solution)/shard_map/all_gather | solution.py:695
  150.7 152.4 %all-gather.9.cloned.1.call-start = ((), (), s32[]{:S(2)}) async-start(), calls=%async_computation.6 | async-start | bytes 14155776 | tf_op jit(solution)/shard_map/all_gather | solution.py:723
  158.1 44.4 %collective-permute-start.22 = (bf16[192,1024]{1,0:T(8,128)(2,1)S(1)}, bf16[192,1024]{1,0:T(8,128)(2,1)S(1)}, u32[]{:S(2)}, u32[]{:S(2)}) collective-permute-start(bf16[192,1024]{1,0:T(8,128)(2,1)S(1)} %bitcast.192), channel_id=1, source_target_pairs={{0,2},{1,3},{2,0},{3,1},{4,6},{5,7},{6,4},{7,5},{8,10},{9,11},{10,... | collective-permute-start | bytes 1179656 | tf_op jit(solution)/shard_map/ppermute | solution.py:575
  160.0 51.5 %collective-permute-start.21 = (bf16[192,2048]{1,0:T(8,128)(2,1)S(1)}, bf16[192,2048]{1,0:T(8,128)(2,1)S(1)}, u32[]{:S(2)}, u32[]{:S(2)}) collective-permute-start(bf16[192,2048]{1,0:T(8,128)(2,1)S(1)} %pad_maximum_fusion.5), channel_id=1, source_target_pairs={{0,2},{1,3},{2,0},{3,1},{4,6},{5,7},{6,4},{7,5},{8,10},{9,11},{10,... | collective-permute-start | bytes 2359304 | tf_op jit(solution)/shard_map/ppermute | solution.py:575
  161.1 53.7 %collective-permute-start.23 = (bf16[416,1536]{1,0:T(8,128)(2,1)S(1)}, bf16[416,1536]{1,0:T(8,128)(2,1)S(1)}, u32[]{:S(2)}, u32[]{:S(2)}) collective-permute-start(bf16[416,1536]{1,0:T(8,128)(2,1)S(1)} %copy-done.11), channel_id=1, source_target_pairs={{0,1},{1,0},{2,3},{3,2},{4,5},{5,4},{6,7},{7,6},{8,9},{9,8},{10,11... | collective-permute-start | bytes 3833864 | tf_op jit(solution)/shard_map/ppermute | solution.py:580
  217.2 142.0 %all-gather.11.cloned.1.call-start = ((), (), s32[]{:S(2)}) async-start(), calls=%async_computation.7 | async-start | bytes 7077888 | tf_op jit(solution)/shard_map/all_gather | solution.py:727
  218.1 47.4 %collective-permute-start.16 = (bf16[416,256]{1,0:T(8,128)(2,1)S(1)}, bf16[416,256]{1,0:T(8,128)(2,1)S(1)}, u32[]{:S(2)}, u32[]{:S(2)}) collective-permute-start(bf16[416,256]{1,0:T(8,128)(2,1)S(1)} %get-tuple-element.229), channel_id=1, source_target_pairs={{0,2},{1,3},{2,0},{3,1},{4,6},{5,7},{6,4},{7,5},{8,10},{9,11},{10,... | collective-permute-start | bytes 638984 | tf_op jit(solution)/shard_map/ppermute | solution.py:575
  218.1 46.7 %collective-permute-start.15 = (bf16[416,256]{1,0:T(8,128)(2,1)S(1)}, bf16[416,256]{1,0:T(8,128)(2,1)S(1)}, u32[]{:S(2)}, u32[]{:S(2)}) collective-permute-start(bf16[416,256]{1,0:T(8,128)(2,1)S(1)} %get-tuple-element.230), channel_id=1, source_target_pairs={{0,1},{1,2},{2,3},{3,0},{4,5},{5,6},{6,7},{7,4},{8,9},{9,10},{10,1... | collective-permute-start | bytes 638984 | tf_op jit(solution)/shard_map/ppermute | solution.py:575
  219.6 345.7 %reduce-scatter.7.cloned.1.call-start = ((), (), s32[]{:S(2)}) async-start(), calls=%async_computation.9 | async-start | bytes 7077888 | tf_op jit(solution)/shard_map/reduce_scatter | solution.py:745
  359.1 206.2 %reduce-scatter.5.cloned.1.call-start = ((), (), s32[]{:S(2)}) async-start(), calls=%async_computation.8 | async-start | bytes 14155776 | tf_op jit(solution)/shard_map/reduce_scatter | solution.py:766
  422.1 238.9 %reduce-scatter.9.cloned.1.call-start = ((), (), s32[]{:S(2)}) async-start(), calls=%async_computation.10 | async-start | bytes 7077888 | tf_op jit(solution)/shard_map/reduce_scatter | solution.py:811
  456.8 108.5 %collective-permute-start.30 = (bf16[416,256]{1,0:T(8,128)(2,1)S(1)}, bf16[416,256]{1,0:T(8,128)(2,1)S(1)}, u32[]{:S(2)}, u32[]{:S(2)}) collective-permute-start(bf16[416,256]{1,0:T(8,128)(2,1)S(1)} %get-tuple-element.212), channel_id=1, source_target_pairs={{0,1},{1,2},{2,3},{3,0},{4,5},{5,6},{6,7},{7,4},{8,9},{9,10},{10,1... | collective-permute-start | bytes 638984 | tf_op jit(solution)/shard_map/ppermute | solution.py:575
  457.3 107.9 %collective-permute-start.29 = (bf16[416,256]{1,0:T(8,128)(2,1)S(1)}, bf16[416,256]{1,0:T(8,128)(2,1)S(1)}, u32[]{:S(2)}, u32[]{:S(2)}) collective-permute-start(bf16[416,256]{1,0:T(8,128)(2,1)S(1)} %get-tuple-element.213), channel_id=1, source_target_pairs={{0,2},{1,3},{2,0},{3,1},{4,6},{5,7},{6,4},{7,5},{8,10},{9,11},{10,... | collective-permute-start | bytes 638984 | tf_op jit(solution)/shard_map/ppermute | solution.py:575
  470.0 95.2 %collective-permute-start.28 = (bf16[416,256]{1,0:T(8,128)(2,1)S(1)}, bf16[416,256]{1,0:T(8,128)(2,1)S(1)}, u32[]{:S(2)}, u32[]{:S(2)}) collective-permute-start(bf16[416,256]{1,0:T(8,128)(2,1)S(1)} %get-tuple-element.214), channel_id=1, source_target_pairs={{0,3},{1,0},{2,1},{3,2},{4,7},{5,4},{6,5},{7,6},{8,11},{9,8},{10,9... | collective-permute-start | bytes 638984 | tf_op jit(solution)/shard_map/ppermute | solution.py:575
  565.1 272.4 %reduce-scatter.11.cloned.1.call-start = ((), (), s32[]{:S(2)}) async-start(), calls=%async_computation.11 | async-start | bytes 5308416 | tf_op jit(solution)/shard_map/reduce_scatter | solution.py:840
  567.5 91.7 %collective-permute-start.34 = (bf16[192,3072]{1,0:T(8,128)(2,1)S(1)}, bf16[192,3072]{1,0:T(8,128)(2,1)S(1)}, u32[]{:S(2)}, u32[]{:S(2)}) collective-permute-start(bf16[192,3072]{1,0:T(8,128)(2,1)S(1)} %pad_maximum_fusion.4), channel_id=1, source_target_pairs={{0,2},{1,3},{2,0},{3,1},{4,6},{5,7},{6,4},{7,5},{8,10},{9,11},{10,... | collective-permute-start | bytes 3538952 | tf_op jit(solution)/shard_map/ppermute | solution.py:575
  712.3 50.1 %collective-permute-start.27 = (bf16[416,1536]{1,0:T(8,128)(2,1)}, bf16[416,1536]{1,0:T(8,128)(2,1)}, u32[]{:S(2)}, u32[]{:S(2)}) collective-permute-start(bf16[416,1536]{1,0:T(8,128)(2,1)} %convolution_convert_fusion.7), channel_id=1, source_target_pairs={{0,1},{1,0},{2,3},{3,2},{4,5},{5,4},{6,7},{7,6},{8,9},{9,8},{10,11... | collective-permute-start | bytes 3833864 | tf_op jit(solution)/shard_map/ppermute | solution.py:580
  712.4 50.9 %collective-permute-start.37 = (bf16[416,768]{1,0:T(8,128)(2,1)}, bf16[416,768]{1,0:T(8,128)(2,1)}, u32[]{:S(2)}, u32[]{:S(2)}) collective-permute-start(bf16[416,768]{1,0:T(8,128)(2,1)} %get-tuple-element.199), channel_id=1, source_target_pairs={{0,2},{1,3},{2,0},{3,1},{4,6},{5,7},{6,4},{7,5},{8,10},{9,11},{10,... | collective-permute-start | bytes 1916936 | tf_op jit(solution)/shard_map/ppermute | solution.py:575
  712.5 67.8 %collective-permute-start.38 = (bf16[416,768]{1,0:T(8,128)(2,1)}, bf16[416,768]{1,0:T(8,128)(2,1)}, u32[]{:S(2)}, u32[]{:S(2)}) collective-permute-start(bf16[416,768]{1,0:T(8,128)(2,1)} %get-tuple-element.200), channel_id=1, source_target_pairs={{0,3},{1,0},{2,1},{3,2},{4,7},{5,4},{6,5},{7,6},{8,11},{9,8},{10,9... | collective-permute-start | bytes 1916936 | tf_op jit(solution)/shard_map/ppermute | solution.py:575
  716.8 69.0 %collective-permute-start.39 = (bf16[416,768]{1,0:T(8,128)(2,1)}, bf16[416,768]{1,0:T(8,128)(2,1)}, u32[]{:S(2)}, u32[]{:S(2)}) collective-permute-start(bf16[416,768]{1,0:T(8,128)(2,1)} %get-tuple-element.202), channel_id=1, source_target_pairs={{0,2},{1,3},{2,0},{3,1},{4,6},{5,7},{6,4},{7,5},{8,10},{9,11},{10,... | collective-permute-start | bytes 1916936 | tf_op jit(solution)/shard_map/ppermute | solution.py:575
  716.8 78.3 %collective-permute-start.40 = (bf16[416,768]{1,0:T(8,128)(2,1)}, bf16[416,768]{1,0:T(8,128)(2,1)}, u32[]{:S(2)}, u32[]{:S(2)}) collective-permute-start(bf16[416,768]{1,0:T(8,128)(2,1)} %get-tuple-element.203), channel_id=1, source_target_pairs={{0,3},{1,0},{2,1},{3,2},{4,7},{5,4},{6,5},{7,6},{8,11},{9,8},{10,9... | collective-permute-start | bytes 1916936 | tf_op jit(solution)/shard_map/ppermute | solution.py:575
  763.2 44.2 %collective-permute-start.44 = (f32[48,128]{1,0:T(8,128)S(1)}, f32[48,128]{1,0:T(8,128)S(1)}, u32[]{:S(2)}, u32[]{:S(2)}) collective-permute-start(f32[48,128]{1,0:T(8,128)S(1)} %pad_bitcast_fusion), channel_id=1, source_target_pairs={{0,4},{4,0},{8,12},{12,8},{16,20},{20,16},{24,28},{28,24},{1,5},{5... | collective-permute-start | bytes 73736 | tf_op jit(solution)/shard_map/ppermute | solution.py:632
  (140 other events, 2263.2 us)
Sparse Core Ops, SparseCore 0:
  32.1 39.4 all-gather.4
  150.8 45.3 all-gather.6
  217.3 70.6 all-gather.8
  290.4 45.5 all-gather.10
  359.2 61.5 reduce-scatter.6
  424.6 92.3 reduce-scatter.4
  565.2 66.1 reduce-scatter.8
  712.3 51.8 reduce-scatter.10
